TPU v7x, 32 devices: a whole 2x2x4 slice. The times are simulated.
32 devices in a mesh: groups: 2 (over y), patch: 4 (over z), chan: 2 (over x), sub: 2 (over core).
Axes of the slice: x: 2, y: 2, z: 4, core: 2. Of those that a mesh axis runs over, the one named last changes fastest.
Arguments:
- latent: bfloat16 [640, 2048], P(('chan', 'sub'), ('groups', 'patch')), parts along dimension 1, may hold values from -18 to 18
- timestep: int32 [2], P('groups'), parts along dimension 0, may hold values from 0 to 999
- time_w1: bfloat16 [1280, 320], replicated, may hold values from -0.3125 to 0.3125
- time_proj: bfloat16 [640, 1280], P(('chan', 'sub')), may hold values from -0.15625 to 0.15625
- conv1_w: bfloat16 [9, 640, 640], P(None, ('chan', 'sub')), may hold values from -0.078125 to 0.078125
- conv2_w: bfloat16 [9, 640, 640], P(None, ('chan', 'sub')), may hold values from -0.078125 to 0.078125
- proj_in_w: bfloat16 [640, 640], P(('chan', 'sub')), may hold values from -0.25 to 0.25
- q_w: bfloat16 [640, 640], P(('chan', 'sub')), may hold values from -8 to 8
- kv_w: bfloat16 [2, 640, 640], P(None, ('chan', 'sub')), may hold values from -8 to 8
- out_w: bfloat16 [640, 640], P(('chan', 'sub')), may hold values from -0.25 to 0.25
- proj_out_w: bfloat16 [640, 640], P(('chan', 'sub')), may hold values from -0.25 to 0.25
Outputs:
- output: bfloat16 [640, 2048], P(('chan', 'sub'), ('groups', 'patch')), parts along dimension 1
There are 2 independent parts, one for each index of `groups`. A program takes and returns all parts, laid end to end along the dimension named above; an argument that names none is the same for every part. Nothing has to cross between parts.
All inputs are finite; a program needn't handle non-finite values.
Results may differ from a plain program's by a relative error of at most 0.02.
Values may be sent and summed in bfloat16 or wider, within the bound.
No kernel may reach another device: no remote copies, remote signals or barrier semaphores. Data moves between devices by JAX's collectives and lax.ppermute only.
A program may use at most 64 MiB of HBM per device.

v0:
```python
import math

import jax
import jax.numpy as jnp
from jax import lax
from jax.experimental import pallas as pl
from jax.experimental.pallas import tpu as pltpu
from jax.sharding import PartitionSpec as P


C = 640
HEADS = 10
HEAD_DIM = 64
NGROUPS = 32
GROUP = C // NGROUPS
FREQ = 320
WIDTH = 256
BF16 = jnp.bfloat16
F32 = jnp.float32

OWN = C // 4
CHUNK = OWN // 2
FLIPS = (0, 2, 1, 3)


def own_place():
    return lax.axis_index("chan") * 2 + lax.axis_index("sub")


def call(kernel, outs, *args, scratch=(), flops=0, limit=24):
    specs = [pl.BlockSpec(memory_space=pltpu.VMEM)] * len(args)
    moved = sum(math.prod(a.shape) * a.dtype.itemsize for a in args)
    return pl.pallas_call(
        kernel,
        out_shape=[jax.ShapeDtypeStruct(s, t) for s, t in outs],
        in_specs=specs,
        out_specs=[pl.BlockSpec(memory_space=pltpu.VMEM)] * len(outs),
        scratch_shapes=[pltpu.VMEM(s, t) for s, t in scratch],
        compiler_params=pltpu.CompilerParams(vmem_limit_bytes=limit << 20),
        cost_estimate=pl.CostEstimate(flops=flops, transcendentals=0, bytes_accessed=moved),
    )(*args)


def group_sums(sums):
    wide = jnp.broadcast_to(sums, (sums.shape[0], 128))
    row = lax.broadcasted_iota(jnp.int32, wide.shape, 0)
    result = jnp.zeros_like(wide)
    for start in range(0, wide.shape[0], GROUP):
        inside = (row >= start) & (row < start + GROUP)
        total = jnp.sum(jnp.where(inside, wide, 0.0), axis=0, keepdims=True)
        result = jnp.where(inside, total, result)
    return result[:, :1]


def normal_form(rows, epsilon):
    cell_count = GROUP * len(rows) * rows[0].shape[1]
    centre = group_sums(sum(jnp.sum(row, axis=1, keepdims=True) for row in rows)) / cell_count
    shifted = [row - centre for row in rows]
    spread = group_sums(sum(jnp.sum(row * row, axis=1, keepdims=True) for row in shifted))
    scale = lax.rsqrt(spread / cell_count + epsilon)
    return [row * scale for row in shifted]


def silu(values):
    return values * jax.nn.sigmoid(values)


def first_norm(*refs):
    rows_ref, *chunk_refs = refs[-3:]
    pieces = refs[:-3]
    count = len(pieces) // 2
    position = lax.axis_index("patch")
    places = [position ^ by for by in range(count)]
    for piece, place in zip(pieces, places):
        rows_ref[place] = piece[...]
    for part, out in enumerate(chunk_refs):
        for side in range(2):
            values = [
                piece[part * CHUNK : (part + 1) * CHUNK, :].astype(F32)
                for piece in pieces[side * count : (side + 1) * count]
            ]
            for value, place in zip(normal_form(values, 1e-05), places):
                out[side, place] = silu(value).astype(BF16)


def arrange(weight, half_ref, *rest_refs):
    for tap in range(9):
        i, j = divmod(tap, 3)
        for part, rest_ref in enumerate(rest_refs):
            source = weight[tap, part * CHUNK : (part + 1) * CHUNK, :]
            for block in range(4):
                at = block * OWN
                to = (i * 4 + block) * CHUNK
                row = (part * 3 + j) * CHUNK
                half_ref[row : row + CHUNK, to : to + CHUNK] = source[:, at : at + CHUNK]
                row, at = j * CHUNK, at + CHUNK
                rest_ref[row : row + CHUNK, to : to + CHUNK] = source[:, at : at + CHUNK]


def place_blocks(blocks, padded):
    if len(blocks) == 2:
        blocks = [block.at[side] for block in blocks for side in range(2)]
    rows = blocks[0].shape[0]
    edge = jnp.zeros(padded.shape[1:], padded.dtype)
    padded[0] = edge
    padded[rows + 1] = edge
    for flip, block in zip(FLIPS, blocks):
        at = pl.multiple_of((own_place() ^ flip) * CHUNK, 16)
        padded[1 : rows + 1, pl.ds(at, CHUNK), :] = block[...]


def taps(weight, padded, row):
    window = padded[row : row + 3].reshape(3 * 4 * CHUNK, WIDTH)
    every = jnp.dot(weight[...], window, preferred_element_type=F32)
    lane = lax.broadcasted_iota(jnp.int32, (CHUNK, WIDTH), 1)
    results = []
    for start in range(0, every.shape[0], 3 * CHUNK):
        left, here, right = (
            every[start + j * CHUNK : start + (j + 1) * CHUNK] for j in range(3)
        )
        left = jnp.where(lane == 0, 0.0, pltpu.roll(left, 1, 1))
        right = jnp.where(lane == WIDTH - 1, 0.0, pltpu.roll(right, WIDTH - 1, 1))
        results.append(here + left + right)
    return results


def half_conv(*refs):
    *blocks, weight, one_ref, two_ref, padded = refs
    place_blocks(blocks, padded)
    for row in range(one_ref.shape[0]):
        one_ref[row], two_ref[row] = taps(weight, padded, row)


def first_conv(part):
    def kernel(*refs):
        *blocks, weight, half, bias, act_ref, padded = refs
        place_blocks(blocks, padded)
        added = bias[part * CHUNK : (part + 1) * CHUNK, :]
        rows = []
        for row in range(act_ref.shape[0]):
            (rest,) = taps(weight, padded, row)
            rows.append((half[row] + rest + added).astype(BF16).astype(F32))
        for row, value in enumerate(normal_form(rows, 1e-05)):
            act_ref[row] = silu(value).astype(BF16)

    return kernel


def second_conv(part):
    def kernel(*refs):
        *blocks, weight, half, latent, act_ref, resnet_ref, padded, sums = refs
        place_blocks(blocks, padded)
        rows = []
        for row in range(act_ref.shape[0]):
            (rest,) = taps(weight, padded, row)
            value = latent[row, part * CHUNK : (part + 1) * CHUNK, :].astype(F32) + (half[row] + rest)
            value = value.astype(BF16)
            sums[row] = value
            rows.append(value.astype(F32))
        resnet_ref[...] = sums[lax.axis_index("patch")]
        for row, value in enumerate(normal_form(rows, 1e-06)):
            act_ref[row] = value.astype(BF16)

    return kernel


def stack_rows(own, chan, sub, both, full):
    for flip, block in zip(FLIPS, (own, chan, sub, both)):
        full[pl.ds(pl.multiple_of((own_place() ^ flip) * OWN, 16), OWN), :] = block[...]


def stack_heads(q_own, kv_own, q_sub, kv_sub, q_ref, k_ref, v_ref):
    here = pl.multiple_of(lax.axis_index("sub") * OWN, 16)
    there = pl.multiple_of((1 - lax.axis_index("sub")) * OWN, 16)
    for at, q_part, kv_part in ((here, q_own, kv_own), (there, q_sub, kv_sub)):
        q_ref[pl.ds(at, OWN), :] = q_part[...]
        k_ref[pl.ds(at, OWN), :] = kv_part[0]
        v_ref[pl.ds(at, OWN), :] = kv_part[1]


def attend(*refs):
    blocks, refs = refs[:8], refs[8:]
    proj_w, q_w, k_w, v_w, out_ref, proj_ref, normed, projected, layered, keys, values = refs
    rows = normed.shape[0]
    for half in range(2):
        for flip, block in zip(FLIPS, blocks[half * 4 : half * 4 + 4]):
            at = pl.multiple_of((own_place() ^ flip) * OWN + half * CHUNK, 16)
            normed[:, pl.ds(at, CHUNK), :] = block[...]
    for row in range(rows):
        value = jnp.dot(proj_w[...], normed[row], preferred_element_type=F32).astype(BF16)
        projected[row] = value
        value = value.astype(F32)
        shifted = value - jnp.sum(value, axis=0, keepdims=True) / C
        spread = jnp.sum(shifted * shifted, axis=0, keepdims=True) / C
        layer = (shifted * lax.rsqrt(spread + 1e-05)).astype(BF16)
        layered[row] = layer
        at = slice(row * WIDTH, (row + 1) * WIDTH)
        keys[:, at] = jnp.dot(k_w[...], layer, preferred_element_type=F32).astype(BF16)
        values[:, at] = jnp.dot(v_w[...], layer, preferred_element_type=F32).astype(BF16)
    proj_ref[...] = projected[lax.axis_index("patch")]
    share = out_ref.shape[1]
    mine = layered[lax.axis_index("patch"), :, pl.ds(pl.multiple_of(lax.axis_index("sub") * share, 128), share)]
    query = (jnp.dot(q_w[...], mine, preferred_element_type=F32) * 0.125).astype(BF16)
    for head in range(query.shape[0] // HEAD_DIM):
        at = slice(head * HEAD_DIM, (head + 1) * HEAD_DIM)
        scores = lax.dot_general(
            keys[at, :], query[at], (((0,), (0,)), ((), ())), preferred_element_type=F32
        )
        weights = jnp.exp(scores - jnp.max(scores, axis=0, keepdims=True))
        total = jnp.sum(weights, axis=0, keepdims=True)
        weighted = jnp.dot(values[at, :], weights.astype(BF16), preferred_element_type=F32)
        out_ref[at, :] = (weighted / total).astype(BF16)


def finish(own, chan, sub, both, proj, res_one, res_two, out_w, last_w, out_ref, attended):
    channels, share = own.shape
    for flip, block in zip(FLIPS, (own, chan, sub, both)):
        place = own_place() ^ flip
        at = pl.multiple_of((place >> 1) * channels, 16)
        lanes = pl.multiple_of((place & 1) * share, 128)
        attended[pl.ds(at, channels), pl.ds(lanes, share)] = block[...]
    mixed = proj[...].astype(F32) + jnp.dot(
        out_w[...], attended[...], preferred_element_type=F32
    )
    last = jnp.dot(last_w[...], mixed.astype(BF16), preferred_element_type=F32)
    for part, res in enumerate((res_one, res_two)):
        at = slice(part * CHUNK, (part + 1) * CHUNK)
        out_ref[at, :] = (res[...].astype(F32) + last[at]).astype(BF16)


def swapped(array, axis, by=1):
    return lax.ppermute(array, axis, [(i, i ^ by) for i in range(lax.axis_size(axis))])


def embedding_of(timestep):
    half_width = FREQ // 2
    frequency = jnp.exp(-math.log(10000.0) * jnp.arange(half_width, dtype=F32) / half_width)
    angles = timestep[0].astype(F32) * frequency
    return jnp.concatenate([jnp.cos(angles), jnp.sin(angles)]).astype(BF16)


def time_bias(embedded, time_w1, time_proj, bias_ref):
    contract_last = (((1,), (1,)), ((), ()))
    wide = jnp.broadcast_to(embedded[...], (16, FREQ))
    hidden = silu(jnp.dot(wide, time_w1[...], preferred_element_type=F32))
    act = silu(hidden).astype(BF16)
    bias_ref[...] = lax.dot_general(
        time_proj[...], act, contract_last, preferred_element_type=F32
    )[:, :1]


def whole_rows(
    latent, timestep, time_w1, time_proj, conv1_w, conv2_w, proj_in_w, q_w, kv_w, out_w, proj_out_w
):
    rows = lax.axis_size("patch")
    chunk = (rows, CHUNK, WIDTH)
    padded = ((rows + 2, 4 * CHUNK, WIDTH), BF16)
    tap_flops = 2 * 3 * CHUNK * 12 * CHUNK * rows * WIDTH
    barrier = lax.optimization_barrier

    def arranged(weight):
        outs = [((width * CHUNK, 12 * CHUNK), BF16) for width in (6, 3, 3)]
        return call(arrange, outs, weight, flops=10**9)

    def stacked(blocks):
        return call(stack_rows, [((C, C), BF16)], *blocks, flops=10**8)[0]

    def exchanged(own, *beside):
        chan = swapped(own, "chan")
        own, chan, beside = barrier((own, chan, beside))
        sub = swapped(own, "sub")
        return (own, chan, sub, swapped(chan, "sub")), beside

    pieces = [latent] + [swapped(latent, "patch", by) for by in range(1, rows)]
    others = [swapped(piece, "chan") for piece in pieces]
    proj_in_chan = swapped(proj_in_w, "chan")
    embedded = embedding_of(timestep)[None]
    (_, *heads_w), embedded = barrier(((pieces[-1], q_w, kv_w), embedded))
    (bias,) = call(time_bias, [((OWN, 1), F32)], embedded, time_w1.T, time_proj, flops=10**8)
    heads_w = (*heads_w, *(swapped(weight, "sub") for weight in heads_w))
    others, conv1_w, bias = barrier((others, arranged(conv1_w), bias))
    pair = (2,) + chunk
    latent_rows, one, two = call(
        first_norm, [((rows, OWN, WIDTH), BF16), (pair, BF16), (pair, BF16)], *pieces, *others,
    )
    one, two = (one, swapped(one, "sub")), (two, swapped(two, "sub"))

    def halves(blocks, weight):
        return call(
            half_conv, [(chunk, F32)] * 2, *blocks, weight, scratch=[padded],
            flops=2 * tap_flops,
        )

    half = halves(one, conv1_w[0])
    one, two = (
        call(
            first_conv(part), [(chunk, BF16)], *two, conv1_w[1 + part], half[part], bias,
            scratch=[padded], flops=tap_flops,
        )[0]
        for part in range(2)
    )
    _, heads_w, conv2_w, proj_in_chan = barrier((one, heads_w, conv2_w, proj_in_chan))
    heads_w = call(stack_heads, [((2 * OWN, C), BF16)] * 3, *heads_w, flops=10**8)
    proj_in = (
        proj_in_w, proj_in_chan, swapped(proj_in_w, "sub"),
        swapped(proj_in_chan, "sub"),
    )
    one, (heads_w, conv2_w, proj_in) = exchanged(one, heads_w, arranged(conv2_w), proj_in)
    two, _ = exchanged(two)
    half = halves(one, conv2_w[0])
    (one, res_one), (two, res_two) = (
        call(
            second_conv(part), [(chunk, BF16), ((CHUNK, WIDTH), BF16)],
            *two, conv2_w[1 + part], half[part], latent_rows,
            scratch=[padded, (chunk, BF16)], flops=tap_flops,
        )
        for part in range(2)
    )
    _, proj_in, out_w = barrier((one, proj_in, out_w))
    one, (proj_in, out_sub) = exchanged(one, stacked(proj_in), swapped(out_w, "sub"))
    two, _ = exchanged(two)
    _, out_chan = barrier((two, out_w))
    out_chan = swapped(out_chan, "chan")
    share = WIDTH // 2
    attended, projected = call(
        attend, [((2 * OWN, share), BF16), ((C, WIDTH), BF16)],
        *one, *two, proj_in, *heads_w,
        scratch=[((rows, C, WIDTH), BF16)] * 3 + [((2 * OWN, rows * WIDTH), BF16)] * 2,
        flops=4 * 10**9, limit=32,
    )
    _, out_chan = barrier((attended, out_chan))
    out_all = stacked((out_w, out_chan, out_sub, swapped(out_chan, "sub")))
    attended, (out_all,) = exchanged(attended, out_all)
    return call(
        finish, [((OWN, WIDTH), BF16)], *attended, projected, res_one, res_two,
        out_all, proj_out_w, scratch=[((C, WIDTH), BF16)],
    )[0]


def banded_with_halo(cells, sides, width):
    for axis, dim in sides:
        count = lax.axis_size(axis)
        ends = count - 1
        head = lax.slice_in_dim(cells, 0, width, axis=dim)
        tail = lax.slice_in_dim(cells, cells.shape[dim] - width, cells.shape[dim], axis=dim)
        cells = jnp.concatenate(
            [
                lax.ppermute(tail, axis, [(i, (i + 1) % count) for i in range(ends)]),
                cells,
                lax.ppermute(head, axis, [((i + 1) % count, i) for i in range(ends)]),
            ],
            axis=dim,
        )
    return cells


def banded_from_behind(array, axis, by):
    count = lax.axis_size(axis)
    return lax.ppermute(array, axis, [(i, (i + by) % count) for i in range(count)])


def banded_merged(array, axis, combine):
    everything = jax.tree.map(lambda part: lax.all_gather(part, axis), array)
    first = jax.tree.map(lambda part: part[0], everything)

    def turn(k, so_far):
        return combine(so_far, jax.tree.map(lambda part: part[k], everything))

    return lax.fori_loop(1, lax.axis_size(axis), turn, first)


def banded_group_norm(values, epsilon):
    channels, band_len = values.shape
    group_size = C // NGROUPS
    grouped = values.reshape(channels // group_size, group_size, band_len)
    cell_count = group_size * band_len * lax.axis_size("patch")
    centre = lax.psum(jnp.sum(grouped, axis=(1, 2)), "patch") / cell_count
    shifted = grouped - centre[:, None, None]
    spread = lax.psum(jnp.sum(shifted * shifted, axis=(1, 2)), "patch") / cell_count
    normal_form = (grouped - centre[:, None, None]) * lax.rsqrt(spread + epsilon)[:, None, None]
    return normal_form.reshape(channels, band_len)


def banded_convolve(active, weight):
    _, band_len = active.shape
    height = band_len // WIDTH
    whole_rows = lax.all_gather(active, ("chan", "sub"), axis=0, tiled=True)
    image_grid = whole_rows.reshape(whole_rows.shape[0], height, WIDTH)
    padded = banded_with_halo(image_grid, (("patch", 1),), 1)
    channels = padded.shape[0]
    padded = jnp.pad(padded, ((0, 0), (0, 0), (1, 1)))
    running = jnp.zeros((weight.shape[1], band_len), jnp.float32)
    for offset in range(9):
        row_step, col_step = divmod(offset, 3)
        window = padded[:, row_step : row_step + height, col_step : col_step + WIDTH].reshape(
            channels, band_len
        )
        running = running + jnp.dot(weight[offset], window, preferred_element_type=jnp.float32)
    return running


def banded_combine_parts(earlier_part, later_part):
    peak_one, total_one, sums_one = earlier_part
    peak_two, total_two, sums_two = later_part
    new_peak = jnp.maximum(peak_one, peak_two)
    factor_one = jnp.exp(peak_one - new_peak)
    factor_two = jnp.exp(peak_two - new_peak)
    new_total = total_one * factor_one + total_two * factor_two
    new_sums = sums_one * factor_one[:, None, :] + sums_two * factor_two[:, None, :]
    return (new_peak, new_total, new_sums)


def banded_advance(kv_piece):
    return banded_from_behind(kv_piece, "patch", 1)


def banded(
    latent, timestep, time_w1, time_proj, conv1_w, conv2_w, proj_in_w, q_w, kv_w, out_w, proj_out_w
):
    latent_f32 = latent.astype(jnp.float32)
    band_len = latent.shape[1]
    half_width = FREQ // 2
    frequency = jnp.exp(-math.log(10000.0) * jnp.arange(half_width, dtype=jnp.float32) / half_width)
    angles = timestep[0].astype(jnp.float32) * frequency
    embedded = jnp.concatenate([jnp.cos(angles), jnp.sin(angles)]).astype(jnp.bfloat16)
    time_hidden = jax.nn.silu(jnp.dot(time_w1, embedded, preferred_element_type=jnp.float32))
    time_bias = jnp.dot(
        time_proj, jax.nn.silu(time_hidden).astype(jnp.bfloat16), preferred_element_type=jnp.float32
    )
    act_one = jax.nn.silu(banded_group_norm(latent_f32, 1e-05)).astype(jnp.bfloat16)
    conv_one = (banded_convolve(act_one, conv1_w) + time_bias[:, None]).astype(jnp.bfloat16)
    act_two = jax.nn.silu(banded_group_norm(conv_one.astype(jnp.float32), 1e-05)).astype(jnp.bfloat16)
    resnet = (latent_f32 + banded_convolve(act_two, conv2_w)).astype(jnp.bfloat16)
    normed = banded_group_norm(resnet.astype(jnp.float32), 1e-06).astype(jnp.bfloat16)
    columns = proj_in_w
    projected = jnp.dot(
        columns,
        lax.all_gather(normed, ("chan", "sub"), axis=0, tiled=True),
        preferred_element_type=jnp.float32,
    ).astype(jnp.bfloat16)
    whole_proj = lax.all_gather(projected, ("chan", "sub"), axis=0, tiled=True).astype(jnp.float32)
    centre = jnp.mean(whole_proj, axis=0, keepdims=True)
    spread = jnp.mean((whole_proj - centre) * (whole_proj - centre), axis=0, keepdims=True)
    layer_normed = ((whole_proj - centre) / jnp.sqrt(spread + 1e-05)).astype(jnp.bfloat16)
    query_own = (jnp.dot(q_w, layer_normed, preferred_element_type=jnp.float32) * 0.125).astype(
        jnp.bfloat16
    )
    queries = lax.all_gather(query_own, ("chan", "sub"), axis=0, tiled=True).reshape(
        HEADS, HEAD_DIM, band_len
    )
    key_value = jnp.einsum(
        "joc,cb->jbo", kv_w, layer_normed, preferred_element_type=jnp.float32
    ).astype(jnp.bfloat16)
    slot_pairs = lax.all_to_all(key_value, ("chan", "sub"), split_axis=1, concat_axis=2, tiled=True)

    def attend(softmax_state, kv_piece):
        row_peak, row_total, weighted = softmax_state
        slot_len = kv_piece.shape[1]
        key_heads = kv_piece[0].reshape(slot_len, HEADS, HEAD_DIM)
        value_heads = kv_piece[1].reshape(slot_len, HEADS, HEAD_DIM)
        scores = jnp.einsum("khd,hdb->hkb", key_heads, queries, preferred_element_type=jnp.float32)
        new_peak = jnp.maximum(row_peak, jnp.max(scores, axis=1))
        factor = jnp.exp(row_peak - new_peak)
        weights = jnp.exp(scores - new_peak[:, None, :])
        new_total = row_total * factor + jnp.sum(weights, axis=1)
        update = jnp.einsum(
            "khd,hkb->hdb",
            value_heads,
            weights.astype(jnp.bfloat16),
            preferred_element_type=jnp.float32,
        )
        return (new_peak, new_total, weighted * factor[:, None, :] + update)

    start_state = (
        jnp.full((HEADS, band_len), -1e30, jnp.float32),
        jnp.zeros((HEADS, band_len), jnp.float32),
        jnp.zeros((HEADS, HEAD_DIM, band_len), jnp.float32),
    )
    softmax_state = attend(start_state, slot_pairs)
    band_count = lax.axis_size("patch")

    def one_side(step_index, packed):
        state_now, ahead = packed
        ahead = banded_advance(ahead)
        return (attend(state_now, ahead), ahead)

    softmax_state, _ = lax.fori_loop(0, band_count - 1, one_side, (softmax_state, slot_pairs))
    _, row_total, weighted = banded_merged(softmax_state, ("chan", "sub"), banded_combine_parts)
    attended = (
        (weighted / row_total[:, None, :]).reshape(HEADS * HEAD_DIM, band_len).astype(jnp.bfloat16)
    )
    mixed = (
        projected.astype(jnp.float32) + jnp.dot(out_w, attended, preferred_element_type=jnp.float32)
    ).astype(jnp.bfloat16)
    columns = proj_out_w
    final_sum = resnet.astype(jnp.float32) + jnp.dot(
        columns,
        lax.all_gather(mixed, ("chan", "sub"), axis=0, tiled=True),
        preferred_element_type=jnp.float32,
    )
    return final_sum.astype(jnp.bfloat16)


def solution(mesh):
    in_specs = (
        P(("chan", "sub"), ("groups", "patch")),
        P("groups"),
        P(),
        P(("chan", "sub"), None),
        P(None, ("chan", "sub"), None),
        P(None, ("chan", "sub"), None),
        P(("chan", "sub"), None),
        P(("chan", "sub"), None),
        P(None, ("chan", "sub"), None),
        P(("chan", "sub"), None),
        P(("chan", "sub"), None),
    )
    out_specs = P(("chan", "sub"), ("groups", "patch"))

    few = mesh.shape["patch"] in (1, 2, 4) and mesh.shape["chan"] == 2 and mesh.shape["sub"] == 2

    def local(latent, *rest):
        if not few or latent.shape[1] != WIDTH:
            return banded(latent, *rest)
        return whole_rows(latent, *rest)

    return jax.shard_map(local, mesh=mesh, in_specs=in_specs, out_specs=out_specs, check_vma=False)
```

profile of v0, /device:TPU:0, one launch (start us, length us, event | category | flops | bytes accessed | tf_op | source)
XLA Modules:
  0.0 66.8 jit_solution(4883268297302822988)
XLA Ops:
  0.0 5.1 %collective-permute-start.2 = (bf16[160,256]{1,0:T(8,128)(2,1)}, bf16[160,256]{1,0:T(8,128)(2,1)S(1)}, u32[]{:S(2)}, u32[]{:S(2)}) collective-permute-start(bf16[160,256]{1,0:T(8,128)(2,1)} %refs_0_.1), channel_id=1, source_target_pairs={{0,12},{4,8},{8,4},{12,0},{1,13},{5,9},{9,5},{13,1},{2,14},{6,10},... | collective-permute-start | bytes 245768 | tf_op jit(solution)/shard_map/ppermute | solution.py:232
  5.6 1.7 %collective-permute-start.3 = (bf16[160,256]{1,0:T(8,128)(2,1)}, bf16[160,256]{1,0:T(8,128)(2,1)S(1)}, u32[]{:S(2)}, u32[]{:S(2)}) collective-permute-start(bf16[160,256]{1,0:T(8,128)(2,1)} %refs_0_.1), channel_id=1, source_target_pairs={{0,2},{2,0},{1,3},{3,1},{4,6},{6,4},{5,7},{7,5},{8,10},{10,8},{9,1... | collective-permute-start | bytes 245768 | tf_op jit(solution)/shard_map/ppermute | solution.py:232
  8.2 1.8 %collective-permute-start.6 = (bf16[160,256]{1,0:T(8,128)(2,1)S(1)}, bf16[160,256]{1,0:T(8,128)(2,1)S(1)}, u32[]{:S(2)}, u32[]{:S(2)}) collective-permute-start(bf16[160,256]{1,0:T(8,128)(2,1)S(1)} %collective-permute-done.2.refs_3_), channel_id=1, source_target_pairs={{0,2},{2,0},{1,3},{3,1},{4,6},{6,4},{5,7},{7,5},{8,10},{10,8},{9,1... | collective-permute-start | bytes 245768 | tf_op jit(solution)/shard_map/ppermute | solution.py:232
  10.0 2.1 %collective-permute-done.1.refs_2_ = bf16[160,256]{1,0:T(8,128)(2,1)S(1)} collective-permute-done((bf16[160,256]{1,0:T(8,128)(2,1)}, bf16[160,256]{1,0:T(8,128)(2,1)S(1)}, u32[]{:S(2)}, u32[]{:S(2)}) %collective-permute-start.1) | collective-permute-done | bytes 81952 | tf_op jit(solution)/shard_map/ppermute | solution.py:232
  12.2 1.5 %collective-permute-start.5 = (bf16[160,256]{1,0:T(8,128)(2,1)S(1)}, bf16[160,256]{1,0:T(8,128)(2,1)S(1)}, u32[]{:S(2)}, u32[]{:S(2)}) collective-permute-start(bf16[160,256]{1,0:T(8,128)(2,1)S(1)} %collective-permute-done.1.refs_2_), channel_id=1, source_target_pairs={{0,2},{2,0},{1,3},{3,1},{4,6},{6,4},{5,7},{7,5},{8,10},{10,8},{9,1... | collective-permute-start | bytes 245768 | tf_op jit(solution)/shard_map/ppermute | solution.py:232
  14.2 1.5 %copy-done.8 = bf16[9,160,640]{2,1,0:T(8,128)(2,1)S(1)} copy-done((bf16[9,160,640]{2,1,0:T(8,128)(2,1)S(1)}, bf16[9,160,640]{2,1,0:T(8,128)(2,1)}, u32[]{:S(2)}) %copy-start.8) | copy-done | bytes 1843224
  15.7 1.2 %shard_map.109 = (bf16[480,960]{1,0:T(8,128)(2,1)S(1)}, bf16[240,960]{1,0:T(8,128)(2,1)S(1)}, bf16[240,960]{1,0:T(8,128)(2,1)S(1)}) custom-call(bf16[9,160,640]{2,1,0:T(8,128)(2,1)S(1)} %copy-done.8), custom_call_target="tpu_custom_call" | custom-call | flops 1000000000 | bytes 1843200 | tf_op jit(solution)/shard_map/pallas_call | solution.py:33
  17.5 0.6 collective-permute-done.4.refs_5_
  18.1 0.9 %shard_map.111 = (bf16[4,160,256]{2,1,0:T(8,128)(2,1)S(1)}, bf16[2,4,80,256]{3,2,1,0:T(8,128)(2,1)S(1)}, bf16[2,4,80,256]{3,2,1,0:T(8,128)(2,1)S(1)}) custom-call(bf16[160,256]{1,0:T(8,128)(2,1)S(1)} %copy-done.7, bf16[160,256]{1,0:T(8,128)(2,1)S(1)} %collective-permute-done.refs_1_, bf16[160,256]{1,0:T(8,128)(2,1)S(1)} %collective-permute-done.1.refs_2_, ...), custom_call_target="tpu_custom_call" | custom-call | bytes 655360 | tf_op jit(solution)/shard_map/pallas_call | solution.py:33
  19.6 1.1 %collective-permute-start.15 = (bf16[160,640]{1,0:T(8,128)(2,1)S(1)}, bf16[160,640]{1,0:T(8,128)(2,1)S(1)}, u32[]{:S(2)}, u32[]{:S(2)}) collective-permute-start(bf16[160,640]{1,0:T(8,128)(2,1)S(1)} %copy-done.4), channel_id=1, source_target_pairs={{0,2},{2,0},{1,3},{3,1},{4,6},{6,4},{5,7},{7,5},{8,10},{10,8},{9,1... | collective-permute-start | bytes 614408 | tf_op jit(solution)/shard_map/ppermute | solution.py:232
  21.2 1.4 %shard_map.112 = (f32[4,80,256]{2,1,0:T(8,128)S(1)}, f32[4,80,256]{2,1,0:T(8,128)S(1)}) custom-call(bf16[2,4,80,256]{3,2,1,0:T(8,128)(2,1)S(1)} %get-tuple-element.84.refs_0_, bf16[2,4,80,256]{3,2,1,0:T(8,128)(2,1)S(1)} %collective-permute-done.8.refs_1_, bf16[480,960]{1,0:T(8,128)(2,1)S(1)} %get-tuple-element.85.refs_2_), custom_call_target="tpu_custom_call" | custom-call | flops 943718400 | bytes 1576960 | tf_op jit(solution)/shard_map/pallas_call | solution.py:33
  22.6 1.1 %shard_map.114.refs_0_ = bf16[4,80,256]{2,1,0:T(8,128)(2,1)S(1)} custom-call(bf16[2,4,80,256]{3,2,1,0:T(8,128)(2,1)S(1)} %get-tuple-element.82.refs_0_, bf16[2,4,80,256]{3,2,1,0:T(8,128)(2,1)S(1)} %collective-permute-done.7.refs_1_, bf16[240,960]{1,0:T(8,128)(2,1)S(1)} %get-tuple-element.90.refs_2_, f32[4,80,256]{2,1,0:T(8,128)S(1)} %get-tuple-element.91.refs_3_, ...), custom_call_target="tpu_custom_call" | custom-call | flops 471859200 | bytes 1444480 | tf_op jit(solution)/shard_map/pallas_call | solution.py:33
  23.7 3.3 %collective-permute-done.15.chan = bf16[160,640]{1,0:T(8,128)(2,1)S(1)} collective-permute-done((bf16[160,640]{1,0:T(8,128)(2,1)S(1)}, bf16[160,640]{1,0:T(8,128)(2,1)S(1)}, u32[]{:S(2)}, u32[]{:S(2)}) %collective-permute-start.15) | collective-permute-done | bytes 204832 | tf_op jit(solution)/shard_map/ppermute | solution.py:232
  27.0 1.1 %collective-permute-start.12 = (bf16[4,80,256]{2,1,0:T(8,128)(2,1)S(1)}, bf16[4,80,256]{2,1,0:T(8,128)(2,1)S(1)}, u32[]{:S(2)}, u32[]{:S(2)}) collective-permute-start(bf16[4,80,256]{2,1,0:T(8,128)(2,1)S(1)} %shard_map.114.refs_0_), channel_id=1, source_target_pairs={{0,2},{2,0},{1,3},{3,1},{4,6},{6,4},{5,7},{7,5},{8,10},{10,8},{9,1... | collective-permute-start | bytes 491528 | tf_op jit(solution)/shard_map/ppermute | solution.py:232
  28.2 1.1 %shard_map.113.refs_0_ = bf16[4,80,256]{2,1,0:T(8,128)(2,1)S(1)} custom-call(bf16[2,4,80,256]{3,2,1,0:T(8,128)(2,1)S(1)} %get-tuple-element.82.refs_0_, bf16[2,4,80,256]{3,2,1,0:T(8,128)(2,1)S(1)} %collective-permute-done.7.refs_1_, bf16[240,960]{1,0:T(8,128)(2,1)S(1)} %get-tuple-element.83.refs_2_, f32[4,80,256]{2,1,0:T(8,128)S(1)} %get-tuple-element.86.refs_3_, ...), custom_call_target="tpu_custom_call" | custom-call | flops 471859200 | bytes 1444480 | tf_op jit(solution)/shard_map/pallas_call | solution.py:33
  29.3 1.0 %collective-permute-start.9 = (bf16[4,80,256]{2,1,0:T(8,128)(2,1)S(1)}, bf16[4,80,256]{2,1,0:T(8,128)(2,1)S(1)}, u32[]{:S(2)}, u32[]{:S(2)}) collective-permute-start(bf16[4,80,256]{2,1,0:T(8,128)(2,1)S(1)} %shard_map.113.refs_0_), channel_id=1, source_target_pairs={{0,2},{2,0},{1,3},{3,1},{4,6},{6,4},{5,7},{7,5},{8,10},{10,8},{9,1... | collective-permute-start | bytes 491528 | tf_op jit(solution)/shard_map/ppermute | solution.py:232
  30.4 1.2 %shard_map.116 = (bf16[480,960]{1,0:T(8,128)(2,1)S(1)}, bf16[240,960]{1,0:T(8,128)(2,1)S(1)}, bf16[240,960]{1,0:T(8,128)(2,1)S(1)}) custom-call(bf16[9,160,640]{2,1,0:T(8,128)(2,1)S(1)} %copy-done.9), custom_call_target="tpu_custom_call" | custom-call | flops 1000000000 | bytes 1843200 | tf_op jit(solution)/shard_map/pallas_call | solution.py:33
  31.7 2.5 %collective-permute-done.12.refs_1_ = bf16[4,80,256]{2,1,0:T(8,128)(2,1)S(1)} collective-permute-done((bf16[4,80,256]{2,1,0:T(8,128)(2,1)S(1)}, bf16[4,80,256]{2,1,0:T(8,128)(2,1)S(1)}, u32[]{:S(2)}, u32[]{:S(2)}) %collective-permute-start.12) | collective-permute-done | bytes 163872 | tf_op jit(solution)/shard_map/ppermute | solution.py:232
  34.7 2.5 %collective-permute-done.9.refs_1_ = bf16[4,80,256]{2,1,0:T(8,128)(2,1)S(1)} collective-permute-done((bf16[4,80,256]{2,1,0:T(8,128)(2,1)S(1)}, bf16[4,80,256]{2,1,0:T(8,128)(2,1)S(1)}, u32[]{:S(2)}, u32[]{:S(2)}) %collective-permute-start.9) | collective-permute-done | bytes 163872 | tf_op jit(solution)/shard_map/ppermute | solution.py:232
  37.7 1.4 %shard_map.117 = (f32[4,80,256]{2,1,0:T(8,128)S(1)}, f32[4,80,256]{2,1,0:T(8,128)S(1)}) custom-call(bf16[4,80,256]{2,1,0:T(8,128)(2,1)S(1)} %shard_map.114.refs_0_, bf16[4,80,256]{2,1,0:T(8,128)(2,1)S(1)} %collective-permute-done.12.refs_1_, bf16[4,80,256]{2,1,0:T(8,128)(2,1)S(1)} %collective-permute-done.18.refs_2_, ...), custom_call_target="tpu_custom_call" | custom-call | flops 943718400 | bytes 1576960 | tf_op jit(solution)/shard_map/pallas_call | solution.py:33
  39.1 1.1 %shard_map.118 = (bf16[4,80,256]{2,1,0:T(8,128)(2,1)S(1)}, bf16[80,256]{1,0:T(8,128)(2,1)S(1)}) custom-call(bf16[4,80,256]{2,1,0:T(8,128)(2,1)S(1)} %shard_map.113.refs_0_, bf16[4,80,256]{2,1,0:T(8,128)(2,1)S(1)} %collective-permute-done.9.refs_1_, bf16[4,80,256]{2,1,0:T(8,128)(2,1)S(1)} %collective-permute-done.10.refs_2_, ...), custom_call_target="tpu_custom_call" | custom-call | flops 471859200 | bytes 1771520 | tf_op jit(solution)/shard_map/pallas_call | solution.py:33
  40.3 1.1 %shard_map.120 = (bf16[4,80,256]{2,1,0:T(8,128)(2,1)S(1)}, bf16[80,256]{1,0:T(8,128)(2,1)S(1)}) custom-call(bf16[4,80,256]{2,1,0:T(8,128)(2,1)S(1)} %shard_map.113.refs_0_, bf16[4,80,256]{2,1,0:T(8,128)(2,1)S(1)} %collective-permute-done.9.refs_1_, bf16[4,80,256]{2,1,0:T(8,128)(2,1)S(1)} %collective-permute-done.10.refs_2_, ...), custom_call_target="tpu_custom_call" | custom-call | flops 471859200 | bytes 1771520 | tf_op jit(solution)/shard_map/pallas_call | solution.py:33
  41.4 1.1 %collective-permute-start.24 = (bf16[4,80,256]{2,1,0:T(8,128)(2,1)S(1)}, bf16[4,80,256]{2,1,0:T(8,128)(2,1)S(1)}, u32[]{:S(2)}, u32[]{:S(2)}) collective-permute-start(bf16[4,80,256]{2,1,0:T(8,128)(2,1)S(1)} %get-tuple-element.127.refs_4_), channel_id=1, source_target_pairs={{0,2},{2,0},{1,3},{3,1},{4,6},{6,4},{5,7},{7,5},{8,10},{10,8},{9,1... | collective-permute-start | bytes 491528 | tf_op jit(solution)/shard_map/ppermute | solution.py:232
  42.5 1.0 %collective-permute-start.20 = (bf16[4,80,256]{2,1,0:T(8,128)(2,1)S(1)}, bf16[4,80,256]{2,1,0:T(8,128)(2,1)S(1)}, u32[]{:S(2)}, u32[]{:S(2)}) collective-permute-start(bf16[4,80,256]{2,1,0:T(8,128)(2,1)S(1)} %get-tuple-element.122.refs_0_), channel_id=1, source_target_pairs={{0,2},{2,0},{1,3},{3,1},{4,6},{6,4},{5,7},{7,5},{8,10},{10,8},{9,1... | collective-permute-start | bytes 491528 | tf_op jit(solution)/shard_map/ppermute | solution.py:232
  43.6 5.0 %collective-permute-done.24.refs_5_ = bf16[4,80,256]{2,1,0:T(8,128)(2,1)S(1)} collective-permute-done((bf16[4,80,256]{2,1,0:T(8,128)(2,1)S(1)}, bf16[4,80,256]{2,1,0:T(8,128)(2,1)S(1)}, u32[]{:S(2)}, u32[]{:S(2)}) %collective-permute-start.24) | collective-permute-done | bytes 163872 | tf_op jit(solution)/shard_map/ppermute | solution.py:232
  49.0 2.5 %collective-permute-done.20.refs_1_ = bf16[4,80,256]{2,1,0:T(8,128)(2,1)S(1)} collective-permute-done((bf16[4,80,256]{2,1,0:T(8,128)(2,1)S(1)}, bf16[4,80,256]{2,1,0:T(8,128)(2,1)S(1)}, u32[]{:S(2)}, u32[]{:S(2)}) %collective-permute-start.20) | collective-permute-done | bytes 163872 | tf_op jit(solution)/shard_map/ppermute | solution.py:232
  52.1 1.1 %collective-permute-start.28 = (bf16[160,640]{1,0:T(8,128)(2,1)S(1)}, bf16[160,640]{1,0:T(8,128)(2,1)S(1)}, u32[]{:S(2)}, u32[]{:S(2)}) collective-permute-start(bf16[160,640]{1,0:T(8,128)(2,1)S(1)} %copy-done.5), channel_id=1, source_target_pairs={{0,2},{2,0},{1,3},{3,1},{4,6},{6,4},{5,7},{7,5},{8,10},{10,8},{9,1... | collective-permute-start | bytes 614408 | tf_op jit(solution)/shard_map/ppermute | solution.py:232
  53.2 5.5 %shard_map.121 = (bf16[320,128]{1,0:T(8,128)(2,1)S(1)}, bf16[640,256]{1,0:T(8,128)(2,1)S(1)}) custom-call(bf16[4,80,256]{2,1,0:T(8,128)(2,1)S(1)} %get-tuple-element.122.refs_0_, bf16[4,80,256]{2,1,0:T(8,128)(2,1)S(1)} %collective-permute-done.20.refs_1_, bf16[4,80,256]{2,1,0:T(8,128)(2,1)S(1)} %collective-permute-done.22.refs_2_, ...), custom_call_target="tpu_custom_call" | custom-call | flops 4000000000 | bytes 3358720 | tf_op jit(solution)/shard_map/pallas_call | solution.py:33
  59.1 1.1 %collective-permute-start.27 = (bf16[320,128]{1,0:T(8,128)(2,1)S(1)}, bf16[320,128]{1,0:T(8,128)(2,1)S(1)}, u32[]{:S(2)}, u32[]{:S(2)}) collective-permute-start(bf16[320,128]{1,0:T(8,128)(2,1)S(1)} %get-tuple-element.137.own), channel_id=1, source_target_pairs={{0,2},{2,0},{1,3},{3,1},{4,6},{6,4},{5,7},{7,5},{8,10},{10,8},{9,1... | collective-permute-start | bytes 245768 | tf_op jit(solution)/shard_map/ppermute | solution.py:232
  60.7 3.3 %collective-permute-done.27.chan = bf16[320,128]{1,0:T(8,128)(2,1)S(1)} collective-permute-done((bf16[320,128]{1,0:T(8,128)(2,1)S(1)}, bf16[320,128]{1,0:T(8,128)(2,1)S(1)}, u32[]{:S(2)}, u32[]{:S(2)}) %collective-permute-start.27) | collective-permute-done | bytes 81952 | tf_op jit(solution)/shard_map/ppermute | solution.py:232
  64.5 0.8 %collective-permute-done.30.sub = bf16[320,128]{1,0:T(8,128)(2,1)S(1)} collective-permute-done((bf16[320,128]{1,0:T(8,128)(2,1)S(1)}, bf16[320,128]{1,0:T(8,128)(2,1)S(1)}, u32[]{:S(2)}, u32[]{:S(2)}) %collective-permute-start.30) | collective-permute-done | bytes 81952 | tf_op jit(solution)/shard_map/ppermute | solution.py:232
  65.4 1.4 %shard_map.123 = bf16[160,256]{1,0:T(8,128)(2,1)} custom-call(bf16[320,128]{1,0:T(8,128)(2,1)S(1)} %get-tuple-element.137.own, bf16[320,128]{1,0:T(8,128)(2,1)S(1)} %collective-permute-done.27.chan, bf16[320,128]{1,0:T(8,128)(2,1)S(1)} %collective-permute-done.30.sub, bf16[320,128]{1,0:T(8,128)(2,1)S(1)} %collective-permute-done.31.both, ...), custom_call_target="tpu_custom_call" | custom-call | bytes 1761280 | tf_op jit(solution)/shard_map/pallas_call | solution.py:33
  (71 shorter events, 6.9 us)
Async XLA Ops:
  0.0 8.2 %collective-permute-start.2 = (bf16[160,256]{1,0:T(8,128)(2,1)}, bf16[160,256]{1,0:T(8,128)(2,1)S(1)}, u32[]{:S(2)}, u32[]{:S(2)}) collective-permute-start(bf16[160,256]{1,0:T(8,128)(2,1)} %refs_0_.1), channel_id=1, source_target_pairs={{0,12},{4,8},{8,4},{12,0},{1,13},{5,9},{9,5},{13,1},{2,14},{6,10},... | collective-permute-start | bytes 245768 | tf_op jit(solution)/shard_map/ppermute | solution.py:232
  5.1 7.1 %collective-permute-start.1 = (bf16[160,256]{1,0:T(8,128)(2,1)}, bf16[160,256]{1,0:T(8,128)(2,1)S(1)}, u32[]{:S(2)}, u32[]{:S(2)}) collective-permute-start(bf16[160,256]{1,0:T(8,128)(2,1)} %refs_0_.1), channel_id=1, source_target_pairs={{0,8},{4,12},{8,0},{12,4},{1,9},{5,13},{9,1},{13,5},{2,10},{6,14},... | collective-permute-start | bytes 245768 | tf_op jit(solution)/shard_map/ppermute | solution.py:232
  5.1 8.6 %collective-permute-start = (bf16[160,256]{1,0:T(8,128)(2,1)}, bf16[160,256]{1,0:T(8,128)(2,1)S(1)}, u32[]{:S(2)}, u32[]{:S(2)}) collective-permute-start(bf16[160,256]{1,0:T(8,128)(2,1)} %refs_0_.1), channel_id=1, source_target_pairs={{0,4},{4,0},{8,12},{12,8},{1,5},{5,1},{9,13},{13,9},{2,6},{6,2},{1... | collective-permute-start | bytes 245768 | tf_op jit(solution)/shard_map/ppermute | solution.py:232
  5.6 11.8 %collective-permute-start.3 = (bf16[160,256]{1,0:T(8,128)(2,1)}, bf16[160,256]{1,0:T(8,128)(2,1)S(1)}, u32[]{:S(2)}, u32[]{:S(2)}) collective-permute-start(bf16[160,256]{1,0:T(8,128)(2,1)} %refs_0_.1), channel_id=1, source_target_pairs={{0,2},{2,0},{1,3},{3,1},{4,6},{6,4},{5,7},{7,5},{8,10},{10,8},{9,1... | collective-permute-start | bytes 245768 | tf_op jit(solution)/shard_map/ppermute | solution.py:232
  8.2 9.2 %collective-permute-start.6 = (bf16[160,256]{1,0:T(8,128)(2,1)S(1)}, bf16[160,256]{1,0:T(8,128)(2,1)S(1)}, u32[]{:S(2)}, u32[]{:S(2)}) collective-permute-start(bf16[160,256]{1,0:T(8,128)(2,1)S(1)} %collective-permute-done.2.refs_3_), channel_id=1, source_target_pairs={{0,2},{2,0},{1,3},{3,1},{4,6},{6,4},{5,7},{7,5},{8,10},{10,8},{9,1... | collective-permute-start | bytes 245768 | tf_op jit(solution)/shard_map/ppermute | solution.py:232
  12.2 5.3 %collective-permute-start.5 = (bf16[160,256]{1,0:T(8,128)(2,1)S(1)}, bf16[160,256]{1,0:T(8,128)(2,1)S(1)}, u32[]{:S(2)}, u32[]{:S(2)}) collective-permute-start(bf16[160,256]{1,0:T(8,128)(2,1)S(1)} %collective-permute-done.1.refs_2_), channel_id=1, source_target_pairs={{0,2},{2,0},{1,3},{3,1},{4,6},{6,4},{5,7},{7,5},{8,10},{10,8},{9,1... | collective-permute-start | bytes 245768 | tf_op jit(solution)/shard_map/ppermute | solution.py:232
  13.6 4.4 %collective-permute-start.4 = (bf16[160,256]{1,0:T(8,128)(2,1)S(1)}, bf16[160,256]{1,0:T(8,128)(2,1)S(1)}, u32[]{:S(2)}, u32[]{:S(2)}) collective-permute-start(bf16[160,256]{1,0:T(8,128)(2,1)S(1)} %collective-permute-done.refs_1_), channel_id=1, source_target_pairs={{0,2},{2,0},{1,3},{3,1},{4,6},{6,4},{5,7},{7,5},{8,10},{10,8},{9,1... | collective-permute-start | bytes 245768 | tf_op jit(solution)/shard_map/ppermute | solution.py:232
  19.0 1.9 %collective-permute-start.8 = (bf16[2,4,80,256]{3,2,1,0:T(8,128)(2,1)S(1)}, bf16[2,4,80,256]{3,2,1,0:T(8,128)(2,1)S(1)}, u32[]{:S(2)}, u32[]{:S(2)}) collective-permute-start(bf16[2,4,80,256]{3,2,1,0:T(8,128)(2,1)S(1)} %get-tuple-element.84.refs_0_), channel_id=1, source_target_pairs={{0,1},{1,0},{2,3},{3,2},{4,5},{5,4},{6,7},{7,6},{8,9},{9,8},{10,11... | collective-permute-start | bytes 983048 | tf_op jit(solution)/shard_map/ppermute | solution.py:232
  19.0 8.0 %collective-permute-start.14 = (bf16[2,160,640]{2,1,0:T(8,128)(2,1)S(1)}, bf16[2,160,640]{2,1,0:T(8,128)(2,1)S(1)}, u32[]{:S(2)}, u32[]{:S(2)}) collective-permute-start(bf16[2,160,640]{2,1,0:T(8,128)(2,1)S(1)} %copy-done.2), channel_id=1, source_target_pairs={{0,1},{1,0},{2,3},{3,2},{4,5},{5,4},{6,7},{7,6},{8,9},{9,8},{10,11... | collective-permute-start | bytes 1228808 | tf_op jit(solution)/shard_map/ppermute | solution.py:232
  19.5 3.0 %collective-permute-start.7 = (bf16[2,4,80,256]{3,2,1,0:T(8,128)(2,1)S(1)}, bf16[2,4,80,256]{3,2,1,0:T(8,128)(2,1)S(1)}, u32[]{:S(2)}, u32[]{:S(2)}) collective-permute-start(bf16[2,4,80,256]{3,2,1,0:T(8,128)(2,1)S(1)} %get-tuple-element.82.refs_0_), channel_id=1, source_target_pairs={{0,1},{1,0},{2,3},{3,2},{4,5},{5,4},{6,7},{7,6},{8,9},{9,8},{10,11... | collective-permute-start | bytes 983048 | tf_op jit(solution)/shard_map/ppermute | solution.py:232
  19.6 7.4 %collective-permute-start.15 = (bf16[160,640]{1,0:T(8,128)(2,1)S(1)}, bf16[160,640]{1,0:T(8,128)(2,1)S(1)}, u32[]{:S(2)}, u32[]{:S(2)}) collective-permute-start(bf16[160,640]{1,0:T(8,128)(2,1)S(1)} %copy-done.4), channel_id=1, source_target_pairs={{0,2},{2,0},{1,3},{3,1},{4,6},{6,4},{5,7},{7,5},{8,10},{10,8},{9,1... | collective-permute-start | bytes 614408 | tf_op jit(solution)/shard_map/ppermute | solution.py:232
  20.7 6.3 %collective-permute-start.13 = (bf16[160,640]{1,0:T(8,128)(2,1)S(1)}, bf16[160,640]{1,0:T(8,128)(2,1)S(1)}, u32[]{:S(2)}, u32[]{:S(2)}) collective-permute-start(bf16[160,640]{1,0:T(8,128)(2,1)S(1)} %copy-done.3), channel_id=1, source_target_pairs={{0,1},{1,0},{2,3},{3,2},{4,5},{5,4},{6,7},{7,6},{8,9},{9,8},{10,11... | collective-permute-start | bytes 614408 | tf_op jit(solution)/shard_map/ppermute | solution.py:232
  20.8 10.8 %collective-permute-start.16 = (bf16[160,640]{1,0:T(8,128)(2,1)S(1)}, bf16[160,640]{1,0:T(8,128)(2,1)S(1)}, u32[]{:S(2)}, u32[]{:S(2)}) collective-permute-start(bf16[160,640]{1,0:T(8,128)(2,1)S(1)} %copy-done.4), channel_id=1, source_target_pairs={{0,1},{1,0},{2,3},{3,2},{4,5},{5,4},{6,7},{7,6},{8,9},{9,8},{10,11... | collective-permute-start | bytes 614408 | tf_op jit(solution)/shard_map/ppermute | solution.py:232
  27.0 7.1 %collective-permute-start.17 = (bf16[160,640]{1,0:T(8,128)(2,1)S(1)}, bf16[160,640]{1,0:T(8,128)(2,1)S(1)}, u32[]{:S(2)}, u32[]{:S(2)}) collective-permute-start(bf16[160,640]{1,0:T(8,128)(2,1)S(1)} %collective-permute-done.15.chan), channel_id=1, source_target_pairs={{0,1},{1,0},{2,3},{3,2},{4,5},{5,4},{6,7},{7,6},{8,9},{9,8},{10,11... | collective-permute-start | bytes 614408 | tf_op jit(solution)/shard_map/ppermute | solution.py:232
  27.0 7.1 %collective-permute-start.12 = (bf16[4,80,256]{2,1,0:T(8,128)(2,1)S(1)}, bf16[4,80,256]{2,1,0:T(8,128)(2,1)S(1)}, u32[]{:S(2)}, u32[]{:S(2)}) collective-permute-start(bf16[4,80,256]{2,1,0:T(8,128)(2,1)S(1)} %shard_map.114.refs_0_), channel_id=1, source_target_pairs={{0,2},{2,0},{1,3},{3,1},{4,6},{6,4},{5,7},{7,5},{8,10},{10,8},{9,1... | collective-permute-start | bytes 491528 | tf_op jit(solution)/shard_map/ppermute | solution.py:232
  29.3 7.9 %collective-permute-start.9 = (bf16[4,80,256]{2,1,0:T(8,128)(2,1)S(1)}, bf16[4,80,256]{2,1,0:T(8,128)(2,1)S(1)}, u32[]{:S(2)}, u32[]{:S(2)}) collective-permute-start(bf16[4,80,256]{2,1,0:T(8,128)(2,1)S(1)} %shard_map.113.refs_0_), channel_id=1, source_target_pairs={{0,2},{2,0},{1,3},{3,1},{4,6},{6,4},{5,7},{7,5},{8,10},{10,8},{9,1... | collective-permute-start | bytes 491528 | tf_op jit(solution)/shard_map/ppermute | solution.py:232
  34.2 3.5 %collective-permute-start.18 = (bf16[4,80,256]{2,1,0:T(8,128)(2,1)S(1)}, bf16[4,80,256]{2,1,0:T(8,128)(2,1)S(1)}, u32[]{:S(2)}, u32[]{:S(2)}) collective-permute-start(bf16[4,80,256]{2,1,0:T(8,128)(2,1)S(1)} %shard_map.114.refs_0_), channel_id=1, source_target_pairs={{0,1},{1,0},{2,3},{3,2},{4,5},{5,4},{6,7},{7,6},{8,9},{9,8},{10,11... | collective-permute-start | bytes 491528 | tf_op jit(solution)/shard_map/ppermute | solution.py:232
  34.2 3.5 %collective-permute-start.19 = (bf16[4,80,256]{2,1,0:T(8,128)(2,1)S(1)}, bf16[4,80,256]{2,1,0:T(8,128)(2,1)S(1)}, u32[]{:S(2)}, u32[]{:S(2)}) collective-permute-start(bf16[4,80,256]{2,1,0:T(8,128)(2,1)S(1)} %collective-permute-done.12.refs_1_), channel_id=1, source_target_pairs={{0,1},{1,0},{2,3},{3,2},{4,5},{5,4},{6,7},{7,6},{8,9},{9,8},{10,11... | collective-permute-start | bytes 491528 | tf_op jit(solution)/shard_map/ppermute | solution.py:232
  37.2 1.9 %collective-permute-start.10 = (bf16[4,80,256]{2,1,0:T(8,128)(2,1)S(1)}, bf16[4,80,256]{2,1,0:T(8,128)(2,1)S(1)}, u32[]{:S(2)}, u32[]{:S(2)}) collective-permute-start(bf16[4,80,256]{2,1,0:T(8,128)(2,1)S(1)} %shard_map.113.refs_0_), channel_id=1, source_target_pairs={{0,1},{1,0},{2,3},{3,2},{4,5},{5,4},{6,7},{7,6},{8,9},{9,8},{10,11... | collective-permute-start | bytes 491528 | tf_op jit(solution)/shard_map/ppermute | solution.py:232
  37.2 1.9 %collective-permute-start.11 = (bf16[4,80,256]{2,1,0:T(8,128)(2,1)S(1)}, bf16[4,80,256]{2,1,0:T(8,128)(2,1)S(1)}, u32[]{:S(2)}, u32[]{:S(2)}) collective-permute-start(bf16[4,80,256]{2,1,0:T(8,128)(2,1)S(1)} %collective-permute-done.9.refs_1_), channel_id=1, source_target_pairs={{0,1},{1,0},{2,3},{3,2},{4,5},{5,4},{6,7},{7,6},{8,9},{9,8},{10,11... | collective-permute-start | bytes 491528 | tf_op jit(solution)/shard_map/ppermute | solution.py:232
  40.2 11.4 %collective-permute-start.21 = (bf16[160,640]{1,0:T(8,128)(2,1)S(1)}, bf16[160,640]{1,0:T(8,128)(2,1)S(1)}, u32[]{:S(2)}, u32[]{:S(2)}) collective-permute-start(bf16[160,640]{1,0:T(8,128)(2,1)S(1)} %copy-done.5), channel_id=1, source_target_pairs={{0,1},{1,0},{2,3},{3,2},{4,5},{5,4},{6,7},{7,6},{8,9},{9,8},{10,11... | collective-permute-start | bytes 614408 | tf_op jit(solution)/shard_map/ppermute | solution.py:232
  41.4 7.1 %collective-permute-start.24 = (bf16[4,80,256]{2,1,0:T(8,128)(2,1)S(1)}, bf16[4,80,256]{2,1,0:T(8,128)(2,1)S(1)}, u32[]{:S(2)}, u32[]{:S(2)}) collective-permute-start(bf16[4,80,256]{2,1,0:T(8,128)(2,1)S(1)} %get-tuple-element.127.refs_4_), channel_id=1, source_target_pairs={{0,2},{2,0},{1,3},{3,1},{4,6},{6,4},{5,7},{7,5},{8,10},{10,8},{9,1... | collective-permute-start | bytes 491528 | tf_op jit(solution)/shard_map/ppermute | solution.py:232
  42.5 9.0 %collective-permute-start.20 = (bf16[4,80,256]{2,1,0:T(8,128)(2,1)S(1)}, bf16[4,80,256]{2,1,0:T(8,128)(2,1)S(1)}, u32[]{:S(2)}, u32[]{:S(2)}) collective-permute-start(bf16[4,80,256]{2,1,0:T(8,128)(2,1)S(1)} %get-tuple-element.122.refs_0_), channel_id=1, source_target_pairs={{0,2},{2,0},{1,3},{3,1},{4,6},{6,4},{5,7},{7,5},{8,10},{10,8},{9,1... | collective-permute-start | bytes 491528 | tf_op jit(solution)/shard_map/ppermute | solution.py:232
  48.5 3.6 %collective-permute-start.25 = (bf16[4,80,256]{2,1,0:T(8,128)(2,1)S(1)}, bf16[4,80,256]{2,1,0:T(8,128)(2,1)S(1)}, u32[]{:S(2)}, u32[]{:S(2)}) collective-permute-start(bf16[4,80,256]{2,1,0:T(8,128)(2,1)S(1)} %get-tuple-element.127.refs_4_), channel_id=1, source_target_pairs={{0,1},{1,0},{2,3},{3,2},{4,5},{5,4},{6,7},{7,6},{8,9},{9,8},{10,11... | collective-permute-start | bytes 491528 | tf_op jit(solution)/shard_map/ppermute | solution.py:232
  48.5 3.6 %collective-permute-start.26 = (bf16[4,80,256]{2,1,0:T(8,128)(2,1)S(1)}, bf16[4,80,256]{2,1,0:T(8,128)(2,1)S(1)}, u32[]{:S(2)}, u32[]{:S(2)}) collective-permute-start(bf16[4,80,256]{2,1,0:T(8,128)(2,1)S(1)} %collective-permute-done.24.refs_5_), channel_id=1, source_target_pairs={{0,1},{1,0},{2,3},{3,2},{4,5},{5,4},{6,7},{7,6},{8,9},{9,8},{10,11... | collective-permute-start | bytes 491528 | tf_op jit(solution)/shard_map/ppermute | solution.py:232
  51.5 1.6 %collective-permute-start.22 = (bf16[4,80,256]{2,1,0:T(8,128)(2,1)S(1)}, bf16[4,80,256]{2,1,0:T(8,128)(2,1)S(1)}, u32[]{:S(2)}, u32[]{:S(2)}) collective-permute-start(bf16[4,80,256]{2,1,0:T(8,128)(2,1)S(1)} %get-tuple-element.122.refs_0_), channel_id=1, source_target_pairs={{0,1},{1,0},{2,3},{3,2},{4,5},{5,4},{6,7},{7,6},{8,9},{9,8},{10,11... | collective-permute-start | bytes 491528 | tf_op jit(solution)/shard_map/ppermute | solution.py:232
  51.5 1.6 %collective-permute-start.23 = (bf16[4,80,256]{2,1,0:T(8,128)(2,1)S(1)}, bf16[4,80,256]{2,1,0:T(8,128)(2,1)S(1)}, u32[]{:S(2)}, u32[]{:S(2)}) collective-permute-start(bf16[4,80,256]{2,1,0:T(8,128)(2,1)S(1)} %collective-permute-done.20.refs_1_), channel_id=1, source_target_pairs={{0,1},{1,0},{2,3},{3,2},{4,5},{5,4},{6,7},{7,6},{8,9},{9,8},{10,11... | collective-permute-start | bytes 491528 | tf_op jit(solution)/shard_map/ppermute | solution.py:232
  52.1 7.1 %collective-permute-start.28 = (bf16[160,640]{1,0:T(8,128)(2,1)S(1)}, bf16[160,640]{1,0:T(8,128)(2,1)S(1)}, u32[]{:S(2)}, u32[]{:S(2)}) collective-permute-start(bf16[160,640]{1,0:T(8,128)(2,1)S(1)} %copy-done.5), channel_id=1, source_target_pairs={{0,2},{2,0},{1,3},{3,1},{4,6},{6,4},{5,7},{7,5},{8,10},{10,8},{9,1... | collective-permute-start | bytes 614408 | tf_op jit(solution)/shard_map/ppermute | solution.py:232
  59.1 1.5 %collective-permute-start.29 = (bf16[160,640]{1,0:T(8,128)(2,1)S(1)}, bf16[160,640]{1,0:T(8,128)(2,1)S(1)}, u32[]{:S(2)}, u32[]{:S(2)}) collective-permute-start(bf16[160,640]{1,0:T(8,128)(2,1)S(1)} %collective-permute-done.28.chan), channel_id=1, source_target_pairs={{0,1},{1,0},{2,3},{3,2},{4,5},{5,4},{6,7},{7,6},{8,9},{9,8},{10,11... | collective-permute-start | bytes 614408 | tf_op jit(solution)/shard_map/ppermute | solution.py:232
  59.1 4.9 %collective-permute-start.27 = (bf16[320,128]{1,0:T(8,128)(2,1)S(1)}, bf16[320,128]{1,0:T(8,128)(2,1)S(1)}, u32[]{:S(2)}, u32[]{:S(2)}) collective-permute-start(bf16[320,128]{1,0:T(8,128)(2,1)S(1)} %get-tuple-element.137.own), channel_id=1, source_target_pairs={{0,2},{2,0},{1,3},{3,1},{4,6},{6,4},{5,7},{7,5},{8,10},{10,8},{9,1... | collective-permute-start | bytes 245768 | tf_op jit(solution)/shard_map/ppermute | solution.py:232
  64.0 1.3 %collective-permute-start.30 = (bf16[320,128]{1,0:T(8,128)(2,1)S(1)}, bf16[320,128]{1,0:T(8,128)(2,1)S(1)}, u32[]{:S(2)}, u32[]{:S(2)}) collective-permute-start(bf16[320,128]{1,0:T(8,128)(2,1)S(1)} %get-tuple-element.137.own), channel_id=1, source_target_pairs={{0,1},{1,0},{2,3},{3,2},{4,5},{5,4},{6,7},{7,6},{8,9},{9,8},{10,11... | collective-permute-start | bytes 245768 | tf_op jit(solution)/shard_map/ppermute | solution.py:232
  64.0 1.4 %collective-permute-start.31 = (bf16[320,128]{1,0:T(8,128)(2,1)S(1)}, bf16[320,128]{1,0:T(8,128)(2,1)S(1)}, u32[]{:S(2)}, u32[]{:S(2)}) collective-permute-start(bf16[320,128]{1,0:T(8,128)(2,1)S(1)} %collective-permute-done.27.chan), channel_id=1, source_target_pairs={{0,1},{1,0},{2,3},{3,2},{4,5},{5,4},{6,7},{7,6},{8,9},{9,8},{10,11... | collective-permute-start | bytes 245768 | tf_op jit(solution)/shard_map/ppermute | solution.py:232
  (10 other events, 72.2 us)
where the time goes:
time: 66.9 us; the launch traced here: 66.8 us
  waiting for transfers between devices  23.7 us (35%)
  starting transfers between devices  22.4 us (33%)
  Pallas kernels  18 us (27%)
  local copies, waits for them, and re-layouts  1.56 us (2%)
  between operations  0.95 us (1%)
    ppermute x32, waiting for transfers between devices, swapped(): lax.ppermute(array, axis, [(i, i ^ by) for i in range(lax.axis_size(axis))])  23.7 us
    ppermute x32, starting transfers between devices, swapped(): lax.ppermute(array, axis, [(i, i ^ by) for i in range(lax.axis_size(axis))])  22.4 us
    pallas_call x15, Pallas kernels, call(): pl.pallas_call(kernel, out_shape=[jax.ShapeDtypeStruct(s, t) for s, t in...  18 us
    unnamed x20, local copies, waits for them, and re-layouts  1.55 us
  transfers between devices with their start and end apart: 32, of which 13 were waited for; matrix products, arithmetic and copies ran while one was open for 0% of the time, Pallas kernels for 22%

commit v1 on v0

--- a/solution.py
+++ b/solution.py
@@ -169,18 +169,18 @@
         full[pl.ds(pl.multiple_of((own_place() ^ flip) * OWN, 16), OWN), :] = block[...]
 
 
-def stack_heads(q_own, kv_own, q_sub, kv_sub, q_ref, k_ref, v_ref):
-    here = pl.multiple_of(lax.axis_index("sub") * OWN, 16)
-    there = pl.multiple_of((1 - lax.axis_index("sub")) * OWN, 16)
-    for at, q_part, kv_part in ((here, q_own, kv_own), (there, q_sub, kv_sub)):
+def stack_heads(q_own, kv_own, q_sub, kv_sub, q_ref, kv_ref):
+    here = lax.axis_index("sub") * OWN
+    for at, q_part, kv_part in ((here, q_own, kv_own), (OWN - here, q_sub, kv_sub)):
+        at = pl.multiple_of(at, 16)
         q_ref[pl.ds(at, OWN), :] = q_part[...]
-        k_ref[pl.ds(at, OWN), :] = kv_part[0]
-        v_ref[pl.ds(at, OWN), :] = kv_part[1]
+        kv_ref[pl.ds(at, OWN), :] = kv_part[0]
+        kv_ref[pl.ds(at + 2 * OWN, OWN), :] = kv_part[1]
 
 
 def attend(*refs):
     blocks, refs = refs[:8], refs[8:]
-    proj_w, q_w, k_w, v_w, out_ref, proj_ref, normed, projected, layered, keys, values = refs
+    proj_w, q_w, kv_w, out_ref, proj_ref, normed, projected, layered, heads = refs
     rows = normed.shape[0]
     for half in range(2):
         for flip, block in zip(FLIPS, blocks[half * 4 : half * 4 + 4]):
@@ -195,20 +195,24 @@
         layer = (shifted * lax.rsqrt(spread + 1e-05)).astype(BF16)
         layered[row] = layer
         at = slice(row * WIDTH, (row + 1) * WIDTH)
-        keys[:, at] = jnp.dot(k_w[...], layer, preferred_element_type=F32).astype(BF16)
-        values[:, at] = jnp.dot(v_w[...], layer, preferred_element_type=F32).astype(BF16)
+        heads[:, at] = jnp.dot(kv_w[...], layer, preferred_element_type=F32).astype(BF16)
     proj_ref[...] = projected[lax.axis_index("patch")]
     share = out_ref.shape[1]
     mine = layered[lax.axis_index("patch"), :, pl.ds(pl.multiple_of(lax.axis_index("sub") * share, 128), share)]
     query = (jnp.dot(q_w[...], mine, preferred_element_type=F32) * 0.125).astype(BF16)
-    for head in range(query.shape[0] // HEAD_DIM):
-        at = slice(head * HEAD_DIM, (head + 1) * HEAD_DIM)
+    channels = query.shape[0]
+    for start in range(0, channels, HEAD_DIM):
+        at = slice(start, start + HEAD_DIM)
         scores = lax.dot_general(
-            keys[at, :], query[at], (((0,), (0,)), ((), ())), preferred_element_type=F32
+            heads[at, :], query[at], (((0,), (0,)), ((), ())), preferred_element_type=F32
         )
         weights = jnp.exp(scores - jnp.max(scores, axis=0, keepdims=True))
         total = jnp.sum(weights, axis=0, keepdims=True)
-        weighted = jnp.dot(values[at, :], weights.astype(BF16), preferred_element_type=F32)
+        weighted = jnp.dot(
+            heads[channels + start : channels + start + HEAD_DIM, :],
+            weights.astype(BF16),
+            preferred_element_type=F32,
+        )
         out_ref[at, :] = (weighted / total).astype(BF16)
 
 
@@ -274,16 +278,16 @@
     pieces = [latent] + [swapped(latent, "patch", by) for by in range(1, rows)]
     others = [swapped(piece, "chan") for piece in pieces]
     proj_in_chan = swapped(proj_in_w, "chan")
+    _, timestep, *heads_w = barrier((pieces[-1], timestep, q_w, kv_w))
     embedded = embedding_of(timestep)[None]
-    (_, *heads_w), embedded = barrier(((pieces[-1], q_w, kv_w), embedded))
-    (bias,) = call(time_bias, [((OWN, 1), F32)], embedded, time_w1.T, time_proj, flops=10**8)
     heads_w = (*heads_w, *(swapped(weight, "sub") for weight in heads_w))
-    others, conv1_w, bias = barrier((others, arranged(conv1_w), bias))
+    others, conv1_w, embedded = barrier((others, arranged(conv1_w), embedded))
     pair = (2,) + chunk
     latent_rows, one, two = call(
         first_norm, [((rows, OWN, WIDTH), BF16), (pair, BF16), (pair, BF16)], *pieces, *others,
     )
     one, two = (one, swapped(one, "sub")), (two, swapped(two, "sub"))
+    (bias,) = call(time_bias, [((OWN, 1), F32)], embedded, time_w1.T, time_proj, flops=10**8)
 
     def halves(blocks, weight):
         return call(
@@ -299,13 +303,13 @@
         )[0]
         for part in range(2)
     )
-    _, heads_w, conv2_w, proj_in_chan = barrier((one, heads_w, conv2_w, proj_in_chan))
-    heads_w = call(stack_heads, [((2 * OWN, C), BF16)] * 3, *heads_w, flops=10**8)
-    proj_in = (
-        proj_in_w, proj_in_chan, swapped(proj_in_w, "sub"),
-        swapped(proj_in_chan, "sub"),
-    )
-    one, (heads_w, conv2_w, proj_in) = exchanged(one, heads_w, arranged(conv2_w), proj_in)
+    _, heads_w, conv2_w = barrier((one, heads_w, conv2_w))
+    heads_w = call(
+        stack_heads, [((2 * OWN, C), BF16), ((4 * OWN, C), BF16)], *heads_w,
+        flops=10**8,
+    )
+    proj_in_sub = swapped(proj_in_w, "sub")
+    one, (heads_w, conv2_w, proj_in_sub) = exchanged(one, heads_w, arranged(conv2_w), proj_in_sub)
     two, _ = exchanged(two)
     half = halves(one, conv2_w[0])
     (one, res_one), (two, res_two) = (
@@ -316,16 +320,16 @@
         )
         for part in range(2)
     )
-    _, proj_in, out_w = barrier((one, proj_in, out_w))
+    _, proj_in_chan, out_w = barrier((one, proj_in_chan, out_w))
+    proj_in = (proj_in_w, proj_in_chan, proj_in_sub, swapped(proj_in_chan, "sub"))
     one, (proj_in, out_sub) = exchanged(one, stacked(proj_in), swapped(out_w, "sub"))
     two, _ = exchanged(two)
-    _, out_chan = barrier((two, out_w))
-    out_chan = swapped(out_chan, "chan")
+    out_chan = swapped(out_w, "chan")
     share = WIDTH // 2
     attended, projected = call(
         attend, [((2 * OWN, share), BF16), ((C, WIDTH), BF16)],
         *one, *two, proj_in, *heads_w,
-        scratch=[((rows, C, WIDTH), BF16)] * 3 + [((2 * OWN, rows * WIDTH), BF16)] * 2,
+        scratch=[((rows, C, WIDTH), BF16)] * 3 + [((4 * OWN, rows * WIDTH), BF16)],
         flops=4 * 10**9, limit=32,
     )
     _, out_chan = barrier((attended, out_chan))

time: 66.9 us -> 67.8 us (1.013)
  transfers between devices with their start and end apart: 32 -> 32, of which waited for: 13 -> 12; matrix products, arithmetic and copies ran while one was open for 0% -> 0% of each run, Pallas kernels for 22% -> 23%
where the time goes in v1:
time: 67.8 us; the launch traced here: 67.7 us
  waiting for transfers between devices  24.2 us (36%)
  starting transfers between devices  22.9 us (34%)
  Pallas kernels  18 us (27%)
  local copies, waits for them, and re-layouts  1.55 us (2%)
  between operations  0.92 us (1%)
    ppermute x32, waiting for transfers between devices, swapped(): lax.ppermute(array, axis, [(i, i ^ by) for i in range(lax.axis_size(axis))])  24.2 us
    ppermute x32, starting transfers between devices, swapped(): lax.ppermute(array, axis, [(i, i ^ by) for i in range(lax.axis_size(axis))])  22.9 us
    pallas_call x15, Pallas kernels, call(): pl.pallas_call(kernel, out_shape=[jax.ShapeDtypeStruct(s, t) for s, t in...  18 us
    unnamed x20, local copies, waits for them, and re-layouts  1.55 us
  transfers between devices with their start and end apart: 32, of which 12 were waited for; matrix products, arithmetic and copies ran while one was open for 0% of the time, Pallas kernels for 23%

profile of v1, /device:TPU:0, one launch (start us, length us, event | category | flops | bytes accessed | tf_op | source)
XLA Modules:
  0.0 67.7 jit_solution(8407418225518786436)
XLA Ops:
  0.0 5.1 %collective-permute-start.2 = (bf16[160,256]{1,0:T(8,128)(2,1)}, bf16[160,256]{1,0:T(8,128)(2,1)S(1)}, u32[]{:S(2)}, u32[]{:S(2)}) collective-permute-start(bf16[160,256]{1,0:T(8,128)(2,1)} %refs_0_.1), channel_id=1, source_target_pairs={{0,12},{4,8},{8,4},{12,0},{1,13},{5,9},{9,5},{13,1},{2,14},{6,10},... | collective-permute-start | bytes 245768 | tf_op jit(solution)/shard_map/ppermute | solution.py:236
  5.6 1.7 %collective-permute-start.3 = (bf16[160,256]{1,0:T(8,128)(2,1)}, bf16[160,256]{1,0:T(8,128)(2,1)S(1)}, u32[]{:S(2)}, u32[]{:S(2)}) collective-permute-start(bf16[160,256]{1,0:T(8,128)(2,1)} %refs_0_.1), channel_id=1, source_target_pairs={{0,2},{2,0},{1,3},{3,1},{4,6},{6,4},{5,7},{7,5},{8,10},{10,8},{9,1... | collective-permute-start | bytes 245768 | tf_op jit(solution)/shard_map/ppermute | solution.py:236
  8.2 3.3 %collective-permute-done.refs_1_ = bf16[160,256]{1,0:T(8,128)(2,1)S(1)} collective-permute-done((bf16[160,256]{1,0:T(8,128)(2,1)}, bf16[160,256]{1,0:T(8,128)(2,1)S(1)}, u32[]{:S(2)}, u32[]{:S(2)}) %collective-permute-start) | collective-permute-done | bytes 81952 | tf_op jit(solution)/shard_map/ppermute | solution.py:236
  11.5 1.6 %collective-permute-start.4 = (bf16[160,256]{1,0:T(8,128)(2,1)S(1)}, bf16[160,256]{1,0:T(8,128)(2,1)S(1)}, u32[]{:S(2)}, u32[]{:S(2)}) collective-permute-start(bf16[160,256]{1,0:T(8,128)(2,1)S(1)} %collective-permute-done.refs_1_), channel_id=1, source_target_pairs={{0,2},{2,0},{1,3},{3,1},{4,6},{6,4},{5,7},{7,5},{8,10},{10,8},{9,1... | collective-permute-start | bytes 245768 | tf_op jit(solution)/shard_map/ppermute | solution.py:236
  13.6 1.6 %collective-permute-start.6 = (bf16[160,256]{1,0:T(8,128)(2,1)S(1)}, bf16[160,256]{1,0:T(8,128)(2,1)S(1)}, u32[]{:S(2)}, u32[]{:S(2)}) collective-permute-start(bf16[160,256]{1,0:T(8,128)(2,1)S(1)} %collective-permute-done.2.refs_3_), channel_id=1, source_target_pairs={{0,2},{2,0},{1,3},{3,1},{4,6},{6,4},{5,7},{7,5},{8,10},{10,8},{9,1... | collective-permute-start | bytes 245768 | tf_op jit(solution)/shard_map/ppermute | solution.py:236
  15.2 1.5 %copy-done.8 = bf16[9,160,640]{2,1,0:T(8,128)(2,1)S(1)} copy-done((bf16[9,160,640]{2,1,0:T(8,128)(2,1)S(1)}, bf16[9,160,640]{2,1,0:T(8,128)(2,1)}, u32[]{:S(2)}) %copy-start.8) | copy-done | bytes 1843224
  16.7 1.2 %shard_map.109 = (bf16[480,960]{1,0:T(8,128)(2,1)S(1)}, bf16[240,960]{1,0:T(8,128)(2,1)S(1)}, bf16[240,960]{1,0:T(8,128)(2,1)S(1)}) custom-call(bf16[9,160,640]{2,1,0:T(8,128)(2,1)S(1)} %copy-done.8), custom_call_target="tpu_custom_call" | custom-call | flops 1000000000 | bytes 1843200 | tf_op jit(solution)/shard_map/pallas_call | solution.py:33
  17.9 0.6 collective-permute-done.6.refs_7_
  18.6 0.9 %shard_map.110 = (bf16[4,160,256]{2,1,0:T(8,128)(2,1)S(1)}, bf16[2,4,80,256]{3,2,1,0:T(8,128)(2,1)S(1)}, bf16[2,4,80,256]{3,2,1,0:T(8,128)(2,1)S(1)}) custom-call(bf16[160,256]{1,0:T(8,128)(2,1)S(1)} %copy-done.7, bf16[160,256]{1,0:T(8,128)(2,1)S(1)} %collective-permute-done.refs_1_, bf16[160,256]{1,0:T(8,128)(2,1)S(1)} %collective-permute-done.1.refs_2_, ...), custom_call_target="tpu_custom_call" | custom-call | bytes 655360 | tf_op jit(solution)/shard_map/pallas_call | solution.py:33
  21.1 1.4 %shard_map.111 = (f32[4,80,256]{2,1,0:T(8,128)S(1)}, f32[4,80,256]{2,1,0:T(8,128)S(1)}) custom-call(bf16[2,4,80,256]{3,2,1,0:T(8,128)(2,1)S(1)} %get-tuple-element.74.refs_0_, bf16[2,4,80,256]{3,2,1,0:T(8,128)(2,1)S(1)} %collective-permute-done.8.refs_1_, bf16[480,960]{1,0:T(8,128)(2,1)S(1)} %get-tuple-element.75.refs_2_), custom_call_target="tpu_custom_call" | custom-call | flops 943718400 | bytes 1576960 | tf_op jit(solution)/shard_map/pallas_call | solution.py:33
  22.5 1.1 %shard_map.114.refs_0_ = bf16[4,80,256]{2,1,0:T(8,128)(2,1)S(1)} custom-call(bf16[2,4,80,256]{3,2,1,0:T(8,128)(2,1)S(1)} %get-tuple-element.72.refs_0_, bf16[2,4,80,256]{3,2,1,0:T(8,128)(2,1)S(1)} %collective-permute-done.7.refs_1_, bf16[240,960]{1,0:T(8,128)(2,1)S(1)} %get-tuple-element.80.refs_2_, f32[4,80,256]{2,1,0:T(8,128)S(1)} %get-tuple-element.81.refs_3_, ...), custom_call_target="tpu_custom_call" | custom-call | flops 471859200 | bytes 1444480 | tf_op jit(solution)/shard_map/pallas_call | solution.py:33
  23.7 1.2 %collective-permute-start.12 = (bf16[4,80,256]{2,1,0:T(8,128)(2,1)S(1)}, bf16[4,80,256]{2,1,0:T(8,128)(2,1)S(1)}, u32[]{:S(2)}, u32[]{:S(2)}) collective-permute-start(bf16[4,80,256]{2,1,0:T(8,128)(2,1)S(1)} %shard_map.114.refs_0_), channel_id=1, source_target_pairs={{0,2},{2,0},{1,3},{3,1},{4,6},{6,4},{5,7},{7,5},{8,10},{10,8},{9,1... | collective-permute-start | bytes 491528 | tf_op jit(solution)/shard_map/ppermute | solution.py:236
  24.9 1.1 %shard_map.113.refs_0_ = bf16[4,80,256]{2,1,0:T(8,128)(2,1)S(1)} custom-call(bf16[2,4,80,256]{3,2,1,0:T(8,128)(2,1)S(1)} %get-tuple-element.72.refs_0_, bf16[2,4,80,256]{3,2,1,0:T(8,128)(2,1)S(1)} %collective-permute-done.7.refs_1_, bf16[240,960]{1,0:T(8,128)(2,1)S(1)} %get-tuple-element.73.refs_2_, f32[4,80,256]{2,1,0:T(8,128)S(1)} %get-tuple-element.76.refs_3_, ...), custom_call_target="tpu_custom_call" | custom-call | flops 471859200 | bytes 1444480 | tf_op jit(solution)/shard_map/pallas_call | solution.py:33
  26.0 0.9 %collective-permute-start.9 = (bf16[4,80,256]{2,1,0:T(8,128)(2,1)S(1)}, bf16[4,80,256]{2,1,0:T(8,128)(2,1)S(1)}, u32[]{:S(2)}, u32[]{:S(2)}) collective-permute-start(bf16[4,80,256]{2,1,0:T(8,128)(2,1)S(1)} %shard_map.113.refs_0_), channel_id=1, source_target_pairs={{0,2},{2,0},{1,3},{3,1},{4,6},{6,4},{5,7},{7,5},{8,10},{10,8},{9,1... | collective-permute-start | bytes 491528 | tf_op jit(solution)/shard_map/ppermute | solution.py:236
  27.0 1.2 %shard_map.116 = (bf16[480,960]{1,0:T(8,128)(2,1)S(1)}, bf16[240,960]{1,0:T(8,128)(2,1)S(1)}, bf16[240,960]{1,0:T(8,128)(2,1)S(1)}) custom-call(bf16[9,160,640]{2,1,0:T(8,128)(2,1)S(1)} %copy-done.9), custom_call_target="tpu_custom_call" | custom-call | flops 1000000000 | bytes 1843200 | tf_op jit(solution)/shard_map/pallas_call | solution.py:33
  28.3 2.5 %collective-permute-done.12.refs_1_ = bf16[4,80,256]{2,1,0:T(8,128)(2,1)S(1)} collective-permute-done((bf16[4,80,256]{2,1,0:T(8,128)(2,1)S(1)}, bf16[4,80,256]{2,1,0:T(8,128)(2,1)S(1)}, u32[]{:S(2)}, u32[]{:S(2)}) %collective-permute-start.12) | collective-permute-done | bytes 163872 | tf_op jit(solution)/shard_map/ppermute | solution.py:236
  31.3 2.4 %collective-permute-done.9.refs_1_ = bf16[4,80,256]{2,1,0:T(8,128)(2,1)S(1)} collective-permute-done((bf16[4,80,256]{2,1,0:T(8,128)(2,1)S(1)}, bf16[4,80,256]{2,1,0:T(8,128)(2,1)S(1)}, u32[]{:S(2)}, u32[]{:S(2)}) %collective-permute-start.9) | collective-permute-done | bytes 163872 | tf_op jit(solution)/shard_map/ppermute | solution.py:236
  34.2 1.2 %collective-permute-start.19 = (bf16[160,640]{1,0:T(8,128)(2,1)S(1)}, bf16[160,640]{1,0:T(8,128)(2,1)S(1)}, u32[]{:S(2)}, u32[]{:S(2)}) collective-permute-start(bf16[160,640]{1,0:T(8,128)(2,1)S(1)} %copy-done.4), channel_id=1, source_target_pairs={{0,2},{2,0},{1,3},{3,1},{4,6},{6,4},{5,7},{7,5},{8,10},{10,8},{9,1... | collective-permute-start | bytes 614408 | tf_op jit(solution)/shard_map/ppermute | solution.py:236
  35.4 1.4 %shard_map.117 = (f32[4,80,256]{2,1,0:T(8,128)S(1)}, f32[4,80,256]{2,1,0:T(8,128)S(1)}) custom-call(bf16[4,80,256]{2,1,0:T(8,128)(2,1)S(1)} %shard_map.114.refs_0_, bf16[4,80,256]{2,1,0:T(8,128)(2,1)S(1)} %collective-permute-done.12.refs_1_, bf16[4,80,256]{2,1,0:T(8,128)(2,1)S(1)} %collective-permute-done.16.refs_2_, ...), custom_call_target="tpu_custom_call" | custom-call | flops 943718400 | bytes 1576960 | tf_op jit(solution)/shard_map/pallas_call | solution.py:33
  36.8 1.1 %shard_map.118 = (bf16[4,80,256]{2,1,0:T(8,128)(2,1)S(1)}, bf16[80,256]{1,0:T(8,128)(2,1)S(1)}) custom-call(bf16[4,80,256]{2,1,0:T(8,128)(2,1)S(1)} %shard_map.113.refs_0_, bf16[4,80,256]{2,1,0:T(8,128)(2,1)S(1)} %collective-permute-done.9.refs_1_, bf16[4,80,256]{2,1,0:T(8,128)(2,1)S(1)} %collective-permute-done.10.refs_2_, ...), custom_call_target="tpu_custom_call" | custom-call | flops 471859200 | bytes 1771520 | tf_op jit(solution)/shard_map/pallas_call | solution.py:33
  37.9 3.3 %collective-permute-done.19.chan = bf16[160,640]{1,0:T(8,128)(2,1)S(1)} collective-permute-done((bf16[160,640]{1,0:T(8,128)(2,1)S(1)}, bf16[160,640]{1,0:T(8,128)(2,1)S(1)}, u32[]{:S(2)}, u32[]{:S(2)}) %collective-permute-start.19) | collective-permute-done | bytes 204832 | tf_op jit(solution)/shard_map/ppermute | solution.py:236
  41.7 1.1 %shard_map.120 = (bf16[4,80,256]{2,1,0:T(8,128)(2,1)S(1)}, bf16[80,256]{1,0:T(8,128)(2,1)S(1)}) custom-call(bf16[4,80,256]{2,1,0:T(8,128)(2,1)S(1)} %shard_map.113.refs_0_, bf16[4,80,256]{2,1,0:T(8,128)(2,1)S(1)} %collective-permute-done.9.refs_1_, bf16[4,80,256]{2,1,0:T(8,128)(2,1)S(1)} %collective-permute-done.10.refs_2_, ...), custom_call_target="tpu_custom_call" | custom-call | flops 471859200 | bytes 1771520 | tf_op jit(solution)/shard_map/pallas_call | solution.py:33
  42.8 1.2 %collective-permute-start.24 = (bf16[4,80,256]{2,1,0:T(8,128)(2,1)S(1)}, bf16[4,80,256]{2,1,0:T(8,128)(2,1)S(1)}, u32[]{:S(2)}, u32[]{:S(2)}) collective-permute-start(bf16[4,80,256]{2,1,0:T(8,128)(2,1)S(1)} %get-tuple-element.109.refs_4_), channel_id=1, source_target_pairs={{0,2},{2,0},{1,3},{3,1},{4,6},{6,4},{5,7},{7,5},{8,10},{10,8},{9,1... | collective-permute-start | bytes 491528 | tf_op jit(solution)/shard_map/ppermute | solution.py:236
  44.1 0.9 %collective-permute-start.18 = (bf16[4,80,256]{2,1,0:T(8,128)(2,1)S(1)}, bf16[4,80,256]{2,1,0:T(8,128)(2,1)S(1)}, u32[]{:S(2)}, u32[]{:S(2)}) collective-permute-start(bf16[4,80,256]{2,1,0:T(8,128)(2,1)S(1)} %get-tuple-element.104.refs_0_), channel_id=1, source_target_pairs={{0,2},{2,0},{1,3},{3,1},{4,6},{6,4},{5,7},{7,5},{8,10},{10,8},{9,1... | collective-permute-start | bytes 491528 | tf_op jit(solution)/shard_map/ppermute | solution.py:236
  44.9 5.0 %collective-permute-done.24.refs_5_ = bf16[4,80,256]{2,1,0:T(8,128)(2,1)S(1)} collective-permute-done((bf16[4,80,256]{2,1,0:T(8,128)(2,1)S(1)}, bf16[4,80,256]{2,1,0:T(8,128)(2,1)S(1)}, u32[]{:S(2)}, u32[]{:S(2)}) %collective-permute-start.24) | collective-permute-done | bytes 163872 | tf_op jit(solution)/shard_map/ppermute | solution.py:236
  50.6 1.9 %collective-permute-done.18.refs_1_ = bf16[4,80,256]{2,1,0:T(8,128)(2,1)S(1)} collective-permute-done((bf16[4,80,256]{2,1,0:T(8,128)(2,1)S(1)}, bf16[4,80,256]{2,1,0:T(8,128)(2,1)S(1)}, u32[]{:S(2)}, u32[]{:S(2)}) %collective-permute-start.18) | collective-permute-done | bytes 163872 | tf_op jit(solution)/shard_map/ppermute | solution.py:236
  53.0 1.2 %collective-permute-start.28 = (bf16[160,640]{1,0:T(8,128)(2,1)S(1)}, bf16[160,640]{1,0:T(8,128)(2,1)S(1)}, u32[]{:S(2)}, u32[]{:S(2)}) collective-permute-start(bf16[160,640]{1,0:T(8,128)(2,1)S(1)} %copy-done.5), channel_id=1, source_target_pairs={{0,2},{2,0},{1,3},{3,1},{4,6},{6,4},{5,7},{7,5},{8,10},{10,8},{9,1... | collective-permute-start | bytes 614408 | tf_op jit(solution)/shard_map/ppermute | solution.py:236
  54.2 5.5 %shard_map.121 = (bf16[320,128]{1,0:T(8,128)(2,1)S(1)}, bf16[640,256]{1,0:T(8,128)(2,1)S(1)}) custom-call(bf16[4,80,256]{2,1,0:T(8,128)(2,1)S(1)} %get-tuple-element.104.refs_0_, bf16[4,80,256]{2,1,0:T(8,128)(2,1)S(1)} %collective-permute-done.18.refs_1_, bf16[4,80,256]{2,1,0:T(8,128)(2,1)S(1)} %collective-permute-done.22.refs_2_, ...), custom_call_target="tpu_custom_call" | custom-call | flops 4000000000 | bytes 3358720 | tf_op jit(solution)/shard_map/pallas_call | solution.py:33
  60.0 1.2 %collective-permute-start.27 = (bf16[320,128]{1,0:T(8,128)(2,1)S(1)}, bf16[320,128]{1,0:T(8,128)(2,1)S(1)}, u32[]{:S(2)}, u32[]{:S(2)}) collective-permute-start(bf16[320,128]{1,0:T(8,128)(2,1)S(1)} %get-tuple-element.117.own), channel_id=1, source_target_pairs={{0,2},{2,0},{1,3},{3,1},{4,6},{6,4},{5,7},{7,5},{8,10},{10,8},{9,1... | collective-permute-start | bytes 245768 | tf_op jit(solution)/shard_map/ppermute | solution.py:236
  61.6 3.3 %collective-permute-done.27.chan = bf16[320,128]{1,0:T(8,128)(2,1)S(1)} collective-permute-done((bf16[320,128]{1,0:T(8,128)(2,1)S(1)}, bf16[320,128]{1,0:T(8,128)(2,1)S(1)}, u32[]{:S(2)}, u32[]{:S(2)}) %collective-permute-start.27) | collective-permute-done | bytes 81952 | tf_op jit(solution)/shard_map/ppermute | solution.py:236
  65.4 0.8 %collective-permute-done.30.sub = bf16[320,128]{1,0:T(8,128)(2,1)S(1)} collective-permute-done((bf16[320,128]{1,0:T(8,128)(2,1)S(1)}, bf16[320,128]{1,0:T(8,128)(2,1)S(1)}, u32[]{:S(2)}, u32[]{:S(2)}) %collective-permute-start.30) | collective-permute-done | bytes 81952 | tf_op jit(solution)/shard_map/ppermute | solution.py:236
  66.3 1.4 %shard_map.123 = bf16[160,256]{1,0:T(8,128)(2,1)} custom-call(bf16[320,128]{1,0:T(8,128)(2,1)S(1)} %get-tuple-element.117.own, bf16[320,128]{1,0:T(8,128)(2,1)S(1)} %collective-permute-done.27.chan, bf16[320,128]{1,0:T(8,128)(2,1)S(1)} %collective-permute-done.30.sub, bf16[320,128]{1,0:T(8,128)(2,1)S(1)} %collective-permute-done.31.both, ...), custom_call_target="tpu_custom_call" | custom-call | bytes 1761280 | tf_op jit(solution)/shard_map/pallas_call | solution.py:33
  (71 shorter events, 7.0 us)
Async XLA Ops:
  0.0 13.6 %collective-permute-start.2 = (bf16[160,256]{1,0:T(8,128)(2,1)}, bf16[160,256]{1,0:T(8,128)(2,1)S(1)}, u32[]{:S(2)}, u32[]{:S(2)}) collective-permute-start(bf16[160,256]{1,0:T(8,128)(2,1)} %refs_0_.1), channel_id=1, source_target_pairs={{0,12},{4,8},{8,4},{12,0},{1,13},{5,9},{9,5},{13,1},{2,14},{6,10},... | collective-permute-start | bytes 245768 | tf_op jit(solution)/shard_map/ppermute | solution.py:236
  5.1 6.4 %collective-permute-start = (bf16[160,256]{1,0:T(8,128)(2,1)}, bf16[160,256]{1,0:T(8,128)(2,1)S(1)}, u32[]{:S(2)}, u32[]{:S(2)}) collective-permute-start(bf16[160,256]{1,0:T(8,128)(2,1)} %refs_0_.1), channel_id=1, source_target_pairs={{0,4},{4,0},{8,12},{12,8},{1,5},{5,1},{9,13},{13,9},{2,6},{6,2},{1... | collective-permute-start | bytes 245768 | tf_op jit(solution)/shard_map/ppermute | solution.py:236
  5.1 8.0 %collective-permute-start.1 = (bf16[160,256]{1,0:T(8,128)(2,1)}, bf16[160,256]{1,0:T(8,128)(2,1)S(1)}, u32[]{:S(2)}, u32[]{:S(2)}) collective-permute-start(bf16[160,256]{1,0:T(8,128)(2,1)} %refs_0_.1), channel_id=1, source_target_pairs={{0,8},{4,12},{8,0},{12,4},{1,9},{5,13},{9,1},{13,5},{2,10},{6,14},... | collective-permute-start | bytes 245768 | tf_op jit(solution)/shard_map/ppermute | solution.py:236
  5.6 12.3 %collective-permute-start.3 = (bf16[160,256]{1,0:T(8,128)(2,1)}, bf16[160,256]{1,0:T(8,128)(2,1)S(1)}, u32[]{:S(2)}, u32[]{:S(2)}) collective-permute-start(bf16[160,256]{1,0:T(8,128)(2,1)} %refs_0_.1), channel_id=1, source_target_pairs={{0,2},{2,0},{1,3},{3,1},{4,6},{6,4},{5,7},{7,5},{8,10},{10,8},{9,1... | collective-permute-start | bytes 245768 | tf_op jit(solution)/shard_map/ppermute | solution.py:236
  11.5 6.4 %collective-permute-start.4 = (bf16[160,256]{1,0:T(8,128)(2,1)S(1)}, bf16[160,256]{1,0:T(8,128)(2,1)S(1)}, u32[]{:S(2)}, u32[]{:S(2)}) collective-permute-start(bf16[160,256]{1,0:T(8,128)(2,1)S(1)} %collective-permute-done.refs_1_), channel_id=1, source_target_pairs={{0,2},{2,0},{1,3},{3,1},{4,6},{6,4},{5,7},{7,5},{8,10},{10,8},{9,1... | collective-permute-start | bytes 245768 | tf_op jit(solution)/shard_map/ppermute | solution.py:236
  13.1 4.8 %collective-permute-start.5 = (bf16[160,256]{1,0:T(8,128)(2,1)S(1)}, bf16[160,256]{1,0:T(8,128)(2,1)S(1)}, u32[]{:S(2)}, u32[]{:S(2)}) collective-permute-start(bf16[160,256]{1,0:T(8,128)(2,1)S(1)} %collective-permute-done.1.refs_2_), channel_id=1, source_target_pairs={{0,2},{2,0},{1,3},{3,1},{4,6},{6,4},{5,7},{7,5},{8,10},{10,8},{9,1... | collective-permute-start | bytes 245768 | tf_op jit(solution)/shard_map/ppermute | solution.py:236
  13.6 5.0 %collective-permute-start.6 = (bf16[160,256]{1,0:T(8,128)(2,1)S(1)}, bf16[160,256]{1,0:T(8,128)(2,1)S(1)}, u32[]{:S(2)}, u32[]{:S(2)}) collective-permute-start(bf16[160,256]{1,0:T(8,128)(2,1)S(1)} %collective-permute-done.2.refs_3_), channel_id=1, source_target_pairs={{0,2},{2,0},{1,3},{3,1},{4,6},{6,4},{5,7},{7,5},{8,10},{10,8},{9,1... | collective-permute-start | bytes 245768 | tf_op jit(solution)/shard_map/ppermute | solution.py:236
  19.4 1.7 %collective-permute-start.8 = (bf16[2,4,80,256]{3,2,1,0:T(8,128)(2,1)S(1)}, bf16[2,4,80,256]{3,2,1,0:T(8,128)(2,1)S(1)}, u32[]{:S(2)}, u32[]{:S(2)}) collective-permute-start(bf16[2,4,80,256]{3,2,1,0:T(8,128)(2,1)S(1)} %get-tuple-element.74.refs_0_), channel_id=1, source_target_pairs={{0,1},{1,0},{2,3},{3,2},{4,5},{5,4},{6,7},{7,6},{8,9},{9,8},{10,11... | collective-permute-start | bytes 983048 | tf_op jit(solution)/shard_map/ppermute | solution.py:236
  19.5 3.0 %collective-permute-start.7 = (bf16[2,4,80,256]{3,2,1,0:T(8,128)(2,1)S(1)}, bf16[2,4,80,256]{3,2,1,0:T(8,128)(2,1)S(1)}, u32[]{:S(2)}, u32[]{:S(2)}) collective-permute-start(bf16[2,4,80,256]{3,2,1,0:T(8,128)(2,1)S(1)} %get-tuple-element.72.refs_0_), channel_id=1, source_target_pairs={{0,1},{1,0},{2,3},{3,2},{4,5},{5,4},{6,7},{7,6},{8,9},{9,8},{10,11... | collective-permute-start | bytes 983048 | tf_op jit(solution)/shard_map/ppermute | solution.py:236
  20.0 6.9 %collective-permute-start.14 = (bf16[2,160,640]{2,1,0:T(8,128)(2,1)S(1)}, bf16[2,160,640]{2,1,0:T(8,128)(2,1)S(1)}, u32[]{:S(2)}, u32[]{:S(2)}) collective-permute-start(bf16[2,160,640]{2,1,0:T(8,128)(2,1)S(1)} %copy-done.2), channel_id=1, source_target_pairs={{0,1},{1,0},{2,3},{3,2},{4,5},{5,4},{6,7},{7,6},{8,9},{9,8},{10,11... | collective-permute-start | bytes 1228808 | tf_op jit(solution)/shard_map/ppermute | solution.py:236
  20.1 6.8 %collective-permute-start.13 = (bf16[160,640]{1,0:T(8,128)(2,1)S(1)}, bf16[160,640]{1,0:T(8,128)(2,1)S(1)}, u32[]{:S(2)}, u32[]{:S(2)}) collective-permute-start(bf16[160,640]{1,0:T(8,128)(2,1)S(1)} %copy-done.3), channel_id=1, source_target_pairs={{0,1},{1,0},{2,3},{3,2},{4,5},{5,4},{6,7},{7,6},{8,9},{9,8},{10,11... | collective-permute-start | bytes 614408 | tf_op jit(solution)/shard_map/ppermute | solution.py:236
  20.5 7.7 %collective-permute-start.15 = (bf16[160,640]{1,0:T(8,128)(2,1)S(1)}, bf16[160,640]{1,0:T(8,128)(2,1)S(1)}, u32[]{:S(2)}, u32[]{:S(2)}) collective-permute-start(bf16[160,640]{1,0:T(8,128)(2,1)S(1)} %copy-done.4), channel_id=1, source_target_pairs={{0,1},{1,0},{2,3},{3,2},{4,5},{5,4},{6,7},{7,6},{8,9},{9,8},{10,11... | collective-permute-start | bytes 614408 | tf_op jit(solution)/shard_map/ppermute | solution.py:236
  23.7 7.1 %collective-permute-start.12 = (bf16[4,80,256]{2,1,0:T(8,128)(2,1)S(1)}, bf16[4,80,256]{2,1,0:T(8,128)(2,1)S(1)}, u32[]{:S(2)}, u32[]{:S(2)}) collective-permute-start(bf16[4,80,256]{2,1,0:T(8,128)(2,1)S(1)} %shard_map.114.refs_0_), channel_id=1, source_target_pairs={{0,2},{2,0},{1,3},{3,1},{4,6},{6,4},{5,7},{7,5},{8,10},{10,8},{9,1... | collective-permute-start | bytes 491528 | tf_op jit(solution)/shard_map/ppermute | solution.py:236
  26.0 7.8 %collective-permute-start.9 = (bf16[4,80,256]{2,1,0:T(8,128)(2,1)S(1)}, bf16[4,80,256]{2,1,0:T(8,128)(2,1)S(1)}, u32[]{:S(2)}, u32[]{:S(2)}) collective-permute-start(bf16[4,80,256]{2,1,0:T(8,128)(2,1)S(1)} %shard_map.113.refs_0_), channel_id=1, source_target_pairs={{0,2},{2,0},{1,3},{3,1},{4,6},{6,4},{5,7},{7,5},{8,10},{10,8},{9,1... | collective-permute-start | bytes 491528 | tf_op jit(solution)/shard_map/ppermute | solution.py:236
  30.8 4.6 %collective-permute-start.16 = (bf16[4,80,256]{2,1,0:T(8,128)(2,1)S(1)}, bf16[4,80,256]{2,1,0:T(8,128)(2,1)S(1)}, u32[]{:S(2)}, u32[]{:S(2)}) collective-permute-start(bf16[4,80,256]{2,1,0:T(8,128)(2,1)S(1)} %shard_map.114.refs_0_), channel_id=1, source_target_pairs={{0,1},{1,0},{2,3},{3,2},{4,5},{5,4},{6,7},{7,6},{8,9},{9,8},{10,11... | collective-permute-start | bytes 491528 | tf_op jit(solution)/shard_map/ppermute | solution.py:236
  30.8 4.6 %collective-permute-start.17 = (bf16[4,80,256]{2,1,0:T(8,128)(2,1)S(1)}, bf16[4,80,256]{2,1,0:T(8,128)(2,1)S(1)}, u32[]{:S(2)}, u32[]{:S(2)}) collective-permute-start(bf16[4,80,256]{2,1,0:T(8,128)(2,1)S(1)} %collective-permute-done.12.refs_1_), channel_id=1, source_target_pairs={{0,1},{1,0},{2,3},{3,2},{4,5},{5,4},{6,7},{7,6},{8,9},{9,8},{10,11... | collective-permute-start | bytes 491528 | tf_op jit(solution)/shard_map/ppermute | solution.py:236
  33.7 3.0 %collective-permute-start.10 = (bf16[4,80,256]{2,1,0:T(8,128)(2,1)S(1)}, bf16[4,80,256]{2,1,0:T(8,128)(2,1)S(1)}, u32[]{:S(2)}, u32[]{:S(2)}) collective-permute-start(bf16[4,80,256]{2,1,0:T(8,128)(2,1)S(1)} %shard_map.113.refs_0_), channel_id=1, source_target_pairs={{0,1},{1,0},{2,3},{3,2},{4,5},{5,4},{6,7},{7,6},{8,9},{9,8},{10,11... | collective-permute-start | bytes 491528 | tf_op jit(solution)/shard_map/ppermute | solution.py:236
  33.7 3.1 %collective-permute-start.11 = (bf16[4,80,256]{2,1,0:T(8,128)(2,1)S(1)}, bf16[4,80,256]{2,1,0:T(8,128)(2,1)S(1)}, u32[]{:S(2)}, u32[]{:S(2)}) collective-permute-start(bf16[4,80,256]{2,1,0:T(8,128)(2,1)S(1)} %collective-permute-done.9.refs_1_), channel_id=1, source_target_pairs={{0,1},{1,0},{2,3},{3,2},{4,5},{5,4},{6,7},{7,6},{8,9},{9,8},{10,11... | collective-permute-start | bytes 491528 | tf_op jit(solution)/shard_map/ppermute | solution.py:236
  34.2 7.0 %collective-permute-start.19 = (bf16[160,640]{1,0:T(8,128)(2,1)S(1)}, bf16[160,640]{1,0:T(8,128)(2,1)S(1)}, u32[]{:S(2)}, u32[]{:S(2)}) collective-permute-start(bf16[160,640]{1,0:T(8,128)(2,1)S(1)} %copy-done.4), channel_id=1, source_target_pairs={{0,2},{2,0},{1,3},{3,1},{4,6},{6,4},{5,7},{7,5},{8,10},{10,8},{9,1... | collective-permute-start | bytes 614408 | tf_op jit(solution)/shard_map/ppermute | solution.py:236
  41.2 9.3 %collective-permute-start.20 = (bf16[160,640]{1,0:T(8,128)(2,1)S(1)}, bf16[160,640]{1,0:T(8,128)(2,1)S(1)}, u32[]{:S(2)}, u32[]{:S(2)}) collective-permute-start(bf16[160,640]{1,0:T(8,128)(2,1)S(1)} %collective-permute-done.19.chan), channel_id=1, source_target_pairs={{0,1},{1,0},{2,3},{3,2},{4,5},{5,4},{6,7},{7,6},{8,9},{9,8},{10,11... | collective-permute-start | bytes 614408 | tf_op jit(solution)/shard_map/ppermute | solution.py:236
  41.2 11.3 %collective-permute-start.21 = (bf16[160,640]{1,0:T(8,128)(2,1)S(1)}, bf16[160,640]{1,0:T(8,128)(2,1)S(1)}, u32[]{:S(2)}, u32[]{:S(2)}) collective-permute-start(bf16[160,640]{1,0:T(8,128)(2,1)S(1)} %copy-done.5), channel_id=1, source_target_pairs={{0,1},{1,0},{2,3},{3,2},{4,5},{5,4},{6,7},{7,6},{8,9},{9,8},{10,11... | collective-permute-start | bytes 614408 | tf_op jit(solution)/shard_map/ppermute | solution.py:236
  42.8 7.1 %collective-permute-start.24 = (bf16[4,80,256]{2,1,0:T(8,128)(2,1)S(1)}, bf16[4,80,256]{2,1,0:T(8,128)(2,1)S(1)}, u32[]{:S(2)}, u32[]{:S(2)}) collective-permute-start(bf16[4,80,256]{2,1,0:T(8,128)(2,1)S(1)} %get-tuple-element.109.refs_4_), channel_id=1, source_target_pairs={{0,2},{2,0},{1,3},{3,1},{4,6},{6,4},{5,7},{7,5},{8,10},{10,8},{9,1... | collective-permute-start | bytes 491528 | tf_op jit(solution)/shard_map/ppermute | solution.py:236
  44.1 8.5 %collective-permute-start.18 = (bf16[4,80,256]{2,1,0:T(8,128)(2,1)S(1)}, bf16[4,80,256]{2,1,0:T(8,128)(2,1)S(1)}, u32[]{:S(2)}, u32[]{:S(2)}) collective-permute-start(bf16[4,80,256]{2,1,0:T(8,128)(2,1)S(1)} %get-tuple-element.104.refs_0_), channel_id=1, source_target_pairs={{0,2},{2,0},{1,3},{3,1},{4,6},{6,4},{5,7},{7,5},{8,10},{10,8},{9,1... | collective-permute-start | bytes 491528 | tf_op jit(solution)/shard_map/ppermute | solution.py:236
  50.0 4.2 %collective-permute-start.25 = (bf16[4,80,256]{2,1,0:T(8,128)(2,1)S(1)}, bf16[4,80,256]{2,1,0:T(8,128)(2,1)S(1)}, u32[]{:S(2)}, u32[]{:S(2)}) collective-permute-start(bf16[4,80,256]{2,1,0:T(8,128)(2,1)S(1)} %get-tuple-element.109.refs_4_), channel_id=1, source_target_pairs={{0,1},{1,0},{2,3},{3,2},{4,5},{5,4},{6,7},{7,6},{8,9},{9,8},{10,11... | collective-permute-start | bytes 491528 | tf_op jit(solution)/shard_map/ppermute | solution.py:236
  50.0 4.2 %collective-permute-start.26 = (bf16[4,80,256]{2,1,0:T(8,128)(2,1)S(1)}, bf16[4,80,256]{2,1,0:T(8,128)(2,1)S(1)}, u32[]{:S(2)}, u32[]{:S(2)}) collective-permute-start(bf16[4,80,256]{2,1,0:T(8,128)(2,1)S(1)} %collective-permute-done.24.refs_5_), channel_id=1, source_target_pairs={{0,1},{1,0},{2,3},{3,2},{4,5},{5,4},{6,7},{7,6},{8,9},{9,8},{10,11... | collective-permute-start | bytes 491528 | tf_op jit(solution)/shard_map/ppermute | solution.py:236
  52.5 1.7 %collective-permute-start.22 = (bf16[4,80,256]{2,1,0:T(8,128)(2,1)S(1)}, bf16[4,80,256]{2,1,0:T(8,128)(2,1)S(1)}, u32[]{:S(2)}, u32[]{:S(2)}) collective-permute-start(bf16[4,80,256]{2,1,0:T(8,128)(2,1)S(1)} %get-tuple-element.104.refs_0_), channel_id=1, source_target_pairs={{0,1},{1,0},{2,3},{3,2},{4,5},{5,4},{6,7},{7,6},{8,9},{9,8},{10,11... | collective-permute-start | bytes 491528 | tf_op jit(solution)/shard_map/ppermute | solution.py:236
  52.5 1.7 %collective-permute-start.23 = (bf16[4,80,256]{2,1,0:T(8,128)(2,1)S(1)}, bf16[4,80,256]{2,1,0:T(8,128)(2,1)S(1)}, u32[]{:S(2)}, u32[]{:S(2)}) collective-permute-start(bf16[4,80,256]{2,1,0:T(8,128)(2,1)S(1)} %collective-permute-done.18.refs_1_), channel_id=1, source_target_pairs={{0,1},{1,0},{2,3},{3,2},{4,5},{5,4},{6,7},{7,6},{8,9},{9,8},{10,11... | collective-permute-start | bytes 491528 | tf_op jit(solution)/shard_map/ppermute | solution.py:236
  53.0 7.0 %collective-permute-start.28 = (bf16[160,640]{1,0:T(8,128)(2,1)S(1)}, bf16[160,640]{1,0:T(8,128)(2,1)S(1)}, u32[]{:S(2)}, u32[]{:S(2)}) collective-permute-start(bf16[160,640]{1,0:T(8,128)(2,1)S(1)} %copy-done.5), channel_id=1, source_target_pairs={{0,2},{2,0},{1,3},{3,1},{4,6},{6,4},{5,7},{7,5},{8,10},{10,8},{9,1... | collective-permute-start | bytes 614408 | tf_op jit(solution)/shard_map/ppermute | solution.py:236
  60.0 1.5 %collective-permute-start.29 = (bf16[160,640]{1,0:T(8,128)(2,1)S(1)}, bf16[160,640]{1,0:T(8,128)(2,1)S(1)}, u32[]{:S(2)}, u32[]{:S(2)}) collective-permute-start(bf16[160,640]{1,0:T(8,128)(2,1)S(1)} %collective-permute-done.28.chan), channel_id=1, source_target_pairs={{0,1},{1,0},{2,3},{3,2},{4,5},{5,4},{6,7},{7,6},{8,9},{9,8},{10,11... | collective-permute-start | bytes 614408 | tf_op jit(solution)/shard_map/ppermute | solution.py:236
  60.0 4.9 %collective-permute-start.27 = (bf16[320,128]{1,0:T(8,128)(2,1)S(1)}, bf16[320,128]{1,0:T(8,128)(2,1)S(1)}, u32[]{:S(2)}, u32[]{:S(2)}) collective-permute-start(bf16[320,128]{1,0:T(8,128)(2,1)S(1)} %get-tuple-element.117.own), channel_id=1, source_target_pairs={{0,2},{2,0},{1,3},{3,1},{4,6},{6,4},{5,7},{7,5},{8,10},{10,8},{9,1... | collective-permute-start | bytes 245768 | tf_op jit(solution)/shard_map/ppermute | solution.py:236
  64.9 1.3 %collective-permute-start.30 = (bf16[320,128]{1,0:T(8,128)(2,1)S(1)}, bf16[320,128]{1,0:T(8,128)(2,1)S(1)}, u32[]{:S(2)}, u32[]{:S(2)}) collective-permute-start(bf16[320,128]{1,0:T(8,128)(2,1)S(1)} %get-tuple-element.117.own), channel_id=1, source_target_pairs={{0,1},{1,0},{2,3},{3,2},{4,5},{5,4},{6,7},{7,6},{8,9},{9,8},{10,11... | collective-permute-start | bytes 245768 | tf_op jit(solution)/shard_map/ppermute | solution.py:236
  64.9 1.4 %collective-permute-start.31 = (bf16[320,128]{1,0:T(8,128)(2,1)S(1)}, bf16[320,128]{1,0:T(8,128)(2,1)S(1)}, u32[]{:S(2)}, u32[]{:S(2)}) collective-permute-start(bf16[320,128]{1,0:T(8,128)(2,1)S(1)} %collective-permute-done.27.chan), channel_id=1, source_target_pairs={{0,1},{1,0},{2,3},{3,2},{4,5},{5,4},{6,7},{7,6},{8,9},{9,8},{10,11... | collective-permute-start | bytes 245768 | tf_op jit(solution)/shard_map/ppermute | solution.py:236
  (10 other events, 102.4 us)

commit v2 on v1

--- a/solution.py
+++ b/solution.py
@@ -1,3 +1,4 @@
+import functools
 import math
 
 import jax
@@ -178,58 +179,89 @@
         kv_ref[pl.ds(at + 2 * OWN, OWN), :] = kv_part[1]
 
 
+def over_rows(values, combine):
+    return combine(
+        combine(values.reshape(-1, 8, values.shape[1]), axis=0), axis=0, keepdims=True
+    )
+
+
 def attend(*refs):
     blocks, refs = refs[:8], refs[8:]
-    proj_w, q_w, kv_w, out_ref, proj_ref, normed, projected, layered, heads = refs
+    proj_w, q_w, kv_w, out_ref, proj_ref, normed, projected, layered, heads, queries, scores, probs = refs
     rows = normed.shape[0]
     for half in range(2):
         for flip, block in zip(FLIPS, blocks[half * 4 : half * 4 + 4]):
             at = pl.multiple_of((own_place() ^ flip) * OWN + half * CHUNK, 16)
             normed[:, pl.ds(at, CHUNK), :] = block[...]
+    halves = [slice(0, C // 2), slice(C // 2, C)]
     for row in range(rows):
-        value = jnp.dot(proj_w[...], normed[row], preferred_element_type=F32).astype(BF16)
-        projected[row] = value
-        value = value.astype(F32)
-        shifted = value - jnp.sum(value, axis=0, keepdims=True) / C
-        spread = jnp.sum(shifted * shifted, axis=0, keepdims=True) / C
-        layer = (shifted * lax.rsqrt(spread + 1e-05)).astype(BF16)
-        layered[row] = layer
+        for half in halves:
+            projected[row, half, :] = jnp.dot(
+                proj_w[half, :], normed[row], preferred_element_type=F32
+            ).astype(BF16)
+    for row in range(rows):
+        value = projected[row].astype(F32)
+        shifted = value - over_rows(value, jnp.sum) / C
+        spread = over_rows(shifted * shifted, jnp.sum) / C
+        layered[row] = (shifted * lax.rsqrt(spread + 1e-05)).astype(BF16)
         at = slice(row * WIDTH, (row + 1) * WIDTH)
-        heads[:, at] = jnp.dot(kv_w[...], layer, preferred_element_type=F32).astype(BF16)
+        for half in halves:
+            heads[half, at] = jnp.dot(
+                kv_w[half, :], layered[row], preferred_element_type=F32
+            ).astype(BF16)
     proj_ref[...] = projected[lax.axis_index("patch")]
     share = out_ref.shape[1]
     mine = layered[lax.axis_index("patch"), :, pl.ds(pl.multiple_of(lax.axis_index("sub") * share, 128), share)]
     query = (jnp.dot(q_w[...], mine, preferred_element_type=F32) * 0.125).astype(BF16)
+    queries[...] = query
     channels = query.shape[0]
-    for start in range(0, channels, HEAD_DIM):
-        at = slice(start, start + HEAD_DIM)
-        scores = lax.dot_general(
-            heads[at, :], query[at], (((0,), (0,)), ((), ())), preferred_element_type=F32
-        )
-        weights = jnp.exp(scores - jnp.max(scores, axis=0, keepdims=True))
-        total = jnp.sum(weights, axis=0, keepdims=True)
+    count = channels // HEAD_DIM
+
+    def score(head):
+        at = slice(head * HEAD_DIM, (head + 1) * HEAD_DIM)
+        scores[head % 2] = lax.dot_general(
+            heads[at, :], queries[at, :], (((0,), (0,)), ((), ())), preferred_element_type=F32
+        )
+
+    score(0)
+    for head in range(count):
+        if head + 1 < count:
+            score(head + 1)
+        parts = [slice(at, at + WIDTH) for at in range(0, rows * WIDTH, WIDTH)]
+        peak = functools.reduce(
+            jnp.maximum, [over_rows(scores[head % 2, part, :], jnp.max) for part in parts]
+        )
+        total = 0.0
+        for part in parts:
+            weights = jnp.exp(scores[head % 2, part, :] - peak)
+            total = total + over_rows(weights, jnp.sum)
+            probs[head % 2, part, :] = weights.astype(BF16)
+        at = channels + head * HEAD_DIM
         weighted = jnp.dot(
-            heads[channels + start : channels + start + HEAD_DIM, :],
-            weights.astype(BF16),
-            preferred_element_type=F32,
-        )
-        out_ref[at, :] = (weighted / total).astype(BF16)
-
-
-def finish(own, chan, sub, both, proj, res_one, res_two, out_w, last_w, out_ref, attended):
+            heads[at : at + HEAD_DIM, :], probs[head % 2], preferred_element_type=F32
+        )
+        out_ref[head * HEAD_DIM : (head + 1) * HEAD_DIM, :] = (weighted / total).astype(BF16)
+
+
+def fold(proj, res_one, res_two, out_w, last_w, folded_ref, base_ref):
+    folded_ref[...] = jnp.dot(
+        last_w[...], out_w[...], preferred_element_type=F32
+    ).astype(BF16)
+    base = jnp.dot(last_w[...], proj[...], preferred_element_type=F32)
+    for part, res in enumerate((res_one, res_two)):
+        at = slice(part * CHUNK, (part + 1) * CHUNK)
+        base_ref[at, :] = res[...].astype(F32) + base[at]
+
+
+def finish(own, chan, sub, both, folded, base, out_ref, attended):
     channels, share = own.shape
     for flip, block in zip(FLIPS, (own, chan, sub, both)):
         place = own_place() ^ flip
         at = pl.multiple_of((place >> 1) * channels, 16)
         lanes = pl.multiple_of((place & 1) * share, 128)
         attended[pl.ds(at, channels), pl.ds(lanes, share)] = block[...]
-    mixed = proj[...].astype(F32) + jnp.dot(
-        out_w[...], attended[...], preferred_element_type=F32
-    )
-    last = jnp.dot(last_w[...], mixed.astype(BF16), preferred_element_type=F32)
-    for part, res in enumerate((res_one, res_two)):
-        at = slice(part * CHUNK, (part + 1) * CHUNK)
-        out_ref[at, :] = (res[...].astype(F32) + last[at]).astype(BF16)
+    last = jnp.dot(folded[...], attended[...], preferred_element_type=F32)
+    out_ref[...] = (base[...] + last).astype(BF16)
 
 
 def swapped(array, axis, by=1):
@@ -329,15 +361,22 @@
     attended, projected = call(
         attend, [((2 * OWN, share), BF16), ((C, WIDTH), BF16)],
         *one, *two, proj_in, *heads_w,
-        scratch=[((rows, C, WIDTH), BF16)] * 3 + [((4 * OWN, rows * WIDTH), BF16)],
+        scratch=[((rows, C, WIDTH), BF16)] * 3 + [
+            ((4 * OWN, rows * WIDTH), BF16), ((2 * OWN, share), BF16),
+            ((2, rows * WIDTH, share), F32), ((2, rows * WIDTH, share), BF16),
+        ],
         flops=4 * 10**9, limit=32,
     )
     _, out_chan = barrier((attended, out_chan))
     out_all = stacked((out_w, out_chan, out_sub, swapped(out_chan, "sub")))
-    attended, (out_all,) = exchanged(attended, out_all)
+    folded = call(
+        fold, [((OWN, C), BF16), ((OWN, WIDTH), F32)], projected, res_one, res_two,
+        out_all, proj_out_w, flops=10**8,
+    )
+    attended, folded = exchanged(attended, *folded)
     return call(
-        finish, [((OWN, WIDTH), BF16)], *attended, projected, res_one, res_two,
-        out_all, proj_out_w, scratch=[((C, WIDTH), BF16)],
+        finish, [((OWN, WIDTH), BF16)], *attended, *folded,
+        scratch=[((C, WIDTH), BF16)],
     )[0]
 
 

time: 67.8 us -> 67.4 us (level)
  Pallas kernels: 18 us -> 16.8 us
  waiting for transfers between devices: 24.2 us -> 24.9 us
    pallas_call x15 -> x16, Pallas kernels: 18 us -> 16.8 us  [call(): pl.pallas_call(kernel, out_shape=[jax.ShapeDtypeStruct(s, t) for s, t in...]
    ppermute x32, waiting for transfers between devices: 24.2 us -> 24.9 us  [swapped(): lax.ppermute(array, axis, [(i, i ^ by) for i in range(lax.axis_size(axis))])]
  transfers between devices with their start and end apart: 32 -> 32, of which waited for: 12 -> 12; matrix products, arithmetic and copies ran while one was open for 0% -> 0% of each run, Pallas kernels for 23% -> 22%
where the time goes in v2:
time: 67.4 us; the launch traced here: 67.3 us
  waiting for transfers between devices  24.9 us (37%)
  starting transfers between devices  22.9 us (34%)
  Pallas kernels  16.8 us (25%)
  local copies, waits for them, and re-layouts  1.55 us (2%)
  between operations  0.93 us (1%)
    ppermute x32, waiting for transfers between devices, swapped(): lax.ppermute(array, axis, [(i, i ^ by) for i in range(lax.axis_size(axis))])  24.9 us
    ppermute x32, starting transfers between devices, swapped(): lax.ppermute(array, axis, [(i, i ^ by) for i in range(lax.axis_size(axis))])  22.9 us
    pallas_call x16, Pallas kernels, call(): pl.pallas_call(kernel, out_shape=[jax.ShapeDtypeStruct(s, t) for s, t in...  16.8 us
    unnamed x20, local copies, waits for them, and re-layouts  1.55 us
  transfers between devices with their start and end apart: 32, of which 12 were waited for; matrix products, arithmetic and copies ran while one was open for 0% of the time, Pallas kernels for 22%

profile of v2, /device:TPU:0, one launch (start us, length us, event | category | flops | bytes accessed | tf_op | source)
XLA Modules:
  0.0 67.3 jit_solution(11086179646898965554)
XLA Ops:
  0.0 5.1 %collective-permute-start.2 = (bf16[160,256]{1,0:T(8,128)(2,1)}, bf16[160,256]{1,0:T(8,128)(2,1)S(1)}, u32[]{:S(2)}, u32[]{:S(2)}) collective-permute-start(bf16[160,256]{1,0:T(8,128)(2,1)} %refs_0_.1), channel_id=1, source_target_pairs={{0,12},{4,8},{8,4},{12,0},{1,13},{5,9},{9,5},{13,1},{2,14},{6,10},... | collective-permute-start | bytes 245768 | tf_op jit(solution)/shard_map/ppermute | solution.py:268
  5.6 1.7 %collective-permute-start.3 = (bf16[160,256]{1,0:T(8,128)(2,1)}, bf16[160,256]{1,0:T(8,128)(2,1)S(1)}, u32[]{:S(2)}, u32[]{:S(2)}) collective-permute-start(bf16[160,256]{1,0:T(8,128)(2,1)} %refs_0_.1), channel_id=1, source_target_pairs={{0,2},{2,0},{1,3},{3,1},{4,6},{6,4},{5,7},{7,5},{8,10},{10,8},{9,1... | collective-permute-start | bytes 245768 | tf_op jit(solution)/shard_map/ppermute | solution.py:268
  8.2 3.3 %collective-permute-done.refs_1_ = bf16[160,256]{1,0:T(8,128)(2,1)S(1)} collective-permute-done((bf16[160,256]{1,0:T(8,128)(2,1)}, bf16[160,256]{1,0:T(8,128)(2,1)S(1)}, u32[]{:S(2)}, u32[]{:S(2)}) %collective-permute-start) | collective-permute-done | bytes 81952 | tf_op jit(solution)/shard_map/ppermute | solution.py:268
  11.5 1.6 %collective-permute-start.4 = (bf16[160,256]{1,0:T(8,128)(2,1)S(1)}, bf16[160,256]{1,0:T(8,128)(2,1)S(1)}, u32[]{:S(2)}, u32[]{:S(2)}) collective-permute-start(bf16[160,256]{1,0:T(8,128)(2,1)S(1)} %collective-permute-done.refs_1_), channel_id=1, source_target_pairs={{0,2},{2,0},{1,3},{3,1},{4,6},{6,4},{5,7},{7,5},{8,10},{10,8},{9,1... | collective-permute-start | bytes 245768 | tf_op jit(solution)/shard_map/ppermute | solution.py:268
  13.6 1.6 %collective-permute-start.6 = (bf16[160,256]{1,0:T(8,128)(2,1)S(1)}, bf16[160,256]{1,0:T(8,128)(2,1)S(1)}, u32[]{:S(2)}, u32[]{:S(2)}) collective-permute-start(bf16[160,256]{1,0:T(8,128)(2,1)S(1)} %collective-permute-done.2.refs_3_), channel_id=1, source_target_pairs={{0,2},{2,0},{1,3},{3,1},{4,6},{6,4},{5,7},{7,5},{8,10},{10,8},{9,1... | collective-permute-start | bytes 245768 | tf_op jit(solution)/shard_map/ppermute | solution.py:268
  15.2 1.5 %copy-done.8 = bf16[9,160,640]{2,1,0:T(8,128)(2,1)S(1)} copy-done((bf16[9,160,640]{2,1,0:T(8,128)(2,1)S(1)}, bf16[9,160,640]{2,1,0:T(8,128)(2,1)}, u32[]{:S(2)}) %copy-start.8) | copy-done | bytes 1843224
  16.7 1.2 %shard_map.109 = (bf16[480,960]{1,0:T(8,128)(2,1)S(1)}, bf16[240,960]{1,0:T(8,128)(2,1)S(1)}, bf16[240,960]{1,0:T(8,128)(2,1)S(1)}) custom-call(bf16[9,160,640]{2,1,0:T(8,128)(2,1)S(1)} %copy-done.8), custom_call_target="tpu_custom_call" | custom-call | flops 1000000000 | bytes 1843200 | tf_op jit(solution)/shard_map/pallas_call | solution.py:34
  18.6 0.9 %shard_map.110 = (bf16[4,160,256]{2,1,0:T(8,128)(2,1)S(1)}, bf16[2,4,80,256]{3,2,1,0:T(8,128)(2,1)S(1)}, bf16[2,4,80,256]{3,2,1,0:T(8,128)(2,1)S(1)}) custom-call(bf16[160,256]{1,0:T(8,128)(2,1)S(1)} %copy-done.7, bf16[160,256]{1,0:T(8,128)(2,1)S(1)} %collective-permute-done.refs_1_, bf16[160,256]{1,0:T(8,128)(2,1)S(1)} %collective-permute-done.1.refs_2_, ...), custom_call_target="tpu_custom_call" | custom-call | bytes 655360 | tf_op jit(solution)/shard_map/pallas_call | solution.py:34
  21.1 1.4 %shard_map.111 = (f32[4,80,256]{2,1,0:T(8,128)S(1)}, f32[4,80,256]{2,1,0:T(8,128)S(1)}) custom-call(bf16[2,4,80,256]{3,2,1,0:T(8,128)(2,1)S(1)} %get-tuple-element.77.refs_0_, bf16[2,4,80,256]{3,2,1,0:T(8,128)(2,1)S(1)} %collective-permute-done.8.refs_1_, bf16[480,960]{1,0:T(8,128)(2,1)S(1)} %get-tuple-element.78.refs_2_), custom_call_target="tpu_custom_call" | custom-call | flops 943718400 | bytes 1576960 | tf_op jit(solution)/shard_map/pallas_call | solution.py:34
  22.5 1.1 %shard_map.114.refs_0_ = bf16[4,80,256]{2,1,0:T(8,128)(2,1)S(1)} custom-call(bf16[2,4,80,256]{3,2,1,0:T(8,128)(2,1)S(1)} %get-tuple-element.75.refs_0_, bf16[2,4,80,256]{3,2,1,0:T(8,128)(2,1)S(1)} %collective-permute-done.7.refs_1_, bf16[240,960]{1,0:T(8,128)(2,1)S(1)} %get-tuple-element.83.refs_2_, f32[4,80,256]{2,1,0:T(8,128)S(1)} %get-tuple-element.84.refs_3_, ...), custom_call_target="tpu_custom_call" | custom-call | flops 471859200 | bytes 1444480 | tf_op jit(solution)/shard_map/pallas_call | solution.py:34
  23.7 1.2 %collective-permute-start.12 = (bf16[4,80,256]{2,1,0:T(8,128)(2,1)S(1)}, bf16[4,80,256]{2,1,0:T(8,128)(2,1)S(1)}, u32[]{:S(2)}, u32[]{:S(2)}) collective-permute-start(bf16[4,80,256]{2,1,0:T(8,128)(2,1)S(1)} %shard_map.114.refs_0_), channel_id=1, source_target_pairs={{0,2},{2,0},{1,3},{3,1},{4,6},{6,4},{5,7},{7,5},{8,10},{10,8},{9,1... | collective-permute-start | bytes 491528 | tf_op jit(solution)/shard_map/ppermute | solution.py:268
  24.9 1.1 %shard_map.113.refs_0_ = bf16[4,80,256]{2,1,0:T(8,128)(2,1)S(1)} custom-call(bf16[2,4,80,256]{3,2,1,0:T(8,128)(2,1)S(1)} %get-tuple-element.75.refs_0_, bf16[2,4,80,256]{3,2,1,0:T(8,128)(2,1)S(1)} %collective-permute-done.7.refs_1_, bf16[240,960]{1,0:T(8,128)(2,1)S(1)} %get-tuple-element.76.refs_2_, f32[4,80,256]{2,1,0:T(8,128)S(1)} %get-tuple-element.79.refs_3_, ...), custom_call_target="tpu_custom_call" | custom-call | flops 471859200 | bytes 1444480 | tf_op jit(solution)/shard_map/pallas_call | solution.py:34
  26.0 0.9 %collective-permute-start.9 = (bf16[4,80,256]{2,1,0:T(8,128)(2,1)S(1)}, bf16[4,80,256]{2,1,0:T(8,128)(2,1)S(1)}, u32[]{:S(2)}, u32[]{:S(2)}) collective-permute-start(bf16[4,80,256]{2,1,0:T(8,128)(2,1)S(1)} %shard_map.113.refs_0_), channel_id=1, source_target_pairs={{0,2},{2,0},{1,3},{3,1},{4,6},{6,4},{5,7},{7,5},{8,10},{10,8},{9,1... | collective-permute-start | bytes 491528 | tf_op jit(solution)/shard_map/ppermute | solution.py:268
  27.0 1.2 %shard_map.116 = (bf16[480,960]{1,0:T(8,128)(2,1)S(1)}, bf16[240,960]{1,0:T(8,128)(2,1)S(1)}, bf16[240,960]{1,0:T(8,128)(2,1)S(1)}) custom-call(bf16[9,160,640]{2,1,0:T(8,128)(2,1)S(1)} %copy-done.9), custom_call_target="tpu_custom_call" | custom-call | flops 1000000000 | bytes 1843200 | tf_op jit(solution)/shard_map/pallas_call | solution.py:34
  28.3 2.5 %collective-permute-done.12.refs_1_ = bf16[4,80,256]{2,1,0:T(8,128)(2,1)S(1)} collective-permute-done((bf16[4,80,256]{2,1,0:T(8,128)(2,1)S(1)}, bf16[4,80,256]{2,1,0:T(8,128)(2,1)S(1)}, u32[]{:S(2)}, u32[]{:S(2)}) %collective-permute-start.12) | collective-permute-done | bytes 163872 | tf_op jit(solution)/shard_map/ppermute | solution.py:268
  31.3 2.4 %collective-permute-done.9.refs_1_ = bf16[4,80,256]{2,1,0:T(8,128)(2,1)S(1)} collective-permute-done((bf16[4,80,256]{2,1,0:T(8,128)(2,1)S(1)}, bf16[4,80,256]{2,1,0:T(8,128)(2,1)S(1)}, u32[]{:S(2)}, u32[]{:S(2)}) %collective-permute-start.9) | collective-permute-done | bytes 163872 | tf_op jit(solution)/shard_map/ppermute | solution.py:268
  34.2 1.2 %collective-permute-start.19 = (bf16[160,640]{1,0:T(8,128)(2,1)S(1)}, bf16[160,640]{1,0:T(8,128)(2,1)S(1)}, u32[]{:S(2)}, u32[]{:S(2)}) collective-permute-start(bf16[160,640]{1,0:T(8,128)(2,1)S(1)} %copy-done.4), channel_id=1, source_target_pairs={{0,2},{2,0},{1,3},{3,1},{4,6},{6,4},{5,7},{7,5},{8,10},{10,8},{9,1... | collective-permute-start | bytes 614408 | tf_op jit(solution)/shard_map/ppermute | solution.py:268
  35.4 1.4 %shard_map.117 = (f32[4,80,256]{2,1,0:T(8,128)S(1)}, f32[4,80,256]{2,1,0:T(8,128)S(1)}) custom-call(bf16[4,80,256]{2,1,0:T(8,128)(2,1)S(1)} %shard_map.114.refs_0_, bf16[4,80,256]{2,1,0:T(8,128)(2,1)S(1)} %collective-permute-done.12.refs_1_, bf16[4,80,256]{2,1,0:T(8,128)(2,1)S(1)} %collective-permute-done.16.refs_2_, ...), custom_call_target="tpu_custom_call" | custom-call | flops 943718400 | bytes 1576960 | tf_op jit(solution)/shard_map/pallas_call | solution.py:34
  36.8 1.1 %shard_map.118 = (bf16[4,80,256]{2,1,0:T(8,128)(2,1)S(1)}, bf16[80,256]{1,0:T(8,128)(2,1)S(1)}) custom-call(bf16[4,80,256]{2,1,0:T(8,128)(2,1)S(1)} %shard_map.113.refs_0_, bf16[4,80,256]{2,1,0:T(8,128)(2,1)S(1)} %collective-permute-done.9.refs_1_, bf16[4,80,256]{2,1,0:T(8,128)(2,1)S(1)} %collective-permute-done.10.refs_2_, ...), custom_call_target="tpu_custom_call" | custom-call | flops 471859200 | bytes 1771520 | tf_op jit(solution)/shard_map/pallas_call | solution.py:34
  37.9 3.3 %collective-permute-done.19.chan = bf16[160,640]{1,0:T(8,128)(2,1)S(1)} collective-permute-done((bf16[160,640]{1,0:T(8,128)(2,1)S(1)}, bf16[160,640]{1,0:T(8,128)(2,1)S(1)}, u32[]{:S(2)}, u32[]{:S(2)}) %collective-permute-start.19) | collective-permute-done | bytes 204832 | tf_op jit(solution)/shard_map/ppermute | solution.py:268
  41.7 1.1 %shard_map.120 = (bf16[4,80,256]{2,1,0:T(8,128)(2,1)S(1)}, bf16[80,256]{1,0:T(8,128)(2,1)S(1)}) custom-call(bf16[4,80,256]{2,1,0:T(8,128)(2,1)S(1)} %shard_map.113.refs_0_, bf16[4,80,256]{2,1,0:T(8,128)(2,1)S(1)} %collective-permute-done.9.refs_1_, bf16[4,80,256]{2,1,0:T(8,128)(2,1)S(1)} %collective-permute-done.10.refs_2_, ...), custom_call_target="tpu_custom_call" | custom-call | flops 471859200 | bytes 1771520 | tf_op jit(solution)/shard_map/pallas_call | solution.py:34
  42.8 1.2 %collective-permute-start.24 = (bf16[4,80,256]{2,1,0:T(8,128)(2,1)S(1)}, bf16[4,80,256]{2,1,0:T(8,128)(2,1)S(1)}, u32[]{:S(2)}, u32[]{:S(2)}) collective-permute-start(bf16[4,80,256]{2,1,0:T(8,128)(2,1)S(1)} %get-tuple-element.112.refs_4_), channel_id=1, source_target_pairs={{0,2},{2,0},{1,3},{3,1},{4,6},{6,4},{5,7},{7,5},{8,10},{10,8},{9,1... | collective-permute-start | bytes 491528 | tf_op jit(solution)/shard_map/ppermute | solution.py:268
  44.1 0.9 %collective-permute-start.18 = (bf16[4,80,256]{2,1,0:T(8,128)(2,1)S(1)}, bf16[4,80,256]{2,1,0:T(8,128)(2,1)S(1)}, u32[]{:S(2)}, u32[]{:S(2)}) collective-permute-start(bf16[4,80,256]{2,1,0:T(8,128)(2,1)S(1)} %get-tuple-element.107.refs_0_), channel_id=1, source_target_pairs={{0,2},{2,0},{1,3},{3,1},{4,6},{6,4},{5,7},{7,5},{8,10},{10,8},{9,1... | collective-permute-start | bytes 491528 | tf_op jit(solution)/shard_map/ppermute | solution.py:268
  44.9 5.0 %collective-permute-done.24.refs_5_ = bf16[4,80,256]{2,1,0:T(8,128)(2,1)S(1)} collective-permute-done((bf16[4,80,256]{2,1,0:T(8,128)(2,1)S(1)}, bf16[4,80,256]{2,1,0:T(8,128)(2,1)S(1)}, u32[]{:S(2)}, u32[]{:S(2)}) %collective-permute-start.24) | collective-permute-done | bytes 163872 | tf_op jit(solution)/shard_map/ppermute | solution.py:268
  50.6 1.9 %collective-permute-done.18.refs_1_ = bf16[4,80,256]{2,1,0:T(8,128)(2,1)S(1)} collective-permute-done((bf16[4,80,256]{2,1,0:T(8,128)(2,1)S(1)}, bf16[4,80,256]{2,1,0:T(8,128)(2,1)S(1)}, u32[]{:S(2)}, u32[]{:S(2)}) %collective-permute-start.18) | collective-permute-done | bytes 163872 | tf_op jit(solution)/shard_map/ppermute | solution.py:268
  53.0 1.2 %collective-permute-start.28 = (bf16[160,640]{1,0:T(8,128)(2,1)S(1)}, bf16[160,640]{1,0:T(8,128)(2,1)S(1)}, u32[]{:S(2)}, u32[]{:S(2)}) collective-permute-start(bf16[160,640]{1,0:T(8,128)(2,1)S(1)} %copy-done.5), channel_id=1, source_target_pairs={{0,2},{2,0},{1,3},{3,1},{4,6},{6,4},{5,7},{7,5},{8,10},{10,8},{9,1... | collective-permute-start | bytes 614408 | tf_op jit(solution)/shard_map/ppermute | solution.py:268
  54.2 4.3 %shard_map.121 = (bf16[320,128]{1,0:T(8,128)(2,1)S(1)}, bf16[640,256]{1,0:T(8,128)(2,1)S(1)}) custom-call(bf16[4,80,256]{2,1,0:T(8,128)(2,1)S(1)} %get-tuple-element.107.refs_0_, bf16[4,80,256]{2,1,0:T(8,128)(2,1)S(1)} %collective-permute-done.18.refs_1_, bf16[4,80,256]{2,1,0:T(8,128)(2,1)S(1)} %collective-permute-done.22.refs_2_, ...), custom_call_target="tpu_custom_call" | custom-call | flops 4000000000 | bytes 3358720 | tf_op jit(solution)/shard_map/pallas_call | solution.py:34
  58.5 1.5 %collective-permute-done.28.chan = bf16[160,640]{1,0:T(8,128)(2,1)S(1)} collective-permute-done((bf16[160,640]{1,0:T(8,128)(2,1)S(1)}, bf16[160,640]{1,0:T(8,128)(2,1)S(1)}, u32[]{:S(2)}, u32[]{:S(2)}) %collective-permute-start.28) | collective-permute-done | bytes 204832 | tf_op jit(solution)/shard_map/ppermute | solution.py:268
  60.0 1.2 %collective-permute-start.27 = (bf16[320,128]{1,0:T(8,128)(2,1)S(1)}, bf16[320,128]{1,0:T(8,128)(2,1)S(1)}, u32[]{:S(2)}, u32[]{:S(2)}) collective-permute-start(bf16[320,128]{1,0:T(8,128)(2,1)S(1)} %get-tuple-element.125.own), channel_id=1, source_target_pairs={{0,2},{2,0},{1,3},{3,1},{4,6},{6,4},{5,7},{7,5},{8,10},{10,8},{9,1... | collective-permute-start | bytes 245768 | tf_op jit(solution)/shard_map/ppermute | solution.py:268
  62.0 2.9 %collective-permute-done.27.chan = bf16[320,128]{1,0:T(8,128)(2,1)S(1)} collective-permute-done((bf16[320,128]{1,0:T(8,128)(2,1)S(1)}, bf16[320,128]{1,0:T(8,128)(2,1)S(1)}, u32[]{:S(2)}, u32[]{:S(2)}) %collective-permute-start.27) | collective-permute-done | bytes 81952 | tf_op jit(solution)/shard_map/ppermute | solution.py:268
  65.4 0.8 %collective-permute-done.30.sub = bf16[320,128]{1,0:T(8,128)(2,1)S(1)} collective-permute-done((bf16[320,128]{1,0:T(8,128)(2,1)S(1)}, bf16[320,128]{1,0:T(8,128)(2,1)S(1)}, u32[]{:S(2)}, u32[]{:S(2)}) %collective-permute-start.30) | collective-permute-done | bytes 81952 | tf_op jit(solution)/shard_map/ppermute | solution.py:268
  66.3 0.9 %shard_map.124 = bf16[160,256]{1,0:T(8,128)(2,1)} custom-call(bf16[320,128]{1,0:T(8,128)(2,1)S(1)} %get-tuple-element.125.own, bf16[320,128]{1,0:T(8,128)(2,1)S(1)} %collective-permute-done.27.chan, bf16[320,128]{1,0:T(8,128)(2,1)S(1)} %collective-permute-done.30.sub, bf16[320,128]{1,0:T(8,128)(2,1)S(1)} %collective-permute-done.31.both, ...), custom_call_target="tpu_custom_call" | custom-call | bytes 696320 | tf_op jit(solution)/shard_map/pallas_call | solution.py:34
  (72 shorter events, 7.7 us)
Async XLA Ops:
  0.0 13.6 %collective-permute-start.2 = (bf16[160,256]{1,0:T(8,128)(2,1)}, bf16[160,256]{1,0:T(8,128)(2,1)S(1)}, u32[]{:S(2)}, u32[]{:S(2)}) collective-permute-start(bf16[160,256]{1,0:T(8,128)(2,1)} %refs_0_.1), channel_id=1, source_target_pairs={{0,12},{4,8},{8,4},{12,0},{1,13},{5,9},{9,5},{13,1},{2,14},{6,10},... | collective-permute-start | bytes 245768 | tf_op jit(solution)/shard_map/ppermute | solution.py:268
  5.1 6.4 %collective-permute-start = (bf16[160,256]{1,0:T(8,128)(2,1)}, bf16[160,256]{1,0:T(8,128)(2,1)S(1)}, u32[]{:S(2)}, u32[]{:S(2)}) collective-permute-start(bf16[160,256]{1,0:T(8,128)(2,1)} %refs_0_.1), channel_id=1, source_target_pairs={{0,4},{4,0},{8,12},{12,8},{1,5},{5,1},{9,13},{13,9},{2,6},{6,2},{1... | collective-permute-start | bytes 245768 | tf_op jit(solution)/shard_map/ppermute | solution.py:268
  5.1 8.0 %collective-permute-start.1 = (bf16[160,256]{1,0:T(8,128)(2,1)}, bf16[160,256]{1,0:T(8,128)(2,1)S(1)}, u32[]{:S(2)}, u32[]{:S(2)}) collective-permute-start(bf16[160,256]{1,0:T(8,128)(2,1)} %refs_0_.1), channel_id=1, source_target_pairs={{0,8},{4,12},{8,0},{12,4},{1,9},{5,13},{9,1},{13,5},{2,10},{6,14},... | collective-permute-start | bytes 245768 | tf_op jit(solution)/shard_map/ppermute | solution.py:268
  5.6 12.3 %collective-permute-start.3 = (bf16[160,256]{1,0:T(8,128)(2,1)}, bf16[160,256]{1,0:T(8,128)(2,1)S(1)}, u32[]{:S(2)}, u32[]{:S(2)}) collective-permute-start(bf16[160,256]{1,0:T(8,128)(2,1)} %refs_0_.1), channel_id=1, source_target_pairs={{0,2},{2,0},{1,3},{3,1},{4,6},{6,4},{5,7},{7,5},{8,10},{10,8},{9,1... | collective-permute-start | bytes 245768 | tf_op jit(solution)/shard_map/ppermute | solution.py:268
  11.5 6.4 %collective-permute-start.4 = (bf16[160,256]{1,0:T(8,128)(2,1)S(1)}, bf16[160,256]{1,0:T(8,128)(2,1)S(1)}, u32[]{:S(2)}, u32[]{:S(2)}) collective-permute-start(bf16[160,256]{1,0:T(8,128)(2,1)S(1)} %collective-permute-done.refs_1_), channel_id=1, source_target_pairs={{0,2},{2,0},{1,3},{3,1},{4,6},{6,4},{5,7},{7,5},{8,10},{10,8},{9,1... | collective-permute-start | bytes 245768 | tf_op jit(solution)/shard_map/ppermute | solution.py:268
  13.1 4.8 %collective-permute-start.5 = (bf16[160,256]{1,0:T(8,128)(2,1)S(1)}, bf16[160,256]{1,0:T(8,128)(2,1)S(1)}, u32[]{:S(2)}, u32[]{:S(2)}) collective-permute-start(bf16[160,256]{1,0:T(8,128)(2,1)S(1)} %collective-permute-done.1.refs_2_), channel_id=1, source_target_pairs={{0,2},{2,0},{1,3},{3,1},{4,6},{6,4},{5,7},{7,5},{8,10},{10,8},{9,1... | collective-permute-start | bytes 245768 | tf_op jit(solution)/shard_map/ppermute | solution.py:268
  13.6 5.0 %collective-permute-start.6 = (bf16[160,256]{1,0:T(8,128)(2,1)S(1)}, bf16[160,256]{1,0:T(8,128)(2,1)S(1)}, u32[]{:S(2)}, u32[]{:S(2)}) collective-permute-start(bf16[160,256]{1,0:T(8,128)(2,1)S(1)} %collective-permute-done.2.refs_3_), channel_id=1, source_target_pairs={{0,2},{2,0},{1,3},{3,1},{4,6},{6,4},{5,7},{7,5},{8,10},{10,8},{9,1... | collective-permute-start | bytes 245768 | tf_op jit(solution)/shard_map/ppermute | solution.py:268
  19.4 1.7 %collective-permute-start.8 = (bf16[2,4,80,256]{3,2,1,0:T(8,128)(2,1)S(1)}, bf16[2,4,80,256]{3,2,1,0:T(8,128)(2,1)S(1)}, u32[]{:S(2)}, u32[]{:S(2)}) collective-permute-start(bf16[2,4,80,256]{3,2,1,0:T(8,128)(2,1)S(1)} %get-tuple-element.77.refs_0_), channel_id=1, source_target_pairs={{0,1},{1,0},{2,3},{3,2},{4,5},{5,4},{6,7},{7,6},{8,9},{9,8},{10,11... | collective-permute-start | bytes 983048 | tf_op jit(solution)/shard_map/ppermute | solution.py:268
  19.5 3.0 %collective-permute-start.7 = (bf16[2,4,80,256]{3,2,1,0:T(8,128)(2,1)S(1)}, bf16[2,4,80,256]{3,2,1,0:T(8,128)(2,1)S(1)}, u32[]{:S(2)}, u32[]{:S(2)}) collective-permute-start(bf16[2,4,80,256]{3,2,1,0:T(8,128)(2,1)S(1)} %get-tuple-element.75.refs_0_), channel_id=1, source_target_pairs={{0,1},{1,0},{2,3},{3,2},{4,5},{5,4},{6,7},{7,6},{8,9},{9,8},{10,11... | collective-permute-start | bytes 983048 | tf_op jit(solution)/shard_map/ppermute | solution.py:268
  20.0 6.9 %collective-permute-start.14 = (bf16[2,160,640]{2,1,0:T(8,128)(2,1)S(1)}, bf16[2,160,640]{2,1,0:T(8,128)(2,1)S(1)}, u32[]{:S(2)}, u32[]{:S(2)}) collective-permute-start(bf16[2,160,640]{2,1,0:T(8,128)(2,1)S(1)} %copy-done.2), channel_id=1, source_target_pairs={{0,1},{1,0},{2,3},{3,2},{4,5},{5,4},{6,7},{7,6},{8,9},{9,8},{10,11... | collective-permute-start | bytes 1228808 | tf_op jit(solution)/shard_map/ppermute | solution.py:268
  20.1 6.8 %collective-permute-start.13 = (bf16[160,640]{1,0:T(8,128)(2,1)S(1)}, bf16[160,640]{1,0:T(8,128)(2,1)S(1)}, u32[]{:S(2)}, u32[]{:S(2)}) collective-permute-start(bf16[160,640]{1,0:T(8,128)(2,1)S(1)} %copy-done.3), channel_id=1, source_target_pairs={{0,1},{1,0},{2,3},{3,2},{4,5},{5,4},{6,7},{7,6},{8,9},{9,8},{10,11... | collective-permute-start | bytes 614408 | tf_op jit(solution)/shard_map/ppermute | solution.py:268
  20.5 7.7 %collective-permute-start.15 = (bf16[160,640]{1,0:T(8,128)(2,1)S(1)}, bf16[160,640]{1,0:T(8,128)(2,1)S(1)}, u32[]{:S(2)}, u32[]{:S(2)}) collective-permute-start(bf16[160,640]{1,0:T(8,128)(2,1)S(1)} %copy-done.4), channel_id=1, source_target_pairs={{0,1},{1,0},{2,3},{3,2},{4,5},{5,4},{6,7},{7,6},{8,9},{9,8},{10,11... | collective-permute-start | bytes 614408 | tf_op jit(solution)/shard_map/ppermute | solution.py:268
  23.7 7.1 %collective-permute-start.12 = (bf16[4,80,256]{2,1,0:T(8,128)(2,1)S(1)}, bf16[4,80,256]{2,1,0:T(8,128)(2,1)S(1)}, u32[]{:S(2)}, u32[]{:S(2)}) collective-permute-start(bf16[4,80,256]{2,1,0:T(8,128)(2,1)S(1)} %shard_map.114.refs_0_), channel_id=1, source_target_pairs={{0,2},{2,0},{1,3},{3,1},{4,6},{6,4},{5,7},{7,5},{8,10},{10,8},{9,1... | collective-permute-start | bytes 491528 | tf_op jit(solution)/shard_map/ppermute | solution.py:268
  26.0 7.8 %collective-permute-start.9 = (bf16[4,80,256]{2,1,0:T(8,128)(2,1)S(1)}, bf16[4,80,256]{2,1,0:T(8,128)(2,1)S(1)}, u32[]{:S(2)}, u32[]{:S(2)}) collective-permute-start(bf16[4,80,256]{2,1,0:T(8,128)(2,1)S(1)} %shard_map.113.refs_0_), channel_id=1, source_target_pairs={{0,2},{2,0},{1,3},{3,1},{4,6},{6,4},{5,7},{7,5},{8,10},{10,8},{9,1... | collective-permute-start | bytes 491528 | tf_op jit(solution)/shard_map/ppermute | solution.py:268
  30.8 4.6 %collective-permute-start.16 = (bf16[4,80,256]{2,1,0:T(8,128)(2,1)S(1)}, bf16[4,80,256]{2,1,0:T(8,128)(2,1)S(1)}, u32[]{:S(2)}, u32[]{:S(2)}) collective-permute-start(bf16[4,80,256]{2,1,0:T(8,128)(2,1)S(1)} %shard_map.114.refs_0_), channel_id=1, source_target_pairs={{0,1},{1,0},{2,3},{3,2},{4,5},{5,4},{6,7},{7,6},{8,9},{9,8},{10,11... | collective-permute-start | bytes 491528 | tf_op jit(solution)/shard_map/ppermute | solution.py:268
  30.8 4.6 %collective-permute-start.17 = (bf16[4,80,256]{2,1,0:T(8,128)(2,1)S(1)}, bf16[4,80,256]{2,1,0:T(8,128)(2,1)S(1)}, u32[]{:S(2)}, u32[]{:S(2)}) collective-permute-start(bf16[4,80,256]{2,1,0:T(8,128)(2,1)S(1)} %collective-permute-done.12.refs_1_), channel_id=1, source_target_pairs={{0,1},{1,0},{2,3},{3,2},{4,5},{5,4},{6,7},{7,6},{8,9},{9,8},{10,11... | collective-permute-start | bytes 491528 | tf_op jit(solution)/shard_map/ppermute | solution.py:268
  33.7 3.0 %collective-permute-start.10 = (bf16[4,80,256]{2,1,0:T(8,128)(2,1)S(1)}, bf16[4,80,256]{2,1,0:T(8,128)(2,1)S(1)}, u32[]{:S(2)}, u32[]{:S(2)}) collective-permute-start(bf16[4,80,256]{2,1,0:T(8,128)(2,1)S(1)} %shard_map.113.refs_0_), channel_id=1, source_target_pairs={{0,1},{1,0},{2,3},{3,2},{4,5},{5,4},{6,7},{7,6},{8,9},{9,8},{10,11... | collective-permute-start | bytes 491528 | tf_op jit(solution)/shard_map/ppermute | solution.py:268
  33.7 3.1 %collective-permute-start.11 = (bf16[4,80,256]{2,1,0:T(8,128)(2,1)S(1)}, bf16[4,80,256]{2,1,0:T(8,128)(2,1)S(1)}, u32[]{:S(2)}, u32[]{:S(2)}) collective-permute-start(bf16[4,80,256]{2,1,0:T(8,128)(2,1)S(1)} %collective-permute-done.9.refs_1_), channel_id=1, source_target_pairs={{0,1},{1,0},{2,3},{3,2},{4,5},{5,4},{6,7},{7,6},{8,9},{9,8},{10,11... | collective-permute-start | bytes 491528 | tf_op jit(solution)/shard_map/ppermute | solution.py:268
  34.2 7.0 %collective-permute-start.19 = (bf16[160,640]{1,0:T(8,128)(2,1)S(1)}, bf16[160,640]{1,0:T(8,128)(2,1)S(1)}, u32[]{:S(2)}, u32[]{:S(2)}) collective-permute-start(bf16[160,640]{1,0:T(8,128)(2,1)S(1)} %copy-done.4), channel_id=1, source_target_pairs={{0,2},{2,0},{1,3},{3,1},{4,6},{6,4},{5,7},{7,5},{8,10},{10,8},{9,1... | collective-permute-start | bytes 614408 | tf_op jit(solution)/shard_map/ppermute | solution.py:268
  41.2 9.3 %collective-permute-start.20 = (bf16[160,640]{1,0:T(8,128)(2,1)S(1)}, bf16[160,640]{1,0:T(8,128)(2,1)S(1)}, u32[]{:S(2)}, u32[]{:S(2)}) collective-permute-start(bf16[160,640]{1,0:T(8,128)(2,1)S(1)} %collective-permute-done.19.chan), channel_id=1, source_target_pairs={{0,1},{1,0},{2,3},{3,2},{4,5},{5,4},{6,7},{7,6},{8,9},{9,8},{10,11... | collective-permute-start | bytes 614408 | tf_op jit(solution)/shard_map/ppermute | solution.py:268
  41.2 11.3 %collective-permute-start.21 = (bf16[160,640]{1,0:T(8,128)(2,1)S(1)}, bf16[160,640]{1,0:T(8,128)(2,1)S(1)}, u32[]{:S(2)}, u32[]{:S(2)}) collective-permute-start(bf16[160,640]{1,0:T(8,128)(2,1)S(1)} %copy-done.5), channel_id=1, source_target_pairs={{0,1},{1,0},{2,3},{3,2},{4,5},{5,4},{6,7},{7,6},{8,9},{9,8},{10,11... | collective-permute-start | bytes 614408 | tf_op jit(solution)/shard_map/ppermute | solution.py:268
  42.8 7.1 %collective-permute-start.24 = (bf16[4,80,256]{2,1,0:T(8,128)(2,1)S(1)}, bf16[4,80,256]{2,1,0:T(8,128)(2,1)S(1)}, u32[]{:S(2)}, u32[]{:S(2)}) collective-permute-start(bf16[4,80,256]{2,1,0:T(8,128)(2,1)S(1)} %get-tuple-element.112.refs_4_), channel_id=1, source_target_pairs={{0,2},{2,0},{1,3},{3,1},{4,6},{6,4},{5,7},{7,5},{8,10},{10,8},{9,1... | collective-permute-start | bytes 491528 | tf_op jit(solution)/shard_map/ppermute | solution.py:268
  44.1 8.5 %collective-permute-start.18 = (bf16[4,80,256]{2,1,0:T(8,128)(2,1)S(1)}, bf16[4,80,256]{2,1,0:T(8,128)(2,1)S(1)}, u32[]{:S(2)}, u32[]{:S(2)}) collective-permute-start(bf16[4,80,256]{2,1,0:T(8,128)(2,1)S(1)} %get-tuple-element.107.refs_0_), channel_id=1, source_target_pairs={{0,2},{2,0},{1,3},{3,1},{4,6},{6,4},{5,7},{7,5},{8,10},{10,8},{9,1... | collective-permute-start | bytes 491528 | tf_op jit(solution)/shard_map/ppermute | solution.py:268
  50.0 4.2 %collective-permute-start.25 = (bf16[4,80,256]{2,1,0:T(8,128)(2,1)S(1)}, bf16[4,80,256]{2,1,0:T(8,128)(2,1)S(1)}, u32[]{:S(2)}, u32[]{:S(2)}) collective-permute-start(bf16[4,80,256]{2,1,0:T(8,128)(2,1)S(1)} %get-tuple-element.112.refs_4_), channel_id=1, source_target_pairs={{0,1},{1,0},{2,3},{3,2},{4,5},{5,4},{6,7},{7,6},{8,9},{9,8},{10,11... | collective-permute-start | bytes 491528 | tf_op jit(solution)/shard_map/ppermute | solution.py:268
  50.0 4.2 %collective-permute-start.26 = (bf16[4,80,256]{2,1,0:T(8,128)(2,1)S(1)}, bf16[4,80,256]{2,1,0:T(8,128)(2,1)S(1)}, u32[]{:S(2)}, u32[]{:S(2)}) collective-permute-start(bf16[4,80,256]{2,1,0:T(8,128)(2,1)S(1)} %collective-permute-done.24.refs_5_), channel_id=1, source_target_pairs={{0,1},{1,0},{2,3},{3,2},{4,5},{5,4},{6,7},{7,6},{8,9},{9,8},{10,11... | collective-permute-start | bytes 491528 | tf_op jit(solution)/shard_map/ppermute | solution.py:268
  52.5 1.7 %collective-permute-start.22 = (bf16[4,80,256]{2,1,0:T(8,128)(2,1)S(1)}, bf16[4,80,256]{2,1,0:T(8,128)(2,1)S(1)}, u32[]{:S(2)}, u32[]{:S(2)}) collective-permute-start(bf16[4,80,256]{2,1,0:T(8,128)(2,1)S(1)} %get-tuple-element.107.refs_0_), channel_id=1, source_target_pairs={{0,1},{1,0},{2,3},{3,2},{4,5},{5,4},{6,7},{7,6},{8,9},{9,8},{10,11... | collective-permute-start | bytes 491528 | tf_op jit(solution)/shard_map/ppermute | solution.py:268
  52.5 1.7 %collective-permute-start.23 = (bf16[4,80,256]{2,1,0:T(8,128)(2,1)S(1)}, bf16[4,80,256]{2,1,0:T(8,128)(2,1)S(1)}, u32[]{:S(2)}, u32[]{:S(2)}) collective-permute-start(bf16[4,80,256]{2,1,0:T(8,128)(2,1)S(1)} %collective-permute-done.18.refs_1_), channel_id=1, source_target_pairs={{0,1},{1,0},{2,3},{3,2},{4,5},{5,4},{6,7},{7,6},{8,9},{9,8},{10,11... | collective-permute-start | bytes 491528 | tf_op jit(solution)/shard_map/ppermute | solution.py:268
  53.0 7.0 %collective-permute-start.28 = (bf16[160,640]{1,0:T(8,128)(2,1)S(1)}, bf16[160,640]{1,0:T(8,128)(2,1)S(1)}, u32[]{:S(2)}, u32[]{:S(2)}) collective-permute-start(bf16[160,640]{1,0:T(8,128)(2,1)S(1)} %copy-done.5), channel_id=1, source_target_pairs={{0,2},{2,0},{1,3},{3,1},{4,6},{6,4},{5,7},{7,5},{8,10},{10,8},{9,1... | collective-permute-start | bytes 614408 | tf_op jit(solution)/shard_map/ppermute | solution.py:268
  60.0 1.5 %collective-permute-start.29 = (bf16[160,640]{1,0:T(8,128)(2,1)S(1)}, bf16[160,640]{1,0:T(8,128)(2,1)S(1)}, u32[]{:S(2)}, u32[]{:S(2)}) collective-permute-start(bf16[160,640]{1,0:T(8,128)(2,1)S(1)} %collective-permute-done.28.chan), channel_id=1, source_target_pairs={{0,1},{1,0},{2,3},{3,2},{4,5},{5,4},{6,7},{7,6},{8,9},{9,8},{10,11... | collective-permute-start | bytes 614408 | tf_op jit(solution)/shard_map/ppermute | solution.py:268
  60.0 4.9 %collective-permute-start.27 = (bf16[320,128]{1,0:T(8,128)(2,1)S(1)}, bf16[320,128]{1,0:T(8,128)(2,1)S(1)}, u32[]{:S(2)}, u32[]{:S(2)}) collective-permute-start(bf16[320,128]{1,0:T(8,128)(2,1)S(1)} %get-tuple-element.125.own), channel_id=1, source_target_pairs={{0,2},{2,0},{1,3},{3,1},{4,6},{6,4},{5,7},{7,5},{8,10},{10,8},{9,1... | collective-permute-start | bytes 245768 | tf_op jit(solution)/shard_map/ppermute | solution.py:268
  64.9 1.3 %collective-permute-start.30 = (bf16[320,128]{1,0:T(8,128)(2,1)S(1)}, bf16[320,128]{1,0:T(8,128)(2,1)S(1)}, u32[]{:S(2)}, u32[]{:S(2)}) collective-permute-start(bf16[320,128]{1,0:T(8,128)(2,1)S(1)} %get-tuple-element.125.own), channel_id=1, source_target_pairs={{0,1},{1,0},{2,3},{3,2},{4,5},{5,4},{6,7},{7,6},{8,9},{9,8},{10,11... | collective-permute-start | bytes 245768 | tf_op jit(solution)/shard_map/ppermute | solution.py:268
  64.9 1.4 %collective-permute-start.31 = (bf16[320,128]{1,0:T(8,128)(2,1)S(1)}, bf16[320,128]{1,0:T(8,128)(2,1)S(1)}, u32[]{:S(2)}, u32[]{:S(2)}) collective-permute-start(bf16[320,128]{1,0:T(8,128)(2,1)S(1)} %collective-permute-done.27.chan), channel_id=1, source_target_pairs={{0,1},{1,0},{2,3},{3,2},{4,5},{5,4},{6,7},{7,6},{8,9},{9,8},{10,11... | collective-permute-start | bytes 245768 | tf_op jit(solution)/shard_map/ppermute | solution.py:268
  (10 other events, 97.7 us)

commit v3 on v2

--- a/solution.py
+++ b/solution.py
@@ -66,22 +66,26 @@
     return values * jax.nn.sigmoid(values)
 
 
-def first_norm(*refs):
-    rows_ref, *chunk_refs = refs[-3:]
-    pieces = refs[:-3]
-    count = len(pieces) // 2
-    position = lax.axis_index("patch")
-    places = [position ^ by for by in range(count)]
-    for piece, place in zip(pieces, places):
-        rows_ref[place] = piece[...]
-    for part, out in enumerate(chunk_refs):
+def first_norm(part):
+    def kernel(*refs):
+        *pieces, out = refs
+        count = len(pieces) // 2
+        position = lax.axis_index("patch")
         for side in range(2):
             values = [
                 piece[part * CHUNK : (part + 1) * CHUNK, :].astype(F32)
                 for piece in pieces[side * count : (side + 1) * count]
             ]
-            for value, place in zip(normal_form(values, 1e-05), places):
-                out[side, place] = silu(value).astype(BF16)
+            for by, value in enumerate(normal_form(values, 1e-05)):
+                out[side, position ^ by] = silu(value).astype(BF16)
+
+    return kernel
+
+
+def order_rows(*refs):
+    *pieces, rows_ref = refs
+    for by, piece in enumerate(pieces):
+        rows_ref[lax.axis_index("patch") ^ by] = piece[...]
 
 
 def arrange(weight, half_ref, *rest_refs):
@@ -315,10 +319,12 @@
     heads_w = (*heads_w, *(swapped(weight, "sub") for weight in heads_w))
     others, conv1_w, embedded = barrier((others, arranged(conv1_w), embedded))
     pair = (2,) + chunk
-    latent_rows, one, two = call(
-        first_norm, [((rows, OWN, WIDTH), BF16), (pair, BF16), (pair, BF16)], *pieces, *others,
+    one, two = (
+        call(first_norm(part), [(pair, BF16)], *pieces, *others)[0]
+        for part in range(2)
     )
     one, two = (one, swapped(one, "sub")), (two, swapped(two, "sub"))
+    (latent_rows,) = call(order_rows, [((rows, OWN, WIDTH), BF16)], *pieces)
     (bias,) = call(time_bias, [((OWN, 1), F32)], embedded, time_w1.T, time_proj, flops=10**8)
 
     def halves(blocks, weight):

time: 67.4 us -> 67.4 us (level)
    pallas_call x16 -> x18, Pallas kernels: 16.8 us -> 16.8 us  [call(): pl.pallas_call(kernel, out_shape=[jax.ShapeDtypeStruct(s, t) for s, t in...]
  transfers between devices with their start and end apart: 32 -> 32, of which waited for: 12 -> 12; matrix products, arithmetic and copies ran while one was open for 0% -> 0% of each run, Pallas kernels for 22% -> 23%
where the time goes in v3:
time: 67.4 us; the launch traced here: 67.2 us
  waiting for transfers between devices  24.8 us (37%)
  starting transfers between devices  23 us (34%)
  Pallas kernels  16.8 us (25%)
  local copies, waits for them, and re-layouts  1.56 us (2%)
  between operations  0.98 us (1%)
    ppermute x32, waiting for transfers between devices, swapped(): lax.ppermute(array, axis, [(i, i ^ by) for i in range(lax.axis_size(axis))])  24.8 us
    ppermute x32, starting transfers between devices, swapped(): lax.ppermute(array, axis, [(i, i ^ by) for i in range(lax.axis_size(axis))])  23 us
    pallas_call x18, Pallas kernels, call(): pl.pallas_call(kernel, out_shape=[jax.ShapeDtypeStruct(s, t) for s, t in...  16.8 us
    unnamed x20, local copies, waits for them, and re-layouts  1.55 us
  transfers between devices with their start and end apart: 32, of which 12 were waited for; matrix products, arithmetic and copies ran while one was open for 0% of the time, Pallas kernels for 23%

profile of v3, /device:TPU:0, one launch (start us, length us, event | category | flops | bytes accessed | tf_op | source)
XLA Modules:
  0.0 67.2 jit_solution(188316896843104059)
XLA Ops:
  0.0 5.1 %collective-permute-start.2 = (bf16[160,256]{1,0:T(8,128)(2,1)}, bf16[160,256]{1,0:T(8,128)(2,1)S(1)}, u32[]{:S(2)}, u32[]{:S(2)}) collective-permute-start(bf16[160,256]{1,0:T(8,128)(2,1)} %refs_0_.5), channel_id=1, source_target_pairs={{0,12},{4,8},{8,4},{12,0},{1,13},{5,9},{9,5},{13,1},{2,14},{6,10},... | collective-permute-start | bytes 245768 | tf_op jit(solution)/shard_map/ppermute | solution.py:272
  5.6 1.7 %collective-permute-start.3 = (bf16[160,256]{1,0:T(8,128)(2,1)}, bf16[160,256]{1,0:T(8,128)(2,1)S(1)}, u32[]{:S(2)}, u32[]{:S(2)}) collective-permute-start(bf16[160,256]{1,0:T(8,128)(2,1)} %refs_0_.5), channel_id=1, source_target_pairs={{0,2},{2,0},{1,3},{3,1},{4,6},{6,4},{5,7},{7,5},{8,10},{10,8},{9,1... | collective-permute-start | bytes 245768 | tf_op jit(solution)/shard_map/ppermute | solution.py:272
  8.2 3.4 %collective-permute-done.refs_1_ = bf16[160,256]{1,0:T(8,128)(2,1)S(1)} collective-permute-done((bf16[160,256]{1,0:T(8,128)(2,1)}, bf16[160,256]{1,0:T(8,128)(2,1)S(1)}, u32[]{:S(2)}, u32[]{:S(2)}) %collective-permute-start) | collective-permute-done | bytes 81952 | tf_op jit(solution)/shard_map/ppermute | solution.py:272
  11.5 1.6 %collective-permute-start.4 = (bf16[160,256]{1,0:T(8,128)(2,1)S(1)}, bf16[160,256]{1,0:T(8,128)(2,1)S(1)}, u32[]{:S(2)}, u32[]{:S(2)}) collective-permute-start(bf16[160,256]{1,0:T(8,128)(2,1)S(1)} %collective-permute-done.refs_1_), channel_id=1, source_target_pairs={{0,2},{2,0},{1,3},{3,1},{4,6},{6,4},{5,7},{7,5},{8,10},{10,8},{9,1... | collective-permute-start | bytes 245768 | tf_op jit(solution)/shard_map/ppermute | solution.py:272
  13.6 1.6 %collective-permute-start.6 = (bf16[160,256]{1,0:T(8,128)(2,1)S(1)}, bf16[160,256]{1,0:T(8,128)(2,1)S(1)}, u32[]{:S(2)}, u32[]{:S(2)}) collective-permute-start(bf16[160,256]{1,0:T(8,128)(2,1)S(1)} %collective-permute-done.2.refs_3_), channel_id=1, source_target_pairs={{0,2},{2,0},{1,3},{3,1},{4,6},{6,4},{5,7},{7,5},{8,10},{10,8},{9,1... | collective-permute-start | bytes 245768 | tf_op jit(solution)/shard_map/ppermute | solution.py:272
  15.2 1.5 %copy-done.8 = bf16[9,160,640]{2,1,0:T(8,128)(2,1)S(1)} copy-done((bf16[9,160,640]{2,1,0:T(8,128)(2,1)S(1)}, bf16[9,160,640]{2,1,0:T(8,128)(2,1)}, u32[]{:S(2)}) %copy-start.8) | copy-done | bytes 1843224
  16.7 1.2 %shard_map.109 = (bf16[480,960]{1,0:T(8,128)(2,1)S(1)}, bf16[240,960]{1,0:T(8,128)(2,1)S(1)}, bf16[240,960]{1,0:T(8,128)(2,1)S(1)}) custom-call(bf16[9,160,640]{2,1,0:T(8,128)(2,1)S(1)} %copy-done.8), custom_call_target="tpu_custom_call" | custom-call | flops 1000000000 | bytes 1843200 | tf_op jit(solution)/shard_map/pallas_call | solution.py:34
  18.0 0.6 collective-permute-done.6.refs_7_
  21.1 1.4 %shard_map.112 = (f32[4,80,256]{2,1,0:T(8,128)S(1)}, f32[4,80,256]{2,1,0:T(8,128)S(1)}) custom-call(bf16[2,4,80,256]{3,2,1,0:T(8,128)(2,1)S(1)} %shard_map.111.refs_0_, bf16[2,4,80,256]{3,2,1,0:T(8,128)(2,1)S(1)} %collective-permute-done.8.refs_1_, bf16[480,960]{1,0:T(8,128)(2,1)S(1)} %get-tuple-element.73.refs_2_), custom_call_target="tpu_custom_call" | custom-call | flops 943718400 | bytes 1576960 | tf_op jit(solution)/shard_map/pallas_call | solution.py:34
  22.5 1.1 %shard_map.115.refs_0_ = bf16[4,80,256]{2,1,0:T(8,128)(2,1)S(1)} custom-call(bf16[2,4,80,256]{3,2,1,0:T(8,128)(2,1)S(1)} %shard_map.110.refs_0_, bf16[2,4,80,256]{3,2,1,0:T(8,128)(2,1)S(1)} %collective-permute-done.7.refs_1_, bf16[240,960]{1,0:T(8,128)(2,1)S(1)} %get-tuple-element.78.refs_2_, f32[4,80,256]{2,1,0:T(8,128)S(1)} %get-tuple-element.79.refs_3_, ...), custom_call_target="tpu_custom_call" | custom-call | flops 471859200 | bytes 1444480 | tf_op jit(solution)/shard_map/pallas_call | solution.py:34
  23.6 1.2 %collective-permute-start.12 = (bf16[4,80,256]{2,1,0:T(8,128)(2,1)S(1)}, bf16[4,80,256]{2,1,0:T(8,128)(2,1)S(1)}, u32[]{:S(2)}, u32[]{:S(2)}) collective-permute-start(bf16[4,80,256]{2,1,0:T(8,128)(2,1)S(1)} %shard_map.115.refs_0_), channel_id=1, source_target_pairs={{0,2},{2,0},{1,3},{3,1},{4,6},{6,4},{5,7},{7,5},{8,10},{10,8},{9,1... | collective-permute-start | bytes 491528 | tf_op jit(solution)/shard_map/ppermute | solution.py:272
  24.8 1.1 %shard_map.114.refs_0_ = bf16[4,80,256]{2,1,0:T(8,128)(2,1)S(1)} custom-call(bf16[2,4,80,256]{3,2,1,0:T(8,128)(2,1)S(1)} %shard_map.110.refs_0_, bf16[2,4,80,256]{3,2,1,0:T(8,128)(2,1)S(1)} %collective-permute-done.7.refs_1_, bf16[240,960]{1,0:T(8,128)(2,1)S(1)} %get-tuple-element.72.refs_2_, f32[4,80,256]{2,1,0:T(8,128)S(1)} %get-tuple-element.74.refs_3_, ...), custom_call_target="tpu_custom_call" | custom-call | flops 471859200 | bytes 1444480 | tf_op jit(solution)/shard_map/pallas_call | solution.py:34
  25.9 0.9 %collective-permute-start.9 = (bf16[4,80,256]{2,1,0:T(8,128)(2,1)S(1)}, bf16[4,80,256]{2,1,0:T(8,128)(2,1)S(1)}, u32[]{:S(2)}, u32[]{:S(2)}) collective-permute-start(bf16[4,80,256]{2,1,0:T(8,128)(2,1)S(1)} %shard_map.114.refs_0_), channel_id=1, source_target_pairs={{0,2},{2,0},{1,3},{3,1},{4,6},{6,4},{5,7},{7,5},{8,10},{10,8},{9,1... | collective-permute-start | bytes 491528 | tf_op jit(solution)/shard_map/ppermute | solution.py:272
  27.0 1.2 %shard_map.117 = (bf16[480,960]{1,0:T(8,128)(2,1)S(1)}, bf16[240,960]{1,0:T(8,128)(2,1)S(1)}, bf16[240,960]{1,0:T(8,128)(2,1)S(1)}) custom-call(bf16[9,160,640]{2,1,0:T(8,128)(2,1)S(1)} %copy-done.9), custom_call_target="tpu_custom_call" | custom-call | flops 1000000000 | bytes 1843200 | tf_op jit(solution)/shard_map/pallas_call | solution.py:34
  28.2 2.5 %collective-permute-done.12.refs_1_ = bf16[4,80,256]{2,1,0:T(8,128)(2,1)S(1)} collective-permute-done((bf16[4,80,256]{2,1,0:T(8,128)(2,1)S(1)}, bf16[4,80,256]{2,1,0:T(8,128)(2,1)S(1)}, u32[]{:S(2)}, u32[]{:S(2)}) %collective-permute-start.12) | collective-permute-done | bytes 163872 | tf_op jit(solution)/shard_map/ppermute | solution.py:272
  31.2 2.5 %collective-permute-done.9.refs_1_ = bf16[4,80,256]{2,1,0:T(8,128)(2,1)S(1)} collective-permute-done((bf16[4,80,256]{2,1,0:T(8,128)(2,1)S(1)}, bf16[4,80,256]{2,1,0:T(8,128)(2,1)S(1)}, u32[]{:S(2)}, u32[]{:S(2)}) %collective-permute-start.9) | collective-permute-done | bytes 163872 | tf_op jit(solution)/shard_map/ppermute | solution.py:272
  34.2 1.2 %collective-permute-start.19 = (bf16[160,640]{1,0:T(8,128)(2,1)S(1)}, bf16[160,640]{1,0:T(8,128)(2,1)S(1)}, u32[]{:S(2)}, u32[]{:S(2)}) collective-permute-start(bf16[160,640]{1,0:T(8,128)(2,1)S(1)} %copy-done.5), channel_id=1, source_target_pairs={{0,2},{2,0},{1,3},{3,1},{4,6},{6,4},{5,7},{7,5},{8,10},{10,8},{9,1... | collective-permute-start | bytes 614408 | tf_op jit(solution)/shard_map/ppermute | solution.py:272
  35.4 1.4 %shard_map.118 = (f32[4,80,256]{2,1,0:T(8,128)S(1)}, f32[4,80,256]{2,1,0:T(8,128)S(1)}) custom-call(bf16[4,80,256]{2,1,0:T(8,128)(2,1)S(1)} %shard_map.115.refs_0_, bf16[4,80,256]{2,1,0:T(8,128)(2,1)S(1)} %collective-permute-done.12.refs_1_, bf16[4,80,256]{2,1,0:T(8,128)(2,1)S(1)} %collective-permute-done.16.refs_2_, ...), custom_call_target="tpu_custom_call" | custom-call | flops 943718400 | bytes 1576960 | tf_op jit(solution)/shard_map/pallas_call | solution.py:34
  36.8 1.1 %shard_map.120 = (bf16[4,80,256]{2,1,0:T(8,128)(2,1)S(1)}, bf16[80,256]{1,0:T(8,128)(2,1)S(1)}) custom-call(bf16[4,80,256]{2,1,0:T(8,128)(2,1)S(1)} %shard_map.114.refs_0_, bf16[4,80,256]{2,1,0:T(8,128)(2,1)S(1)} %collective-permute-done.9.refs_1_, bf16[4,80,256]{2,1,0:T(8,128)(2,1)S(1)} %collective-permute-done.10.refs_2_, ...), custom_call_target="tpu_custom_call" | custom-call | flops 471859200 | bytes 1771520 | tf_op jit(solution)/shard_map/pallas_call | solution.py:34
  37.9 3.3 %collective-permute-done.19.chan = bf16[160,640]{1,0:T(8,128)(2,1)S(1)} collective-permute-done((bf16[160,640]{1,0:T(8,128)(2,1)S(1)}, bf16[160,640]{1,0:T(8,128)(2,1)S(1)}, u32[]{:S(2)}, u32[]{:S(2)}) %collective-permute-start.19) | collective-permute-done | bytes 204832 | tf_op jit(solution)/shard_map/ppermute | solution.py:272
  41.7 1.1 %shard_map.122 = (bf16[4,80,256]{2,1,0:T(8,128)(2,1)S(1)}, bf16[80,256]{1,0:T(8,128)(2,1)S(1)}) custom-call(bf16[4,80,256]{2,1,0:T(8,128)(2,1)S(1)} %shard_map.114.refs_0_, bf16[4,80,256]{2,1,0:T(8,128)(2,1)S(1)} %collective-permute-done.9.refs_1_, bf16[4,80,256]{2,1,0:T(8,128)(2,1)S(1)} %collective-permute-done.10.refs_2_, ...), custom_call_target="tpu_custom_call" | custom-call | flops 471859200 | bytes 1771520 | tf_op jit(solution)/shard_map/pallas_call | solution.py:34
  42.8 1.2 %collective-permute-start.24 = (bf16[4,80,256]{2,1,0:T(8,128)(2,1)S(1)}, bf16[4,80,256]{2,1,0:T(8,128)(2,1)S(1)}, u32[]{:S(2)}, u32[]{:S(2)}) collective-permute-start(bf16[4,80,256]{2,1,0:T(8,128)(2,1)S(1)} %get-tuple-element.106.refs_4_), channel_id=1, source_target_pairs={{0,2},{2,0},{1,3},{3,1},{4,6},{6,4},{5,7},{7,5},{8,10},{10,8},{9,1... | collective-permute-start | bytes 491528 | tf_op jit(solution)/shard_map/ppermute | solution.py:272
  44.0 0.9 %collective-permute-start.18 = (bf16[4,80,256]{2,1,0:T(8,128)(2,1)S(1)}, bf16[4,80,256]{2,1,0:T(8,128)(2,1)S(1)}, u32[]{:S(2)}, u32[]{:S(2)}) collective-permute-start(bf16[4,80,256]{2,1,0:T(8,128)(2,1)S(1)} %get-tuple-element.101.refs_0_), channel_id=1, source_target_pairs={{0,2},{2,0},{1,3},{3,1},{4,6},{6,4},{5,7},{7,5},{8,10},{10,8},{9,1... | collective-permute-start | bytes 491528 | tf_op jit(solution)/shard_map/ppermute | solution.py:272
  44.9 5.0 %collective-permute-done.24.refs_5_ = bf16[4,80,256]{2,1,0:T(8,128)(2,1)S(1)} collective-permute-done((bf16[4,80,256]{2,1,0:T(8,128)(2,1)S(1)}, bf16[4,80,256]{2,1,0:T(8,128)(2,1)S(1)}, u32[]{:S(2)}, u32[]{:S(2)}) %collective-permute-start.24) | collective-permute-done | bytes 163872 | tf_op jit(solution)/shard_map/ppermute | solution.py:272
  50.6 1.9 %collective-permute-done.18.refs_1_ = bf16[4,80,256]{2,1,0:T(8,128)(2,1)S(1)} collective-permute-done((bf16[4,80,256]{2,1,0:T(8,128)(2,1)S(1)}, bf16[4,80,256]{2,1,0:T(8,128)(2,1)S(1)}, u32[]{:S(2)}, u32[]{:S(2)}) %collective-permute-start.18) | collective-permute-done | bytes 163872 | tf_op jit(solution)/shard_map/ppermute | solution.py:272
  53.0 1.2 %collective-permute-start.28 = (bf16[160,640]{1,0:T(8,128)(2,1)S(1)}, bf16[160,640]{1,0:T(8,128)(2,1)S(1)}, u32[]{:S(2)}, u32[]{:S(2)}) collective-permute-start(bf16[160,640]{1,0:T(8,128)(2,1)S(1)} %copy-done.6), channel_id=1, source_target_pairs={{0,2},{2,0},{1,3},{3,1},{4,6},{6,4},{5,7},{7,5},{8,10},{10,8},{9,1... | collective-permute-start | bytes 614408 | tf_op jit(solution)/shard_map/ppermute | solution.py:272
  54.2 4.3 %shard_map.123 = (bf16[320,128]{1,0:T(8,128)(2,1)S(1)}, bf16[640,256]{1,0:T(8,128)(2,1)S(1)}) custom-call(bf16[4,80,256]{2,1,0:T(8,128)(2,1)S(1)} %get-tuple-element.101.refs_0_, bf16[4,80,256]{2,1,0:T(8,128)(2,1)S(1)} %collective-permute-done.18.refs_1_, bf16[4,80,256]{2,1,0:T(8,128)(2,1)S(1)} %collective-permute-done.22.refs_2_, ...), custom_call_target="tpu_custom_call" | custom-call | flops 4000000000 | bytes 3358720 | tf_op jit(solution)/shard_map/pallas_call | solution.py:34
  58.5 1.5 %collective-permute-done.28.chan = bf16[160,640]{1,0:T(8,128)(2,1)S(1)} collective-permute-done((bf16[160,640]{1,0:T(8,128)(2,1)S(1)}, bf16[160,640]{1,0:T(8,128)(2,1)S(1)}, u32[]{:S(2)}, u32[]{:S(2)}) %collective-permute-start.28) | collective-permute-done | bytes 204832 | tf_op jit(solution)/shard_map/ppermute | solution.py:272
  60.0 1.2 %collective-permute-start.27 = (bf16[320,128]{1,0:T(8,128)(2,1)S(1)}, bf16[320,128]{1,0:T(8,128)(2,1)S(1)}, u32[]{:S(2)}, u32[]{:S(2)}) collective-permute-start(bf16[320,128]{1,0:T(8,128)(2,1)S(1)} %get-tuple-element.119.own), channel_id=1, source_target_pairs={{0,2},{2,0},{1,3},{3,1},{4,6},{6,4},{5,7},{7,5},{8,10},{10,8},{9,1... | collective-permute-start | bytes 245768 | tf_op jit(solution)/shard_map/ppermute | solution.py:272
  62.0 2.9 %collective-permute-done.27.chan = bf16[320,128]{1,0:T(8,128)(2,1)S(1)} collective-permute-done((bf16[320,128]{1,0:T(8,128)(2,1)S(1)}, bf16[320,128]{1,0:T(8,128)(2,1)S(1)}, u32[]{:S(2)}, u32[]{:S(2)}) %collective-permute-start.27) | collective-permute-done | bytes 81952 | tf_op jit(solution)/shard_map/ppermute | solution.py:272
  65.4 0.8 %collective-permute-done.30.sub = bf16[320,128]{1,0:T(8,128)(2,1)S(1)} collective-permute-done((bf16[320,128]{1,0:T(8,128)(2,1)S(1)}, bf16[320,128]{1,0:T(8,128)(2,1)S(1)}, u32[]{:S(2)}, u32[]{:S(2)}) %collective-permute-start.30) | collective-permute-done | bytes 81952 | tf_op jit(solution)/shard_map/ppermute | solution.py:272
  66.3 0.9 %shard_map.126 = bf16[160,256]{1,0:T(8,128)(2,1)} custom-call(bf16[320,128]{1,0:T(8,128)(2,1)S(1)} %get-tuple-element.119.own, bf16[320,128]{1,0:T(8,128)(2,1)S(1)} %collective-permute-done.27.chan, bf16[320,128]{1,0:T(8,128)(2,1)S(1)} %collective-permute-done.30.sub, bf16[320,128]{1,0:T(8,128)(2,1)S(1)} %collective-permute-done.31.both, ...), custom_call_target="tpu_custom_call" | custom-call | bytes 696320 | tf_op jit(solution)/shard_map/pallas_call | solution.py:34
  (74 shorter events, 7.9 us)
Async XLA Ops:
  0.0 13.6 %collective-permute-start.2 = (bf16[160,256]{1,0:T(8,128)(2,1)}, bf16[160,256]{1,0:T(8,128)(2,1)S(1)}, u32[]{:S(2)}, u32[]{:S(2)}) collective-permute-start(bf16[160,256]{1,0:T(8,128)(2,1)} %refs_0_.5), channel_id=1, source_target_pairs={{0,12},{4,8},{8,4},{12,0},{1,13},{5,9},{9,5},{13,1},{2,14},{6,10},... | collective-permute-start | bytes 245768 | tf_op jit(solution)/shard_map/ppermute | solution.py:272
  5.1 6.4 %collective-permute-start = (bf16[160,256]{1,0:T(8,128)(2,1)}, bf16[160,256]{1,0:T(8,128)(2,1)S(1)}, u32[]{:S(2)}, u32[]{:S(2)}) collective-permute-start(bf16[160,256]{1,0:T(8,128)(2,1)} %refs_0_.5), channel_id=1, source_target_pairs={{0,4},{4,0},{8,12},{12,8},{1,5},{5,1},{9,13},{13,9},{2,6},{6,2},{1... | collective-permute-start | bytes 245768 | tf_op jit(solution)/shard_map/ppermute | solution.py:272
  5.1 8.0 %collective-permute-start.1 = (bf16[160,256]{1,0:T(8,128)(2,1)}, bf16[160,256]{1,0:T(8,128)(2,1)S(1)}, u32[]{:S(2)}, u32[]{:S(2)}) collective-permute-start(bf16[160,256]{1,0:T(8,128)(2,1)} %refs_0_.5), channel_id=1, source_target_pairs={{0,8},{4,12},{8,0},{12,4},{1,9},{5,13},{9,1},{13,5},{2,10},{6,14},... | collective-permute-start | bytes 245768 | tf_op jit(solution)/shard_map/ppermute | solution.py:272
  5.6 12.3 %collective-permute-start.3 = (bf16[160,256]{1,0:T(8,128)(2,1)}, bf16[160,256]{1,0:T(8,128)(2,1)S(1)}, u32[]{:S(2)}, u32[]{:S(2)}) collective-permute-start(bf16[160,256]{1,0:T(8,128)(2,1)} %refs_0_.5), channel_id=1, source_target_pairs={{0,2},{2,0},{1,3},{3,1},{4,6},{6,4},{5,7},{7,5},{8,10},{10,8},{9,1... | collective-permute-start | bytes 245768 | tf_op jit(solution)/shard_map/ppermute | solution.py:272
  11.5 6.4 %collective-permute-start.4 = (bf16[160,256]{1,0:T(8,128)(2,1)S(1)}, bf16[160,256]{1,0:T(8,128)(2,1)S(1)}, u32[]{:S(2)}, u32[]{:S(2)}) collective-permute-start(bf16[160,256]{1,0:T(8,128)(2,1)S(1)} %collective-permute-done.refs_1_), channel_id=1, source_target_pairs={{0,2},{2,0},{1,3},{3,1},{4,6},{6,4},{5,7},{7,5},{8,10},{10,8},{9,1... | collective-permute-start | bytes 245768 | tf_op jit(solution)/shard_map/ppermute | solution.py:272
  13.1 4.9 %collective-permute-start.5 = (bf16[160,256]{1,0:T(8,128)(2,1)S(1)}, bf16[160,256]{1,0:T(8,128)(2,1)S(1)}, u32[]{:S(2)}, u32[]{:S(2)}) collective-permute-start(bf16[160,256]{1,0:T(8,128)(2,1)S(1)} %collective-permute-done.1.refs_2_), channel_id=1, source_target_pairs={{0,2},{2,0},{1,3},{3,1},{4,6},{6,4},{5,7},{7,5},{8,10},{10,8},{9,1... | collective-permute-start | bytes 245768 | tf_op jit(solution)/shard_map/ppermute | solution.py:272
  13.6 5.0 %collective-permute-start.6 = (bf16[160,256]{1,0:T(8,128)(2,1)S(1)}, bf16[160,256]{1,0:T(8,128)(2,1)S(1)}, u32[]{:S(2)}, u32[]{:S(2)}) collective-permute-start(bf16[160,256]{1,0:T(8,128)(2,1)S(1)} %collective-permute-done.2.refs_3_), channel_id=1, source_target_pairs={{0,2},{2,0},{1,3},{3,1},{4,6},{6,4},{5,7},{7,5},{8,10},{10,8},{9,1... | collective-permute-start | bytes 245768 | tf_op jit(solution)/shard_map/ppermute | solution.py:272
  19.0 2.1 %collective-permute-start.8 = (bf16[2,4,80,256]{3,2,1,0:T(8,128)(2,1)S(1)}, bf16[2,4,80,256]{3,2,1,0:T(8,128)(2,1)S(1)}, u32[]{:S(2)}, u32[]{:S(2)}) collective-permute-start(bf16[2,4,80,256]{3,2,1,0:T(8,128)(2,1)S(1)} %shard_map.111.refs_0_), channel_id=1, source_target_pairs={{0,1},{1,0},{2,3},{3,2},{4,5},{5,4},{6,7},{7,6},{8,9},{9,8},{10,11... | collective-permute-start | bytes 983048 | tf_op jit(solution)/shard_map/ppermute | solution.py:272
  19.4 3.0 %collective-permute-start.7 = (bf16[2,4,80,256]{3,2,1,0:T(8,128)(2,1)S(1)}, bf16[2,4,80,256]{3,2,1,0:T(8,128)(2,1)S(1)}, u32[]{:S(2)}, u32[]{:S(2)}) collective-permute-start(bf16[2,4,80,256]{3,2,1,0:T(8,128)(2,1)S(1)} %shard_map.110.refs_0_), channel_id=1, source_target_pairs={{0,1},{1,0},{2,3},{3,2},{4,5},{5,4},{6,7},{7,6},{8,9},{9,8},{10,11... | collective-permute-start | bytes 983048 | tf_op jit(solution)/shard_map/ppermute | solution.py:272
  20.0 6.8 %collective-permute-start.14 = (bf16[2,160,640]{2,1,0:T(8,128)(2,1)S(1)}, bf16[2,160,640]{2,1,0:T(8,128)(2,1)S(1)}, u32[]{:S(2)}, u32[]{:S(2)}) collective-permute-start(bf16[2,160,640]{2,1,0:T(8,128)(2,1)S(1)} %copy-done.3), channel_id=1, source_target_pairs={{0,1},{1,0},{2,3},{3,2},{4,5},{5,4},{6,7},{7,6},{8,9},{9,8},{10,11... | collective-permute-start | bytes 1228808 | tf_op jit(solution)/shard_map/ppermute | solution.py:272
  20.1 6.8 %collective-permute-start.13 = (bf16[160,640]{1,0:T(8,128)(2,1)S(1)}, bf16[160,640]{1,0:T(8,128)(2,1)S(1)}, u32[]{:S(2)}, u32[]{:S(2)}) collective-permute-start(bf16[160,640]{1,0:T(8,128)(2,1)S(1)} %copy-done.4), channel_id=1, source_target_pairs={{0,1},{1,0},{2,3},{3,2},{4,5},{5,4},{6,7},{7,6},{8,9},{9,8},{10,11... | collective-permute-start | bytes 614408 | tf_op jit(solution)/shard_map/ppermute | solution.py:272
  20.5 7.7 %collective-permute-start.15 = (bf16[160,640]{1,0:T(8,128)(2,1)S(1)}, bf16[160,640]{1,0:T(8,128)(2,1)S(1)}, u32[]{:S(2)}, u32[]{:S(2)}) collective-permute-start(bf16[160,640]{1,0:T(8,128)(2,1)S(1)} %copy-done.5), channel_id=1, source_target_pairs={{0,1},{1,0},{2,3},{3,2},{4,5},{5,4},{6,7},{7,6},{8,9},{9,8},{10,11... | collective-permute-start | bytes 614408 | tf_op jit(solution)/shard_map/ppermute | solution.py:272
  23.6 7.1 %collective-permute-start.12 = (bf16[4,80,256]{2,1,0:T(8,128)(2,1)S(1)}, bf16[4,80,256]{2,1,0:T(8,128)(2,1)S(1)}, u32[]{:S(2)}, u32[]{:S(2)}) collective-permute-start(bf16[4,80,256]{2,1,0:T(8,128)(2,1)S(1)} %shard_map.115.refs_0_), channel_id=1, source_target_pairs={{0,2},{2,0},{1,3},{3,1},{4,6},{6,4},{5,7},{7,5},{8,10},{10,8},{9,1... | collective-permute-start | bytes 491528 | tf_op jit(solution)/shard_map/ppermute | solution.py:272
  25.9 7.8 %collective-permute-start.9 = (bf16[4,80,256]{2,1,0:T(8,128)(2,1)S(1)}, bf16[4,80,256]{2,1,0:T(8,128)(2,1)S(1)}, u32[]{:S(2)}, u32[]{:S(2)}) collective-permute-start(bf16[4,80,256]{2,1,0:T(8,128)(2,1)S(1)} %shard_map.114.refs_0_), channel_id=1, source_target_pairs={{0,2},{2,0},{1,3},{3,1},{4,6},{6,4},{5,7},{7,5},{8,10},{10,8},{9,1... | collective-permute-start | bytes 491528 | tf_op jit(solution)/shard_map/ppermute | solution.py:272
  30.7 4.7 %collective-permute-start.16 = (bf16[4,80,256]{2,1,0:T(8,128)(2,1)S(1)}, bf16[4,80,256]{2,1,0:T(8,128)(2,1)S(1)}, u32[]{:S(2)}, u32[]{:S(2)}) collective-permute-start(bf16[4,80,256]{2,1,0:T(8,128)(2,1)S(1)} %shard_map.115.refs_0_), channel_id=1, source_target_pairs={{0,1},{1,0},{2,3},{3,2},{4,5},{5,4},{6,7},{7,6},{8,9},{9,8},{10,11... | collective-permute-start | bytes 491528 | tf_op jit(solution)/shard_map/ppermute | solution.py:272
  30.7 4.7 %collective-permute-start.17 = (bf16[4,80,256]{2,1,0:T(8,128)(2,1)S(1)}, bf16[4,80,256]{2,1,0:T(8,128)(2,1)S(1)}, u32[]{:S(2)}, u32[]{:S(2)}) collective-permute-start(bf16[4,80,256]{2,1,0:T(8,128)(2,1)S(1)} %collective-permute-done.12.refs_1_), channel_id=1, source_target_pairs={{0,1},{1,0},{2,3},{3,2},{4,5},{5,4},{6,7},{7,6},{8,9},{9,8},{10,11... | collective-permute-start | bytes 491528 | tf_op jit(solution)/shard_map/ppermute | solution.py:272
  33.7 3.1 %collective-permute-start.10 = (bf16[4,80,256]{2,1,0:T(8,128)(2,1)S(1)}, bf16[4,80,256]{2,1,0:T(8,128)(2,1)S(1)}, u32[]{:S(2)}, u32[]{:S(2)}) collective-permute-start(bf16[4,80,256]{2,1,0:T(8,128)(2,1)S(1)} %shard_map.114.refs_0_), channel_id=1, source_target_pairs={{0,1},{1,0},{2,3},{3,2},{4,5},{5,4},{6,7},{7,6},{8,9},{9,8},{10,11... | collective-permute-start | bytes 491528 | tf_op jit(solution)/shard_map/ppermute | solution.py:272
  33.7 3.1 %collective-permute-start.11 = (bf16[4,80,256]{2,1,0:T(8,128)(2,1)S(1)}, bf16[4,80,256]{2,1,0:T(8,128)(2,1)S(1)}, u32[]{:S(2)}, u32[]{:S(2)}) collective-permute-start(bf16[4,80,256]{2,1,0:T(8,128)(2,1)S(1)} %collective-permute-done.9.refs_1_), channel_id=1, source_target_pairs={{0,1},{1,0},{2,3},{3,2},{4,5},{5,4},{6,7},{7,6},{8,9},{9,8},{10,11... | collective-permute-start | bytes 491528 | tf_op jit(solution)/shard_map/ppermute | solution.py:272
  34.2 7.0 %collective-permute-start.19 = (bf16[160,640]{1,0:T(8,128)(2,1)S(1)}, bf16[160,640]{1,0:T(8,128)(2,1)S(1)}, u32[]{:S(2)}, u32[]{:S(2)}) collective-permute-start(bf16[160,640]{1,0:T(8,128)(2,1)S(1)} %copy-done.5), channel_id=1, source_target_pairs={{0,2},{2,0},{1,3},{3,1},{4,6},{6,4},{5,7},{7,5},{8,10},{10,8},{9,1... | collective-permute-start | bytes 614408 | tf_op jit(solution)/shard_map/ppermute | solution.py:272
  41.2 9.3 %collective-permute-start.20 = (bf16[160,640]{1,0:T(8,128)(2,1)S(1)}, bf16[160,640]{1,0:T(8,128)(2,1)S(1)}, u32[]{:S(2)}, u32[]{:S(2)}) collective-permute-start(bf16[160,640]{1,0:T(8,128)(2,1)S(1)} %collective-permute-done.19.chan), channel_id=1, source_target_pairs={{0,1},{1,0},{2,3},{3,2},{4,5},{5,4},{6,7},{7,6},{8,9},{9,8},{10,11... | collective-permute-start | bytes 614408 | tf_op jit(solution)/shard_map/ppermute | solution.py:272
  41.2 11.3 %collective-permute-start.21 = (bf16[160,640]{1,0:T(8,128)(2,1)S(1)}, bf16[160,640]{1,0:T(8,128)(2,1)S(1)}, u32[]{:S(2)}, u32[]{:S(2)}) collective-permute-start(bf16[160,640]{1,0:T(8,128)(2,1)S(1)} %copy-done.6), channel_id=1, source_target_pairs={{0,1},{1,0},{2,3},{3,2},{4,5},{5,4},{6,7},{7,6},{8,9},{9,8},{10,11... | collective-permute-start | bytes 614408 | tf_op jit(solution)/shard_map/ppermute | solution.py:272
  42.8 7.1 %collective-permute-start.24 = (bf16[4,80,256]{2,1,0:T(8,128)(2,1)S(1)}, bf16[4,80,256]{2,1,0:T(8,128)(2,1)S(1)}, u32[]{:S(2)}, u32[]{:S(2)}) collective-permute-start(bf16[4,80,256]{2,1,0:T(8,128)(2,1)S(1)} %get-tuple-element.106.refs_4_), channel_id=1, source_target_pairs={{0,2},{2,0},{1,3},{3,1},{4,6},{6,4},{5,7},{7,5},{8,10},{10,8},{9,1... | collective-permute-start | bytes 491528 | tf_op jit(solution)/shard_map/ppermute | solution.py:272
  44.0 8.5 %collective-permute-start.18 = (bf16[4,80,256]{2,1,0:T(8,128)(2,1)S(1)}, bf16[4,80,256]{2,1,0:T(8,128)(2,1)S(1)}, u32[]{:S(2)}, u32[]{:S(2)}) collective-permute-start(bf16[4,80,256]{2,1,0:T(8,128)(2,1)S(1)} %get-tuple-element.101.refs_0_), channel_id=1, source_target_pairs={{0,2},{2,0},{1,3},{3,1},{4,6},{6,4},{5,7},{7,5},{8,10},{10,8},{9,1... | collective-permute-start | bytes 491528 | tf_op jit(solution)/shard_map/ppermute | solution.py:272
  49.9 4.2 %collective-permute-start.25 = (bf16[4,80,256]{2,1,0:T(8,128)(2,1)S(1)}, bf16[4,80,256]{2,1,0:T(8,128)(2,1)S(1)}, u32[]{:S(2)}, u32[]{:S(2)}) collective-permute-start(bf16[4,80,256]{2,1,0:T(8,128)(2,1)S(1)} %get-tuple-element.106.refs_4_), channel_id=1, source_target_pairs={{0,1},{1,0},{2,3},{3,2},{4,5},{5,4},{6,7},{7,6},{8,9},{9,8},{10,11... | collective-permute-start | bytes 491528 | tf_op jit(solution)/shard_map/ppermute | solution.py:272
  49.9 4.2 %collective-permute-start.26 = (bf16[4,80,256]{2,1,0:T(8,128)(2,1)S(1)}, bf16[4,80,256]{2,1,0:T(8,128)(2,1)S(1)}, u32[]{:S(2)}, u32[]{:S(2)}) collective-permute-start(bf16[4,80,256]{2,1,0:T(8,128)(2,1)S(1)} %collective-permute-done.24.refs_5_), channel_id=1, source_target_pairs={{0,1},{1,0},{2,3},{3,2},{4,5},{5,4},{6,7},{7,6},{8,9},{9,8},{10,11... | collective-permute-start | bytes 491528 | tf_op jit(solution)/shard_map/ppermute | solution.py:272
  52.5 1.7 %collective-permute-start.22 = (bf16[4,80,256]{2,1,0:T(8,128)(2,1)S(1)}, bf16[4,80,256]{2,1,0:T(8,128)(2,1)S(1)}, u32[]{:S(2)}, u32[]{:S(2)}) collective-permute-start(bf16[4,80,256]{2,1,0:T(8,128)(2,1)S(1)} %get-tuple-element.101.refs_0_), channel_id=1, source_target_pairs={{0,1},{1,0},{2,3},{3,2},{4,5},{5,4},{6,7},{7,6},{8,9},{9,8},{10,11... | collective-permute-start | bytes 491528 | tf_op jit(solution)/shard_map/ppermute | solution.py:272
  52.5 1.7 %collective-permute-start.23 = (bf16[4,80,256]{2,1,0:T(8,128)(2,1)S(1)}, bf16[4,80,256]{2,1,0:T(8,128)(2,1)S(1)}, u32[]{:S(2)}, u32[]{:S(2)}) collective-permute-start(bf16[4,80,256]{2,1,0:T(8,128)(2,1)S(1)} %collective-permute-done.18.refs_1_), channel_id=1, source_target_pairs={{0,1},{1,0},{2,3},{3,2},{4,5},{5,4},{6,7},{7,6},{8,9},{9,8},{10,11... | collective-permute-start | bytes 491528 | tf_op jit(solution)/shard_map/ppermute | solution.py:272
  53.0 7.0 %collective-permute-start.28 = (bf16[160,640]{1,0:T(8,128)(2,1)S(1)}, bf16[160,640]{1,0:T(8,128)(2,1)S(1)}, u32[]{:S(2)}, u32[]{:S(2)}) collective-permute-start(bf16[160,640]{1,0:T(8,128)(2,1)S(1)} %copy-done.6), channel_id=1, source_target_pairs={{0,2},{2,0},{1,3},{3,1},{4,6},{6,4},{5,7},{7,5},{8,10},{10,8},{9,1... | collective-permute-start | bytes 614408 | tf_op jit(solution)/shard_map/ppermute | solution.py:272
  60.0 1.5 %collective-permute-start.29 = (bf16[160,640]{1,0:T(8,128)(2,1)S(1)}, bf16[160,640]{1,0:T(8,128)(2,1)S(1)}, u32[]{:S(2)}, u32[]{:S(2)}) collective-permute-start(bf16[160,640]{1,0:T(8,128)(2,1)S(1)} %collective-permute-done.28.chan), channel_id=1, source_target_pairs={{0,1},{1,0},{2,3},{3,2},{4,5},{5,4},{6,7},{7,6},{8,9},{9,8},{10,11... | collective-permute-start | bytes 614408 | tf_op jit(solution)/shard_map/ppermute | solution.py:272
  60.0 4.9 %collective-permute-start.27 = (bf16[320,128]{1,0:T(8,128)(2,1)S(1)}, bf16[320,128]{1,0:T(8,128)(2,1)S(1)}, u32[]{:S(2)}, u32[]{:S(2)}) collective-permute-start(bf16[320,128]{1,0:T(8,128)(2,1)S(1)} %get-tuple-element.119.own), channel_id=1, source_target_pairs={{0,2},{2,0},{1,3},{3,1},{4,6},{6,4},{5,7},{7,5},{8,10},{10,8},{9,1... | collective-permute-start | bytes 245768 | tf_op jit(solution)/shard_map/ppermute | solution.py:272
  64.8 1.3 %collective-permute-start.30 = (bf16[320,128]{1,0:T(8,128)(2,1)S(1)}, bf16[320,128]{1,0:T(8,128)(2,1)S(1)}, u32[]{:S(2)}, u32[]{:S(2)}) collective-permute-start(bf16[320,128]{1,0:T(8,128)(2,1)S(1)} %get-tuple-element.119.own), channel_id=1, source_target_pairs={{0,1},{1,0},{2,3},{3,2},{4,5},{5,4},{6,7},{7,6},{8,9},{9,8},{10,11... | collective-permute-start | bytes 245768 | tf_op jit(solution)/shard_map/ppermute | solution.py:272
  64.8 1.4 %collective-permute-start.31 = (bf16[320,128]{1,0:T(8,128)(2,1)S(1)}, bf16[320,128]{1,0:T(8,128)(2,1)S(1)}, u32[]{:S(2)}, u32[]{:S(2)}) collective-permute-start(bf16[320,128]{1,0:T(8,128)(2,1)S(1)} %collective-permute-done.27.chan), channel_id=1, source_target_pairs={{0,1},{1,0},{2,3},{3,2},{4,5},{5,4},{6,7},{7,6},{8,9},{9,8},{10,11... | collective-permute-start | bytes 245768 | tf_op jit(solution)/shard_map/ppermute | solution.py:272
  (10 other events, 45.5 us)
